TPU v7x, 32 devices: a whole 2x2x4 slice. The times are simulated.
32 devices in a mesh: section: 2 (over core), dp: 4 (over y, x), ctx: 4 (over z).
Axes of the slice: x: 2, y: 2, z: 4, core: 2. Of those that a mesh axis runs over, the one named last changes fastest.
Arguments:
- tokens: bfloat16 [2, 8, 1024, 768], P(None, 'dp', 'ctx'), may hold values from -6 to 6
- upstream: bfloat16 [2, 8, 1024, 768], P(None, 'dp', 'ctx'), may hold values from -6 to 6
- lengths: int32 [2, 8], P(None, 'dp'), may hold values from 512 to 1024, as said below
- w_qkv: float32 [2, 768, 2304], P('section', ('dp', 'ctx')), may hold values from -0.21875 to 0.21875
- w_out: float32 [2, 768, 768], P('section', ('dp', 'ctx')), may hold values from -4 to 4
- w_in: float32 [2, 768, 3072], P('section', ('dp', 'ctx')), may hold values from -0.21875 to 0.21875
- w_back: float32 [2, 3072, 768], P('section', ('dp', 'ctx')), may hold values from -0.109375 to 0.109375
- gain_attn: float32 [2, 768], P('section', ('dp', 'ctx')), may hold values from 0.1 to 1.9
- gain_ffn: float32 [2, 768], P('section', ('dp', 'ctx')), may hold values from 0.1 to 1.9
Outputs:
- acts: float32 [2, 2, 8, 1024, 768], P('section', None, 'dp', 'ctx')
- grads: float32 [2, 2, 8, 1024, 768], P('section', None, 'dp', 'ctx')
- grad_qkv: float32 [2, 768, 2304], P('section', ('dp', 'ctx'))
- grad_out: float32 [2, 768, 768], P('section', ('dp', 'ctx'))
- grad_in: float32 [2, 768, 3072], P('section', ('dp', 'ctx'))
- grad_back: float32 [2, 3072, 768], P('section', ('dp', 'ctx'))
- grad_gain_attn: float32 [2, 768], P('section', ('dp', 'ctx'))
- grad_gain_ffn: float32 [2, 768], P('section', ('dp', 'ctx'))
Inputs may be any that keep to these rules, and one draw needn't show every extreme that they name: `lengths`: the number of real codons of each sequence, from 512 to 1024; some sequence has exactly 1024 and some exactly 512.
All inputs are finite; a program needn't handle non-finite values.
Results may differ from a plain program's by a relative error of at most 0.038.
Values may be sent and summed in bfloat16 or wider, within the bound.
No kernel may reach another device: no remote copies, remote signals or barrier semaphores. Data moves between devices by JAX's collectives and lax.ppermute only.
A program may use at most 320 MiB of HBM per device.

v0:
```python
from functools import partial

import jax
import jax.numpy as jnp
from jax import lax
from jax.sharding import PartitionSpec as P

HD = 64


def passed_along(value, axis, steps):
    count = lax.axis_size(axis)
    leading, last = (max(0, -steps), min(count, count - steps))
    return lax.ppermute(value, axis, [(source, source + steps) for source in range(leading, last)])


def tables(positions):
    half_width = HD // 2
    frequency = jnp.power(10000.0, -(jnp.arange(half_width).astype(jnp.float32) * 2.0) / HD)
    angles = positions[:, None] * frequency[None, :]
    angles = jnp.concatenate([angles, angles], axis=1)
    return (jnp.cos(angles)[:, None, :], jnp.sin(angles)[:, None, :])


def rotate(tensor, cosine_tab, sine_tab):
    half_width = tensor.shape[-1] // 2
    turned = jnp.concatenate([-tensor[..., half_width:], tensor[..., :half_width]], axis=-1)
    return tensor * cosine_tab + turned * sine_tab


def layer_norm(residual_state, gain_vec):
    centred = residual_state - jnp.mean(residual_state, axis=-1, keepdims=True)
    spread = jnp.mean(centred * centred, axis=-1, keepdims=True)
    return centred * lax.rsqrt(spread + 1e-05) * gain_vec


def contract_rows(left_op, right_op):
    return lax.dot_general(
        left_op, right_op, (((0,), (0,)), ((), ())), preferred_element_type=jnp.float32
    )


def contract_cols(left_op, right_op):
    return lax.dot_general(
        left_op, right_op, (((1,), (1,)), ((), ())), preferred_element_type=jnp.float32
    )


def store(buffer, new_value, position, in_range):
    previous = lax.dynamic_index_in_dim(buffer, position, 0, keepdims=False)
    return lax.dynamic_update_index_in_dim(
        buffer, jnp.where(in_range, new_value, previous), position, 0
    )


def split_heads(tensor):
    return tensor.reshape(tensor.shape[0], tensor.shape[1], tensor.shape[2] // HD, HD)


def masked_scores(query, key_all, key_mask):
    scores = jnp.einsum(
        "sqhd,skhd->shqk",
        split_heads(query),
        split_heads(key_all),
        preferred_element_type=jnp.float32,
    )
    return jnp.where(key_mask[:, None, None, :], scores, -1e30)


def attention_forward(query, key_all, value_all, key_mask):
    scores = masked_scores(query, key_all, key_mask)
    row_peak = jnp.max(scores, axis=-1, keepdims=True)
    log_total = row_peak + jnp.log(jnp.sum(jnp.exp(scores - row_peak), axis=-1, keepdims=True))
    probabilities = jnp.exp(scores - log_total).astype(jnp.bfloat16)
    attended_output = jnp.einsum(
        "shqk,skhd->sqhd", probabilities, split_heads(value_all), preferred_element_type=jnp.float32
    )
    return (attended_output.reshape(query.shape).astype(jnp.bfloat16), log_total)


def attention_backward(query, key_all, value_all, key_mask, log_total, grad_attended):
    scores = masked_scores(query, key_all, key_mask)
    probabilities = jnp.exp(scores - log_total)
    low_probs = probabilities.astype(jnp.bfloat16)
    grad_heads = split_heads(grad_attended)
    grad_probs = jnp.einsum(
        "sqhd,skhd->shqk", grad_heads, split_heads(value_all), preferred_element_type=jnp.float32
    )
    delta = jnp.sum(probabilities * grad_probs, axis=-1, keepdims=True)
    grad_scores = (probabilities * (grad_probs - delta)).astype(jnp.bfloat16)
    grad_query = jnp.einsum(
        "shqk,skhd->sqhd", grad_scores, split_heads(key_all), preferred_element_type=jnp.float32
    )
    grad_keys = jnp.einsum(
        "shqk,sqhd->skhd", grad_scores, split_heads(query), preferred_element_type=jnp.float32
    )
    grad_values = jnp.einsum(
        "shqk,sqhd->skhd", low_probs, grad_heads, preferred_element_type=jnp.float32
    )
    return (
        grad_query.reshape(query.shape),
        grad_keys.reshape(key_all.shape),
        grad_values.reshape(key_all.shape),
    )


def local(tokens, upstream, lengths, w_qkv, w_out, w_in, w_back, gain_attn, gain_ffn):
    section_count = lax.axis_size("section")
    section_index = lax.axis_index("section")
    micro_count, sequences, span_rows, model_width = tokens.shape
    head_count = model_width // HD
    key_count = span_rows * lax.axis_size("ctx")
    ctx_index = lax.axis_index("ctx")
    q_scale = HD ** (-0.5)
    qkv_low = w_qkv[0].astype(jnp.bfloat16)
    out_low = w_out[0].astype(jnp.bfloat16)
    in_low = w_in[0].astype(jnp.bfloat16)
    back_low = w_back[0].astype(jnp.bfloat16)
    attn_low = gain_attn[0].astype(jnp.bfloat16)
    ffn_low = gain_ffn[0].astype(jnp.bfloat16)
    (
        query_key_value_matrix,
        output_weight_matrix,
        input_weight_matrix,
        back_weight_matrix,
        gain_one,
        gain_two,
    ) = (
        lax.all_gather(qkv_low, ("dp", "ctx"), axis=0, tiled=True),
        lax.all_gather(out_low, ("dp", "ctx"), axis=0, tiled=True),
        lax.all_gather(in_low, ("dp", "ctx"), axis=0, tiled=True),
        lax.all_gather(back_low, ("dp", "ctx"), axis=0, tiled=True),
        lax.all_gather(attn_low, ("dp", "ctx"), axis=0, tiled=True),
        lax.all_gather(ffn_low, ("dp", "ctx"), axis=0, tiled=True),
    )
    gain_one = gain_one.astype(jnp.float32)
    gain_two = gain_two.astype(jnp.float32)
    positions = (ctx_index * span_rows + jnp.arange(span_rows)).astype(jnp.float32)
    cosine_tab, sine_tab = tables(positions)
    key_places = jnp.arange(key_count)
    row_total = sequences * span_rows
    span_shape = (sequences, span_rows, model_width)

    def scaled_rotate(tensor):
        return rotate(tensor, cosine_tab, sine_tab) * q_scale

    def plain_rotate(tensor):
        return rotate(tensor, cosine_tab, sine_tab)

    def mask_for(which_batch):
        lengths_now = lax.dynamic_index_in_dim(lengths, which_batch, 0, keepdims=False)
        return key_places[None, :] < lengths_now[:, None]

    moments = micro_count + section_count - 1
    acts = jnp.zeros((micro_count,) + span_shape, jnp.float32)
    inbound = jnp.zeros(span_shape, jnp.float32)
    stored = None
    for moment in range(moments):
        micro_index = moment - section_index
        in_range = (micro_index >= 0) & (micro_index < micro_count)
        which_batch = jnp.clip(micro_index, 0, micro_count - 1)
        fresh = lax.dynamic_index_in_dim(tokens, which_batch, 0, keepdims=False).astype(jnp.float32)
        source = jnp.where(section_index == 0, fresh, inbound)
        forward_residual_in = source.reshape(row_total, model_width)
        forward_normed_input = layer_norm(forward_residual_in, gain_one).astype(jnp.bfloat16)
        query_key_value_rows = jnp.dot(
            forward_normed_input, query_key_value_matrix, preferred_element_type=jnp.float32
        )
        query_key_value_rows = query_key_value_rows.reshape(sequences, span_rows, 3, head_count, HD)
        forward_query = (
            scaled_rotate(query_key_value_rows[:, :, 0]).astype(jnp.bfloat16).reshape(span_shape)
        )
        forward_key_rows = (
            plain_rotate(query_key_value_rows[:, :, 1]).astype(jnp.bfloat16).reshape(span_shape)
        )
        forward_value_rows = query_key_value_rows[:, :, 2].astype(jnp.bfloat16).reshape(span_shape)
        forward_key_all = lax.all_gather(forward_key_rows, "ctx", axis=1, tiled=True)
        forward_value_all = lax.all_gather(forward_value_rows, "ctx", axis=1, tiled=True)
        forward_attended_output, forward_log_total = attention_forward(
            forward_query, forward_key_all, forward_value_all, mask_for(which_batch)
        )
        forward_middle_state = forward_residual_in + jnp.dot(
            forward_attended_output.reshape(row_total, model_width),
            output_weight_matrix,
            preferred_element_type=jnp.float32,
        )
        forward_normed_second = layer_norm(forward_middle_state, gain_two).astype(jnp.bfloat16)
        forward_hidden_before_gelu = jnp.dot(
            forward_normed_second, input_weight_matrix, preferred_element_type=jnp.float32
        )
        forward_hidden_activation = jax.nn.gelu(
            forward_hidden_before_gelu, approximate=False
        ).astype(jnp.bfloat16)
        result = forward_middle_state + jnp.dot(
            forward_hidden_activation, back_weight_matrix, preferred_element_type=jnp.float32
        )
        forward_saved = (
            forward_residual_in,
            forward_query,
            forward_key_rows,
            forward_value_rows,
            forward_log_total,
            forward_attended_output,
            forward_middle_state,
            forward_hidden_before_gelu,
            forward_hidden_activation,
        )
        result, saved = (result.reshape(span_shape), forward_saved)
        if stored is None:
            stored = tuple((jnp.zeros((micro_count,) + item.shape, item.dtype) for item in saved))
        stored = tuple(
            (store(buffer, item, which_batch, in_range) for buffer, item in zip(stored, saved))
        )
        acts = store(acts, result, which_batch, in_range)
        if moment + 1 < moments:
            inbound = passed_along(result.astype(jnp.bfloat16), "section", 1).astype(result.dtype)
    grads_in = jnp.zeros((micro_count,) + span_shape, jnp.float32)
    inbound_grad = jnp.zeros(span_shape, jnp.float32)
    full_totals = (
        jnp.zeros(query_key_value_matrix.shape, jnp.float32),
        jnp.zeros(output_weight_matrix.shape, jnp.float32),
        jnp.zeros(input_weight_matrix.shape, jnp.float32),
        jnp.zeros(back_weight_matrix.shape, jnp.float32),
        jnp.zeros(gain_one.shape, jnp.float32),
        jnp.zeros(gain_two.shape, jnp.float32),
    )
    shard_totals = (
        jnp.zeros_like(w_qkv[0]),
        jnp.zeros_like(w_out[0]),
        jnp.zeros_like(w_in[0]),
        jnp.zeros_like(w_back[0]),
        jnp.zeros_like(gain_attn[0]),
        jnp.zeros_like(gain_ffn[0]),
    )
    for moment in range(moments):
        micro_index = moment - (section_count - 1 - section_index)
        in_range = (micro_index >= 0) & (micro_index < micro_count)
        which_batch = jnp.clip(micro_index, 0, micro_count - 1)
        fresh = lax.dynamic_index_in_dim(upstream, which_batch, 0, keepdims=False).astype(
            jnp.float32
        )
        incoming = jnp.where(section_index == section_count - 1, fresh, inbound_grad)
        saved = tuple(
            (lax.dynamic_index_in_dim(buffer, which_batch, 0, keepdims=False) for buffer in stored)
        )
        (
            residual_in,
            query,
            key_rows,
            value_rows,
            log_total,
            attended_output,
            middle_state,
            hidden_before_gelu,
            hidden_activation,
        ) = saved[:9]
        grad_top = incoming.reshape(row_total, model_width)
        low_top = grad_top.astype(jnp.bfloat16)
        grad_w_back = contract_rows(hidden_activation, low_top)
        grad_hidden = contract_cols(low_top, back_weight_matrix)
        gelu_primal, gelu_back = jax.vjp(
            partial(jax.nn.gelu, approximate=False), hidden_before_gelu
        )
        grad_pre = gelu_back(grad_hidden)[0].astype(jnp.bfloat16)
        normed_second, norm_two_back = jax.vjp(layer_norm, middle_state, gain_two)
        grad_w_in = contract_rows(normed_second.astype(jnp.bfloat16), grad_pre)
        grad_normed_two = contract_cols(grad_pre, input_weight_matrix)
        grad_mid_norm, grad_gain_two = norm_two_back(grad_normed_two)
        grad_middle = grad_top + grad_mid_norm
        low_middle = grad_middle.astype(jnp.bfloat16)
        grad_w_out = contract_rows(attended_output.reshape(row_total, model_width), low_middle)
        grad_attended = (
            contract_cols(low_middle, output_weight_matrix).astype(jnp.bfloat16).reshape(span_shape)
        )
        key_all = lax.all_gather(key_rows, "ctx", axis=1, tiled=True)
        value_all = lax.all_gather(value_rows, "ctx", axis=1, tiled=True)
        grad_query, grad_keys, grad_values = attention_backward(
            query, key_all, value_all, mask_for(which_batch), log_total, grad_attended
        )
        grad_keys, grad_values = (
            lax.psum_scatter(
                grad_keys.astype(jnp.bfloat16), "ctx", scatter_dimension=1, tiled=True
            ).astype(jnp.float32),
            lax.psum_scatter(
                grad_values.astype(jnp.bfloat16), "ctx", scatter_dimension=1, tiled=True
            ).astype(jnp.float32),
        )
        heads_shape = (sequences, span_rows, head_count, HD)
        zero_heads = jnp.zeros(heads_shape, jnp.float32)
        rotated_q, q_back = jax.vjp(scaled_rotate, zero_heads)
        rotated_k, k_back = jax.vjp(plain_rotate, zero_heads)
        low_query = grad_query.astype(jnp.bfloat16).astype(jnp.float32).reshape(heads_shape)
        low_keys = grad_keys.astype(jnp.bfloat16).astype(jnp.float32).reshape(heads_shape)
        part_q = q_back(low_query)[0]
        part_k = k_back(low_keys)[0]
        part_v = grad_values.reshape(heads_shape)
        grad_qkv = (
            jnp.stack([part_q, part_k, part_v], axis=2)
            .reshape(row_total, 3 * model_width)
            .astype(jnp.bfloat16)
        )
        normed_input, norm_one_back = jax.vjp(layer_norm, residual_in, gain_one)
        grad_w_qkv = contract_rows(normed_input.astype(jnp.bfloat16), grad_qkv)
        grad_normed = contract_cols(grad_qkv, query_key_value_matrix)
        grad_in_norm, grad_gain_one = norm_one_back(grad_normed)
        grad_source = grad_middle + grad_in_norm
        partial_grads = (
            grad_w_qkv,
            grad_w_out,
            grad_w_in,
            grad_w_back,
            grad_gain_one,
            grad_gain_two,
        )
        grad_source, partial_grads = (grad_source.reshape(span_shape), partial_grads)
        g_qkv, g_out, g_in, g_back, g_one, g_two = tuple(
            (jnp.where(in_range, item, 0.0) for item in partial_grads)
        )
        grads_in = store(grads_in, grad_source, which_batch, in_range)
        full_totals = tuple(
            (
                total + item
                for total, item in zip(full_totals, (g_qkv, g_out, g_in, g_back, g_one, g_two))
            )
        )
        if moment + 1 < moments:
            inbound_grad = passed_along(grad_source.astype(jnp.bfloat16), "section", -1).astype(
                grad_source.dtype
            )
    sum_qkv, sum_out, sum_in, sum_back, sum_one, sum_two = full_totals
    shard_totals = (
        lax.psum_scatter(sum_qkv, ("dp", "ctx"), scatter_dimension=0, tiled=True),
        lax.psum_scatter(sum_out, ("dp", "ctx"), scatter_dimension=0, tiled=True),
        lax.psum_scatter(sum_in, ("dp", "ctx"), scatter_dimension=0, tiled=True),
        lax.psum_scatter(sum_back, ("dp", "ctx"), scatter_dimension=0, tiled=True),
        lax.psum_scatter(sum_one, ("dp", "ctx"), scatter_dimension=0, tiled=True),
        lax.psum_scatter(sum_two, ("dp", "ctx"), scatter_dimension=0, tiled=True),
    )
    return (
        acts[None],
        grads_in[None],
        shard_totals[0][None],
        shard_totals[1][None],
        shard_totals[2][None],
        shard_totals[3][None],
        shard_totals[4][None],
        shard_totals[5][None],
    )


def solution(mesh):
    return jax.shard_map(
        local,
        mesh=mesh,
        in_specs=(
            P(None, "dp", "ctx", None),
            P(None, "dp", "ctx", None),
            P(None, "dp"),
            P("section", ("dp", "ctx"), None),
            P("section", ("dp", "ctx"), None),
            P("section", ("dp", "ctx"), None),
            P("section", ("dp", "ctx"), None),
            P("section", ("dp", "ctx")),
            P("section", ("dp", "ctx")),
        ),
        out_specs=(
            P("section", None, "dp", "ctx", None),
            P("section", None, "dp", "ctx", None),
            P("section", ("dp", "ctx"), None),
            P("section", ("dp", "ctx"), None),
            P("section", ("dp", "ctx"), None),
            P("section", ("dp", "ctx"), None),
            P("section", ("dp", "ctx")),
            P("section", ("dp", "ctx")),
        ),
        check_vma=False,
    )
```

profile of v0, /device:TPU:1, one launch (start us, length us, event | category | flops | bytes accessed | tf_op | source)
XLA Modules:
  0.0 2273.2 jit_solution(7702583870397529192)
XLA Ops:
  12.7 36.3 %all-reduce.17 = (bf16[768]{0:T(1024)(128)(2,1)S(1)}, bf16[768]{0:T(1024)(128)(2,1)S(1)}) all-reduce(bf16[768]{0:T(1024)(128)(2,1)S(1)} %dynamic-update-slice, bf16[768]{0:T(1024)(128)(2,1)S(1)} %dynamic-update-slice.1), channel_id=2, replica_groups=mesh['section'=2,'dp'=4,'ctx'=4] {'dp','ctx'}, use_global_device_ids=true, to_apply=%add.12 | all-reduce | flops 1536 | bytes 6144
  54.4 29.1 %all-gather.41.cloned.1.call-done = bf16[1,768,2304]{2,1,0:T(8,128)(2,1)} async-done(((bf16[1,48,2304]{2,1,0:T(8,128)(2,1)}), bf16[1,768,2304]{2,1,0:T(8,128)(2,1)}) %all-gather.41.cloned.1.call-update) | async-done | bytes 3538960 | tf_op jit(solution)/shard_map/all_gather | solution.py:129
  107.2 55.9 %all-gather.31.cloned.1.call-done = bf16[2,1024,768]{1,2,0:T(8,128)(2,1)} async-done(((bf16[2,256,768]{1,2,0:T(8,128)(2,1)}), bf16[2,1024,768]{1,2,0:T(8,128)(2,1)}) %all-gather.31.cloned.1.call-update) | async-done | bytes 3145744 | tf_op jit(solution)/shard_map/all_gather | solution.py:177
  189.2 37.0 %all-gather.29.cloned.1.call-done = bf16[2,1024,768]{1,2,0:T(8,128)(2,1)} async-done(((bf16[2,256,768]{1,2,0:T(8,128)(2,1)}), bf16[2,1024,768]{1,2,0:T(8,128)(2,1)}) %all-gather.29.cloned.1.call-update) | async-done | bytes 3145744 | tf_op jit(solution)/shard_map/all_gather | solution.py:178
  240.7 41.6 %all-gather.43.cloned.1.call-done = bf16[1,768,768]{2,1,0:T(8,128)(2,1)} async-done(((bf16[1,48,768]{2,1,0:T(8,128)(2,1)}), bf16[1,768,768]{2,1,0:T(8,128)(2,1)}) %all-gather.43.cloned.1.call-update) | async-done | bytes 1179664 | tf_op jit(solution)/shard_map/all_gather | solution.py:130
  285.5 79.9 %all-gather.45.cloned.1.call-done = bf16[1,768,3072]{2,1,0:T(8,128)(2,1)} async-done(((bf16[1,48,3072]{2,1,0:T(8,128)(2,1)}), bf16[1,768,3072]{2,1,0:T(8,128)(2,1)}) %all-gather.45.cloned.1.call-update) | async-done | bytes 4718608 | tf_op jit(solution)/shard_map/all_gather | solution.py:131
  369.3 21.0 bitcast_dynamic-update-slice_fusion.5
  390.2 57.5 %all-gather.47.cloned.1.call-done = bf16[1,3072,768]{2,1,0:T(8,128)(2,1)} async-done(((bf16[1,192,768]{2,1,0:T(8,128)(2,1)}), bf16[1,3072,768]{2,1,0:T(8,128)(2,1)}) %all-gather.47.cloned.1.call-update) | async-done | bytes 4718608 | tf_op jit(solution)/shard_map/all_gather | solution.py:132
  476.3 54.5 %all-gather.35.cloned.1.call-done = bf16[2,1024,768]{1,2,0:T(8,128)(2,1)} async-done(((bf16[2,256,768]{1,2,0:T(8,128)(2,1)}), bf16[2,1024,768]{1,2,0:T(8,128)(2,1)}) %all-gather.35.cloned.1.call-update) | async-done | bytes 3145744 | tf_op jit(solution)/shard_map/all_gather | solution.py:177
  557.3 36.7 %all-gather.33.cloned.1.call-done = bf16[2,1024,768]{1,2,0:T(8,128)(2,1)} async-done(((bf16[2,256,768]{1,2,0:T(8,128)(2,1)}), bf16[2,1024,768]{1,2,0:T(8,128)(2,1)}) %all-gather.33.cloned.1.call-update) | async-done | bytes 3145744 | tf_op jit(solution)/shard_map/all_gather | solution.py:178
  609.1 20.4 bitcast_dynamic-update-slice_fusion.4
  799.6 20.2 bitcast_dynamic-update-slice_fusion.3
  826.3 18.9 fusion.43
  869.3 29.2 %all-gather.51.cloned.1.call-done = bf16[1,2,1024,768]{3,2,1,0:T(8,128)(2,1)} async-done(((bf16[1,2,256,768]{3,2,1,0:T(8,128)(2,1)}), bf16[1,2,1024,768]{3,2,1,0:T(8,128)(2,1)}) %all-gather.51.cloned.1.call-update) | async-done | bytes 3145744 | tf_op jit(solution)/shard_map/all_gather | solution.py:276
  901.7 17.2 multiply_reduce_fusion.2
  918.9 16.9 multiply_convert_fusion.2
  974.9 51.0 %all-gather.55.cloned.1.call-done = bf16[1,2,1024,768]{3,2,1,0:T(8,128)(2,1)} async-done(((bf16[1,2,256,768]{3,2,1,0:T(8,128)(2,1)}), bf16[1,2,1024,768]{3,2,1,0:T(8,128)(2,1)}) %all-gather.55.cloned.1.call-update) | async-done | bytes 3145744 | tf_op jit(solution)/shard_map/all_gather | solution.py:276
  1030.5 56.3 %reduce-scatter.11.cloned.1.call-done = bf16[2,256,768]{1,2,0:T(8,128)(2,1)} async-done(((bf16[2,1024,768]{1,2,0:T(8,128)(2,1)}), bf16[2,256,768]{1,2,0:T(8,128)(2,1)}) %reduce-scatter.11.cloned.1.call-update) | async-done | bytes 786448 | tf_op jit(solution)/shard_map/reduce_scatter | solution.py:281
  1089.6 59.7 %reduce-scatter.13.cloned.1.call-done = bf16[2,256,768]{1,2,0:T(8,128)(2,1)} async-done(((bf16[2,1024,768]{1,2,0:T(8,128)(2,1)}), bf16[2,256,768]{1,2,0:T(8,128)(2,1)}) %reduce-scatter.13.cloned.1.call-update) | async-done | bytes 786448 | tf_op jit(solution)/shard_map/reduce_scatter | solution.py:284
  1178.6 17.8 fusion.48
  1203.3 17.8 multiply_reduce_fusion.1
  1221.1 17.4 multiply_convert_fusion.1
  1294.8 44.3 %reduce-scatter.15.cloned.1.call-done = bf16[2,256,768]{1,2,0:T(8,128)(2,1)} async-done(((bf16[2,1024,768]{1,2,0:T(8,128)(2,1)}), bf16[2,256,768]{1,2,0:T(8,128)(2,1)}) %reduce-scatter.15.cloned.1.call-update) | async-done | bytes 786448 | tf_op jit(solution)/shard_map/reduce_scatter | solution.py:281
  1342.0 59.7 %reduce-scatter.17.cloned.1.call-done = bf16[2,256,768]{1,2,0:T(8,128)(2,1)} async-done(((bf16[2,1024,768]{1,2,0:T(8,128)(2,1)}), bf16[2,256,768]{1,2,0:T(8,128)(2,1)}) %reduce-scatter.17.cloned.1.call-update) | async-done | bytes 786448 | tf_op jit(solution)/shard_map/reduce_scatter | solution.py:284
  1429.6 18.0 fusion.53
  1460.2 18.2 multiply_reduce_fusion
  1602.7 20.9 reduce-scatter.21.cloned.1.call-done
  1659.0 34.9 %all-reduce.16 = (f32[768]{0:T(1024)S(1)}, f32[768]{0:T(1024)S(1)}) all-reduce(f32[768]{0:T(1024)S(1)} %select_add_fusion.5, f32[768]{0:T(1024)S(1)} %select_add_fusion.4), channel_id=24, replica_groups=mesh['section'=2,'dp'=4,'ctx'=4] {'dp','ctx'}, use_global_device_ids=true, to_apply=%region_58.59.clone | all-reduce | flops 1536 | bytes 12288
  1700.4 55.2 %reduce-scatter.25.cloned.1.call-done = f32[48,768]{1,0:T(8,128)} async-done(((f32[768,768]{1,0:T(8,128)}), f32[48,768]{1,0:T(8,128)}) %reduce-scatter.25.cloned.1.call-update) | async-done | bytes 147472 | tf_op jit(solution)/shard_map/reduce_scatter | solution.py:333
  1755.6 177.9 %reduce-scatter.27.cloned.1.call-done = f32[48,3072]{1,0:T(8,128)} async-done(((f32[768,3072]{1,0:T(8,128)}), f32[48,3072]{1,0:T(8,128)}) %reduce-scatter.27.cloned.1.call-update) | async-done | bytes 589840 | tf_op jit(solution)/shard_map/reduce_scatter | solution.py:334
  1933.5 176.4 %reduce-scatter.29.cloned.1.call-done = f32[192,768]{1,0:T(8,128)} async-done(((f32[3072,768]{1,0:T(8,128)}), f32[192,768]{1,0:T(8,128)}) %reduce-scatter.29.cloned.1.call-update) | async-done | bytes 589840 | tf_op jit(solution)/shard_map/reduce_scatter | solution.py:335
  2109.9 156.6 %reduce-scatter.23.cloned.1.call-done = f32[48,2304]{1,0:T(8,128)} async-done(((f32[768,2304]{1,0:T(8,128)}), f32[48,2304]{1,0:T(8,128)}) %reduce-scatter.23.cloned.1.call-update) | async-done | bytes 442384 | tf_op jit(solution)/shard_map/reduce_scatter | solution.py:332
  (789 shorter events, 700.5 us)
Async XLA Ops:
  7.2 76.3 %all-gather.41.cloned.1.call-start = ((), (), s32[]{:S(2)}) async-start(), calls=%async_computation.26 | async-start | bytes 3760128 | tf_op jit(solution)/shard_map/all_gather | solution.py:129
  9.0 154.1 %all-gather.31.cloned.1.call-start = ((), (), s32[]{:S(2)}) async-start(), calls=%async_computation.11 | async-start | bytes 3932160 | tf_op jit(solution)/shard_map/all_gather | solution.py:177
  49.0 589.4 %copy-start.139 = (f32[768]{0:T(1024)}, f32[768]{0:T(1024)S(1)}, u32[]{:S(2)}) copy-start(f32[768]{0:T(1024)S(1)} %convert_element_type.771) | copy-start | bytes 9220
  99.6 126.7 %all-gather.29.cloned.1.call-start = ((), (), s32[]{:S(2)}) async-start(), calls=%async_computation.10 | async-start | bytes 3932160 | tf_op jit(solution)/shard_map/all_gather | solution.py:178
  102.4 179.8 %all-gather.43.cloned.1.call-start = ((), (), s32[]{:S(2)}) async-start(), calls=%async_computation.27 | async-start | bytes 1253376 | tf_op jit(solution)/shard_map/all_gather | solution.py:130
  103.1 262.2 %all-gather.45.cloned.1.call-start = ((), (), s32[]{:S(2)}) async-start(), calls=%async_computation.28 | async-start | bytes 5013504 | tf_op jit(solution)/shard_map/all_gather | solution.py:131
  104.0 343.7 %all-gather.47.cloned.1.call-start = ((), (), s32[]{:S(2)}) async-start(), calls=%async_computation.29 | async-start | bytes 5013504 | tf_op jit(solution)/shard_map/all_gather | solution.py:132
  104.8 426.0 %all-gather.35.cloned.1.call-start = ((), (), s32[]{:S(2)}) async-start(), calls=%async_computation.13 | async-start | bytes 3932160 | tf_op jit(solution)/shard_map/all_gather | solution.py:177
  105.5 743.4 %copy-start.126 = (f32[768]{0:T(1024)}, f32[768]{0:T(1024)S(1)}, u32[]{:S(2)}) copy-start(f32[768]{0:T(1024)S(1)} %convert_element_type.772) | copy-start | bytes 9220
  454.9 4.8 collective-permute-start
  468.5 125.5 %all-gather.33.cloned.1.call-start = ((), (), s32[]{:S(2)}) async-start(), calls=%async_computation.12 | async-start | bytes 3932160 | tf_op jit(solution)/shard_map/all_gather | solution.py:178
  470.9 281.0 %all-gather.39.cloned.1.call-start = ((), (), s32[]{:S(2)}) async-start(), calls=%async_computation.15 | async-start | bytes 3932160 | tf_op jit(solution)/shard_map/all_gather | solution.py:177
  633.3 4.4 collective-permute-start.1
  647.3 130.7 %all-gather.37.cloned.1.call-start = ((), (), s32[]{:S(2)}) async-start(), calls=%async_computation.14 | async-start | bytes 3932160 | tf_op jit(solution)/shard_map/all_gather | solution.py:178
  649.8 204.1 %all-gather.49.cloned.1.call-start = ((), (), s32[]{:S(2)}) async-start(), calls=%async_computation.30 | async-start | bytes 3932160 | tf_op jit(solution)/shard_map/all_gather | solution.py:275
  706.7 191.8 %all-gather.51.cloned.1.call-start = ((), (), s32[]{:S(2)}) async-start(), calls=%async_computation.31 | async-start | bytes 3932160 | tf_op jit(solution)/shard_map/all_gather | solution.py:276
  713.9 256.3 %all-gather.53.cloned.1.call-start = ((), (), s32[]{:S(2)}) async-start(), calls=%async_computation.32 | async-start | bytes 3932160 | tf_op jit(solution)/shard_map/all_gather | solution.py:275
  719.9 306.0 %all-gather.55.cloned.1.call-start = ((), (), s32[]{:S(2)}) async-start(), calls=%async_computation.33 | async-start | bytes 3932160 | tf_op jit(solution)/shard_map/all_gather | solution.py:276
  751.9 334.9 %reduce-scatter.11.cloned.1.call-start = ((), (), s32[]{:S(2)}) async-start(), calls=%async_computation.16 | async-start | bytes 3932160 | tf_op jit(solution)/shard_map/reduce_scatter | solution.py:281
  941.3 208.0 %reduce-scatter.13.cloned.1.call-start = ((), (), s32[]{:S(2)}) async-start(), calls=%async_computation.17 | async-start | bytes 3932160 | tf_op jit(solution)/shard_map/reduce_scatter | solution.py:284
  954.8 303.9 %all-gather.57.cloned.1.call-start = ((), (), s32[]{:S(2)}) async-start(), calls=%async_computation.34 | async-start | bytes 3932160 | tf_op jit(solution)/shard_map/all_gather | solution.py:275
  955.4 322.7 %all-gather.59.cloned.1.call-start = ((), (), s32[]{:S(2)}) async-start(), calls=%async_computation.35 | async-start | bytes 3932160 | tf_op jit(solution)/shard_map/all_gather | solution.py:276
  958.0 381.1 %reduce-scatter.15.cloned.1.call-start = ((), (), s32[]{:S(2)}) async-start(), calls=%async_computation.18 | async-start | bytes 3932160 | tf_op jit(solution)/shard_map/reduce_scatter | solution.py:281
  1162.8 14.5 collective-permute-start.2
  1243.9 157.7 %reduce-scatter.17.cloned.1.call-start = ((), (), s32[]{:S(2)}) async-start(), calls=%async_computation.19 | async-start | bytes 3932160 | tf_op jit(solution)/shard_map/reduce_scatter | solution.py:284
  1256.4 343.5 %reduce-scatter.19.cloned.1.call-start = ((), (), s32[]{:S(2)}) async-start(), calls=%async_computation.20 | async-start | bytes 3932160 | tf_op jit(solution)/shard_map/reduce_scatter | solution.py:281
  1414.4 13.9 collective-permute-start.3
  1500.7 123.0 %reduce-scatter.21.cloned.1.call-start = ((), (), s32[]{:S(2)}) async-start(), calls=%async_computation.21 | async-start | bytes 3932160 | tf_op jit(solution)/shard_map/reduce_scatter | solution.py:284
  1513.8 241.7 %reduce-scatter.25.cloned.1.call-start = ((), (), s32[]{:S(2)}) async-start(), calls=%async_computation.23 | async-start | bytes 2506752 | tf_op jit(solution)/shard_map/reduce_scatter | solution.py:333
  1535.9 397.6 %reduce-scatter.27.cloned.1.call-start = ((), (), s32[]{:S(2)}) async-start(), calls=%async_computation.24 | async-start | bytes 10027008 | tf_op jit(solution)/shard_map/reduce_scatter | solution.py:334
  1555.3 554.5 %reduce-scatter.29.cloned.1.call-start = ((), (), s32[]{:S(2)}) async-start(), calls=%async_computation.25 | async-start | bytes 10027008 | tf_op jit(solution)/shard_map/reduce_scatter | solution.py:335
  1575.1 691.4 %reduce-scatter.23.cloned.1.call-start = ((), (), s32[]{:S(2)}) async-start(), calls=%async_computation.22 | async-start | bytes 7520256 | tf_op jit(solution)/shard_map/reduce_scatter | solution.py:332
  (211 other events, 4277.8 us)
Sparse Core Ops, SparseCore 0:
  11.3 72.0 all-gather.40
  99.7 63.2 all-gather.30
  164.6 61.5 all-gather.28
  229.4 52.7 all-gather.42
  285.4 79.9 all-gather.44
  368.6 79.0 all-gather.46
  468.6 62.1 all-gather.34
  532.4 61.5 all-gather.32
  647.4 61.2 all-gather.38
  710.1 61.5 all-gather.36
  773.4 61.5 all-gather.48
  836.3 62.1 all-gather.50
  900.1 62.1 all-gather.52
  963.7 62.1 all-gather.54
  1028.0 58.7 reduce-scatter.10
  1089.0 60.2 reduce-scatter.12
  1150.7 63.6 all-gather.56
  1215.8 62.1 all-gather.58
  1280.3 58.7 reduce-scatter.14
  1341.3 60.2 reduce-scatter.16
  1500.8 59.5 reduce-scatter.18
  1563.3 60.2 reduce-scatter.20
  1629.1 126.4 reduce-scatter.24
  1762.6 170.7 reduce-scatter.26
  1939.7 170.1 reduce-scatter.28
  2116.5 149.9 reduce-scatter.22
where the time goes:
time: 2290 us; the launch traced here: 2270 us
  waiting for transfers between devices  1300 us (57%)
  matrix products  478 us (21%)
  local copies, waits for them, and re-layouts  204 us (9%)
  other arithmetic  187 us (8%)
  blocking collectives  71.1 us (3%)
    reduce_scatter x1, waiting for transfers between devices, local(): lax.psum_scatter(sum_in, ('dp', 'ctx'), scatter_dimension=0, tiled=True)  178 us
    reduce_scatter x1, waiting for transfers between devices, local(): lax.psum_scatter(sum_back, ('dp', 'ctx'), scatter_dimension=0, tiled=True)  176 us
    reduce_scatter x1, waiting for transfers between devices, local(): lax.psum_scatter(sum_qkv, ('dp', 'ctx'), scatter_dimension=0, tiled=True)  157 us
    reduce_scatter x3, waiting for transfers between devices, local(): lax.psum_scatter(grad_values.astype(jnp.bfloat16), 'ctx', scatter_dimensi...  140 us
    all_gather x3, waiting for transfers between devices, local(): lax.all_gather(forward_key_rows, 'ctx', axis=1, tiled=True)  110 us
    reduce_scatter x3, waiting for transfers between devices, local(): lax.psum_scatter(grad_keys.astype(jnp.bfloat16), 'ctx', scatter_dimension...  101 us
    all_gather x3, waiting for transfers between devices, local(): value_all = lax.all_gather(value_rows, 'ctx', axis=1, tiled=True)  96.1 us
    all_gather x1, waiting for transfers between devices, local(): lax.all_gather(in_low, ('dp', 'ctx'), axis=0, tiled=True)  79.9 us
  transfers between devices with their start and end apart: 30, of which 22 were waited for; matrix products, arithmetic and copies ran while one was open for 29% of the time, Pallas kernels for 0%

commit v1 on v0

v1 whole, which is shorter than its diff:
```python
import functools

import jax
import jax.numpy as jnp
from jax import lax
from jax.experimental import pallas as pl
from jax.experimental.pallas import tpu as pltpu
from jax.sharding import PartitionSpec as P

HD = 64
PAIR = 2 * HD
BF16 = jnp.bfloat16
F32 = jnp.float32
MASKED = -1e30
VMEM_LIMIT = 56 * 1024 * 1024


def nn(left, right):
    return lax.dot_general(left, right, (((1,), (0,)), ((), ())), preferred_element_type=F32)


def nt(left, right):
    return lax.dot_general(left, right, (((1,), (1,)), ((), ())), preferred_element_type=F32)


def tn(left, right):
    return lax.dot_general(left, right, (((0,), (0,)), ((), ())), preferred_element_type=F32)


def normalise(rows):
    centred = rows - jnp.mean(rows, axis=-1, keepdims=True)
    scale = lax.rsqrt(jnp.mean(centred * centred, axis=-1, keepdims=True) + 1e-05)
    return centred * scale, scale


def norm_back(rows, gain, grad):
    normed, scale = normalise(rows)
    inner = grad * gain
    mean_inner = jnp.mean(inner, axis=-1, keepdims=True)
    mean_along = jnp.mean(inner * normed, axis=-1, keepdims=True)
    grad_rows = scale * (inner - mean_inner - normed * mean_along)
    return grad_rows, jnp.sum(grad * normed, axis=0, keepdims=True)


def swap_halves(pair_block):
    lane = lax.broadcasted_iota(jnp.int32, pair_block.shape, 1)
    ahead = pltpu.roll(pair_block, PAIR - HD // 2, 1)
    behind = pltpu.roll(pair_block, HD // 2, 1)
    return jnp.where(lane % HD < HD // 2, ahead, behind)


class Plan:
    def __init__(self, tokens, w_in):
        micro, seqs, span, width = tokens.shape
        self.width = width
        self.hidden = w_in.shape[-1]
        self.heads = width // HD
        self.pairs = width // PAIR
        self.n_ctx = lax.axis_size("ctx")
        self.n_dp = lax.axis_size("dp")
        self.micro, self.seqs, self.span = micro, seqs, span
        self.n_seq = micro * seqs
        self.parts = self.n_ctx // self.n_seq
        assert self.parts * self.n_seq == self.n_ctx
        self.half = span // 2
        self.sub = self.half // self.parts
        self.rows = self.n_ctx * self.sub
        self.dp_bits = self.n_dp.bit_length() - 1
        assert 1 << self.dp_bits == self.n_dp
        self.section = lax.axis_index("section")
        self.dp = lax.axis_index("dp")
        self.ctx = lax.axis_index("ctx")
        shard = w_in.shape[1]
        self.direct = shard % 16 == 0 and self.n_ctx == 4
        self.pieces_z = self.n_ctx if self.direct else 1
        self.meta = jnp.stack([self.section, self.dp, self.ctx]).astype(jnp.int32)


def other_core(value):
    return lax.ppermute(value, "section", [(0, 1), (1, 0)])


def xor_dp(plan, value, bit):
    return lax.ppermute(value, "dp", [(i, i ^ (1 << bit)) for i in range(plan.n_dp)])


def xor_ctx(plan, value, mask):
    return lax.ppermute(value, "ctx", [(i, i ^ mask) for i in range(plan.n_ctx)])


def spread_ctx(plan, shard):
    if plan.direct:
        parts = [shard] + [xor_ctx(plan, shard, d) for d in range(1, plan.n_ctx)]
        return jnp.concatenate(parts, axis=0)
    return lax.all_gather(shard, "ctx", axis=0, tiled=True)


def spread(plan, shard, low_first):
    pieces = {0: spread_ctx(plan, shard)}
    bits = range(plan.dp_bits) if low_first else reversed(range(plan.dp_bits))
    for bit in bits:
        for mask in list(pieces):
            pieces[mask | (1 << bit)] = xor_dp(plan, pieces[mask], bit)
    own = [pieces[mask] for mask in range(plan.n_dp)]
    return own, [other_core(piece) for piece in own]


def collect(plan, pieces, low_first):
    pieces = dict(enumerate(pieces))
    bits = list(range(plan.dp_bits)) if low_first else list(reversed(range(plan.dp_bits)))
    for bit in bits:
        kept = [mask for mask in pieces if not mask & (1 << bit)]
        got = {mask: xor_dp(plan, pieces[mask | (1 << bit)], bit) for mask in kept}
        pieces = {
            mask: (pieces[mask].astype(F32) + got[mask].astype(F32)).astype(BF16) for mask in kept
        }
    block = pieces[0]
    if plan.direct:
        size = block.shape[0] // plan.n_ctx
        parts = [block[d * size : (d + 1) * size] for d in range(plan.n_ctx)]
        total = parts[0].astype(F32)
        for d in range(1, plan.n_ctx):
            total = total + xor_ctx(plan, parts[d], d).astype(F32)
        return total.astype(BF16)
    return lax.psum_scatter(block, "ctx", scatter_dimension=0, tiled=True)


def smem():
    return pl.BlockSpec(memory_space=pltpu.SMEM)


def vmem():
    return pl.BlockSpec(memory_space=pltpu.VMEM)


def anywhere():
    return pl.BlockSpec(memory_space=pl.ANY)


def params(**kw):
    return pltpu.CompilerParams(vmem_limit_bytes=VMEM_LIMIT, **kw)


def cost(flops, bytes_accessed, transcendentals=0):
    return pl.CostEstimate(
        flops=int(flops), bytes_accessed=int(bytes_accessed), transcendentals=int(transcendentals)
    )


def block_starts(meta, n_dp, n_z, block):
    size = block // n_z
    for mask in range(n_dp):
        for d in range(n_z):
            start = (meta[1] ^ mask) * block
            if n_z > 1:
                start = start + (meta[2] ^ d) * size
            yield mask, d * size, start, size


def piece_copies(meta, refs, place, sems, first, n_z):
    copies = []
    block = refs[0].shape[0]
    for mask, row, start, size in block_starts(meta, len(refs), n_z, block):
        start = pl.multiple_of(start, 16)
        copies.append(
            pltpu.make_async_copy(
                refs[mask].at[pl.ds(row, size), :],
                place(start, size),
                sems.at[first + len(copies)],
            )
        )
    return copies


def run(copies):
    for copy in copies:
        copy.start()


def wait(copies):
    for copy in copies:
        copy.wait()


def qkv_kernel(n_dp, n_z, meta, x_ref, gain_ref, cos_ref, sin_ref, *refs):
    qk_own, qk_other, vo_own, vo_other = (refs[i * n_dp : (i + 1) * n_dp] for i in range(4))
    a_ref, q_ref, kv_ref, wqk, wv, sems = refs[4 * n_dp :]
    section = meta[0]
    count = n_dp * n_z

    def at_half(which):
        return lambda start, size: wqk.at[which, pl.ds(start, size), :]

    def at_v(start, size):
        return wv.at[pl.ds(start, size), :]

    qk = piece_copies(meta, qk_own, at_half(section), sems, 0, n_z)
    qk += piece_copies(meta, qk_other, at_half(1 - section), sems, count, n_z)
    run(qk)
    v_own = piece_copies(meta, vo_own, at_v, sems, 2 * count, n_z)
    v_other = piece_copies(meta, vo_other, at_v, sems, 2 * count, n_z)

    @pl.when(section == 0)
    def _():
        run(v_own)

    @pl.when(section != 0)
    def _():
        run(v_other)

    normed, _ = normalise(x_ref[...])
    a_ref[...] = (normed * gain_ref[...]).astype(BF16)
    wait(qk)

    @pl.when(section == 0)
    def _():
        wait(v_own)

    @pl.when(section != 0)
    def _():
        wait(v_other)

    rows, width = a_ref.shape
    step = 256 if rows % 256 == 0 else rows

    def body(i, carry):
        at = pl.ds(pl.multiple_of(i * step, step), step)
        a = a_ref[at, :]
        cos, sin = cos_ref[at, :], sin_ref[at, :]
        for which in range(2):
            out = nn(a, wqk[which])
            for pair in range(width // PAIR):
                lanes = slice(pair * PAIR, (pair + 1) * PAIR)
                block = out[:, lanes]
                turned = block * cos + swap_halves(block) * sin
                if which == 0:
                    q_ref[at, lanes] = (turned * HD**-0.5).astype(BF16)
                else:
                    kv_ref[0, at, lanes] = turned.astype(BF16)
        kv_ref[1, at, :] = nn(a, wv[...]).astype(BF16)
        return carry

    lax.fori_loop(0, rows // step, body, 0)


def qkv_forward(plan, x, gain, cos, sin, qk, vo):
    rows, width = x.shape
    n = plan.n_dp
    count = n * plan.pieces_z
    return pl.pallas_call(
        functools.partial(qkv_kernel, n, plan.pieces_z),
        out_shape=[
            jax.ShapeDtypeStruct((rows, width), BF16),
            jax.ShapeDtypeStruct((rows, width), BF16),
            jax.ShapeDtypeStruct((2, rows, width), BF16),
        ],
        in_specs=[smem(), vmem(), vmem(), vmem(), vmem()] + [anywhere()] * (4 * n),
        out_specs=[vmem(), vmem(), vmem()],
        scratch_shapes=[
            pltpu.VMEM((2, width, width), BF16),
            pltpu.VMEM((width, width), BF16),
            pltpu.SemaphoreType.DMA((3 * count,)),
        ],
        compiler_params=params(),
        cost_estimate=cost(6 * rows * width * width, 12 * rows * width + 6 * width * width),
        name="qkv_forward",
    )(plan.meta, x, gain, cos, sin, *qk[0], *qk[1], *vo[0], *vo[1])


def lane_mask(shape, head):
    lane = lax.broadcasted_iota(jnp.int32, shape, 1)
    return lane < HD if head == 0 else lane >= HD


def with_ones(query):
    lane = lax.broadcasted_iota(jnp.int32, query.shape, 1)
    return jnp.concatenate([query, jnp.where(lane == 0, 1.0, 0.0).astype(BF16)], axis=1)


def attention_kernel(chunks, key_block, q_ref, *refs):
    kv = refs[:chunks]
    bias_ref, o_ref, lse_ref, s_scr, vt_scr = refs[chunks:]
    rows = q_ref.shape[0]
    per_chunk = rows // key_block
    query = q_ref[...]
    for c in range(chunks):
        vt_scr[:, c * rows : (c + 1) * rows] = jnp.transpose(kv[c][1])
    outs = []
    for head in range(2):
        extended = with_ones(jnp.where(lane_mask(query.shape, head), query, jnp.zeros_like(query)))
        peak = jnp.full((1, rows), -jnp.inf, F32)
        for c in range(chunks):
            for j in range(per_chunk):
                at = slice(j * key_block, (j + 1) * key_block)
                everywhere = slice(c * rows + at.start, c * rows + at.stop)
                keys = jnp.concatenate([kv[c][0, at, :], bias_ref[everywhere, :]], axis=1)
                scores = nt(keys, extended)
                s_scr[everywhere, :] = scores
                peak = jnp.maximum(peak, jnp.max(scores, axis=0, keepdims=True))
        total = jnp.zeros((1, rows), F32)
        out = jnp.zeros((PAIR, rows), F32)
        for c in range(chunks):
            for j in range(per_chunk):
                everywhere = slice(c * rows + j * key_block, c * rows + (j + 1) * key_block)
                weights = jnp.exp(s_scr[everywhere, :] - peak)
                total = total + jnp.sum(weights, axis=0, keepdims=True)
                out = out + nn(vt_scr[:, everywhere], weights.astype(BF16))
        lse_ref[0, head : head + 1, :] = peak + jnp.log(total)
        outs.append(out / total)
    row = lax.broadcasted_iota(jnp.int32, outs[0].shape, 0)
    o_ref[...] = jnp.transpose(jnp.where(row < HD, outs[0], outs[1])).astype(BF16)


def attention_forward(plan, query, kv, bias):
    rows, width = query.shape
    chunks = len(kv)
    keys = chunks * rows
    pair_block = pl.BlockSpec((rows, PAIR), lambda p: (0, p))
    kv_block = pl.BlockSpec((2, rows, PAIR), lambda p: (0, 0, p))
    return pl.pallas_call(
        functools.partial(attention_kernel, chunks, min(256, rows)),
        out_shape=[
            jax.ShapeDtypeStruct((rows, width), BF16),
            jax.ShapeDtypeStruct((plan.pairs, 8, rows), F32),
        ],
        grid=(plan.pairs,),
        in_specs=[pair_block] + [kv_block] * chunks + [pl.BlockSpec((keys, PAIR), lambda p: (0, 0))],
        out_specs=[pair_block, pl.BlockSpec((1, 8, rows), lambda p: (p, 0, 0))],
        scratch_shapes=[pltpu.VMEM((keys, rows), F32), pltpu.VMEM((PAIR, keys), BF16)],
        compiler_params=params(),
        cost_estimate=cost(
            16 * rows * keys * width, 4 * rows * width + 4 * keys * width, rows * keys * plan.heads
        ),
        name="attention_forward",
    )(query, *kv, bias)


def out_kernel(n_dp, n_z, meta, o_ref, x_ref, gain_ref, *refs):
    vo_own, vo_other = refs[:n_dp], refs[n_dp : 2 * n_dp]
    u2_ref, b_ref, wo, sems = refs[2 * n_dp :]
    section = meta[0]

    def at_o(start, size):
        return wo.at[pl.ds(start, size), :]

    own = piece_copies(meta, vo_own, at_o, sems, 0, n_z)
    other = piece_copies(meta, vo_other, at_o, sems, 0, n_z)

    @pl.when(section == 1)
    def _():
        run(own)
        wait(own)

    @pl.when(section != 1)
    def _():
        run(other)
        wait(other)

    rows = o_ref.shape[0]
    step = 256 if rows % 256 == 0 else rows

    def body(i, carry):
        at = pl.ds(pl.multiple_of(i * step, step), step)
        u2 = x_ref[at, :] + nn(o_ref[at, :], wo[...])
        u2_ref[at, :] = u2
        b_ref[at, :] = (normalise(u2)[0] * gain_ref[...]).astype(BF16)
        return carry

    lax.fori_loop(0, rows // step, body, 0)


def out_forward(plan, o, x, gain, vo):
    rows, width = x.shape
    n = plan.n_dp
    return pl.pallas_call(
        functools.partial(out_kernel, n, plan.pieces_z),
        out_shape=[
            jax.ShapeDtypeStruct((rows, width), F32),
            jax.ShapeDtypeStruct((rows, width), BF16),
        ],
        in_specs=[smem(), vmem(), vmem(), vmem()] + [anywhere()] * (2 * n),
        out_specs=[vmem(), vmem()],
        scratch_shapes=[
            pltpu.VMEM((width, width), BF16),
            pltpu.SemaphoreType.DMA((n * plan.pieces_z,)),
        ],
        compiler_params=params(),
        cost_estimate=cost(2 * rows * width * width, 12 * rows * width + 2 * width * width),
        name="out_forward",
    )(plan.meta, o, x, gain, *vo[0], *vo[1])


def ffn_copies(meta, n_z, w1_own, w1_other, w2_own, w2_other, w1, w2, sems):
    section = meta[0]
    half1 = w1.shape[1] // 2
    half2 = w2.shape[1] // 2
    count = len(w1_own) * n_z

    def at(matrix, which, half):
        lanes = pl.ds(pl.multiple_of(which * half, 128), half)
        return lambda start, size: matrix.at[pl.ds(start, size), lanes]

    first = piece_copies(meta, w1_own, at(w1, section, half1), sems, 0, n_z)
    first += piece_copies(meta, w1_other, at(w1, 1 - section, half1), sems, count, n_z)
    second = piece_copies(meta, w2_own, at(w2, section, half2), sems, 2 * count, n_z)
    second += piece_copies(meta, w2_other, at(w2, 1 - section, half2), sems, 3 * count, n_z)
    return first, second


def ffn_kernel(n_dp, n_z, chunk, meta, b_ref, u2_ref, *refs):
    w1_own, w1_other, w2_own, w2_other = (refs[i * n_dp : (i + 1) * n_dp] for i in range(4))
    acts_ref, low_ref, h_ref, slope_ref, w1, w2, sems = refs[4 * n_dp :]
    first, second = ffn_copies(meta, n_z, w1_own, w1_other, w2_own, w2_other, w1, w2, sems)
    run(first)
    run(second)
    acts_ref[...] = u2_ref[...]
    wait(first)
    wait(second)

    def body(i, carry):
        at = pl.ds(pl.multiple_of(i * chunk, chunk), chunk)
        hp = nn(b_ref[...], w1[:, at])
        cdf = 0.5 * (1.0 + lax.erf(hp * (0.5**0.5)))
        density = jnp.exp(-0.5 * hp * hp) * 0.3989422804014327
        h = (hp * cdf).astype(BF16)
        h_ref[:, at] = h
        slope_ref[:, at] = (cdf + hp * density).astype(BF16)
        acts_ref[...] += nn(h, w2[at, :])
        return carry

    lax.fori_loop(0, w1.shape[1] // chunk, body, 0)
    low_ref[...] = acts_ref[...].astype(BF16)


def ffn_forward(plan, b, u2, w1, w2):
    rows, width = u2.shape
    n, hidden = plan.n_dp, plan.hidden
    return pl.pallas_call(
        functools.partial(ffn_kernel, n, plan.pieces_z, 512),
        out_shape=[
            jax.ShapeDtypeStruct((rows, width), F32),
            jax.ShapeDtypeStruct((rows, width), BF16),
            jax.ShapeDtypeStruct((rows, hidden), BF16),
            jax.ShapeDtypeStruct((rows, hidden), BF16),
        ],
        in_specs=[smem(), vmem(), vmem()] + [anywhere()] * (4 * n),
        out_specs=[vmem()] * 4,
        scratch_shapes=[
            pltpu.VMEM((width, hidden), BF16),
            pltpu.VMEM((hidden, width), BF16),
            pltpu.SemaphoreType.DMA((4 * n * plan.pieces_z,)),
        ],
        compiler_params=params(),
        cost_estimate=cost(
            4 * rows * width * hidden + 60 * rows * hidden,
            12 * rows * width + 4 * rows * hidden + 4 * width * hidden,
            2 * rows * hidden,
        ),
        name="ffn_forward",
    )(plan.meta, b, u2, *w1[0], *w1[1], *w2[0], *w2[1])


def ffn_back_kernel(n_dp, n_z, chunk, meta, c_ref, slope_ref, u2_ref, gain_ref, *refs):
    w1_own, w1_other, w2_own, w2_other, vo_own, vo_other = (
        refs[i * n_dp : (i + 1) * n_dp] for i in range(6)
    )
    cf_ref, dhp_ref, du2_ref, dz_ref, do_ref, dg_ref, w1, w2, wo, acc, sems = refs[6 * n_dp :]
    section = meta[0]
    count = n_dp * n_z
    first, second = ffn_copies(meta, n_z, w1_own, w1_other, w2_own, w2_other, w1, w2, sems)
    run(second)
    run(first)

    def at_o(start, size):
        return wo.at[pl.ds(start, size), :]

    own = piece_copies(meta, vo_own, at_o, sems, 4 * count, n_z)
    other = piece_copies(meta, vo_other, at_o, sems, 4 * count, n_z)

    @pl.when(section == 1)
    def _():
        run(own)

    @pl.when(section != 1)
    def _():
        run(other)

    cf_ref[...] = c_ref[...].astype(BF16)
    acc[...] = jnp.zeros_like(acc)
    wait(second)
    wait(first)

    def body(i, carry):
        at = pl.ds(pl.multiple_of(i * chunk, chunk), chunk)
        dh = nt(cf_ref[...], w2[at, :])
        dhp = (dh * slope_ref[:, at].astype(F32)).astype(BF16)
        dhp_ref[:, at] = dhp
        acc[...] += nt(dhp, w1[:, at])
        return carry

    lax.fori_loop(0, w1.shape[1] // chunk, body, 0)

    @pl.when(section == 1)
    def _():
        wait(own)

    @pl.when(section != 1)
    def _():
        wait(other)

    grad, dgain = norm_back(u2_ref[...], gain_ref[...], acc[...])
    du2 = c_ref[...].astype(F32) + grad
    du2_ref[...] = du2
    dg_ref[...] = dgain
    dz = du2.astype(BF16)
    dz_ref[...] = dz
    do_ref[...] = nt(dz, wo[...]).astype(BF16)


def ffn_backward(plan, c, slope, u2, gain, w1, w2, vo):
    rows, width = u2.shape
    n, hidden = plan.n_dp, plan.hidden
    wide = jax.ShapeDtypeStruct((rows, width), BF16)
    return pl.pallas_call(
        functools.partial(ffn_back_kernel, n, plan.pieces_z, 512),
        out_shape=[
            wide,
            jax.ShapeDtypeStruct((rows, hidden), BF16),
            jax.ShapeDtypeStruct((rows, width), F32),
            wide,
            wide,
            jax.ShapeDtypeStruct((1, width), F32),
        ],
        in_specs=[smem()] + [vmem()] * 4 + [anywhere()] * (6 * n),
        out_specs=[vmem()] * 6,
        scratch_shapes=[
            pltpu.VMEM((width, hidden), BF16),
            pltpu.VMEM((hidden, width), BF16),
            pltpu.VMEM((width, width), BF16),
            pltpu.VMEM((rows, width), F32),
            pltpu.SemaphoreType.DMA((5 * n * plan.pieces_z,)),
        ],
        compiler_params=params(),
        cost_estimate=cost(
            4 * rows * width * hidden + 2 * rows * width * width,
            18 * rows * width + 4 * rows * hidden + 4 * width * hidden + 2 * width * width,
        ),
        name="ffn_backward",
    )(plan.meta, c, slope, u2, gain, *w1[0], *w1[1], *w2[0], *w2[1], *vo[0], *vo[1])


def attention_back_kernel(chunks, key_block, q_ref, do_ref, o_ref, lse_ref, bias_ref, *refs):
    kv = refs[:chunks]
    dq_ref, dk_ref, dv_ref = refs[chunks : chunks + 3]
    far = refs[chunks + 3 : 2 * chunks + 2]
    kt_scr, dk_scr, dv_scr = refs[2 * chunks + 2 :]
    rows = q_ref.shape[0]
    per_chunk = rows // key_block
    query, grad = q_ref[...], do_ref[...]
    for c in range(chunks):
        kt_scr[:, c * rows : (c + 1) * rows] = jnp.transpose(kv[c][0])
    products = jnp.transpose(grad.astype(F32) * o_ref[...].astype(F32))
    outs = []
    for head in range(2):
        mask = lane_mask(query.shape, head)
        masked_query = jnp.where(mask, query, jnp.zeros_like(query))
        masked_grad = jnp.where(mask, grad, jnp.zeros_like(grad))
        extended = with_ones(masked_query)
        delta = jnp.sum(products[head * HD : (head + 1) * HD], axis=0, keepdims=True)
        lse = lse_ref[0, head : head + 1, :]
        dqt = jnp.zeros((PAIR, rows), F32)
        for c in range(chunks):
            for j in range(per_chunk):
                at = slice(j * key_block, (j + 1) * key_block)
                everywhere = slice(c * rows + at.start, c * rows + at.stop)
                keys = jnp.concatenate([kv[c][0, at, :], bias_ref[everywhere, :]], axis=1)
                weights = jnp.exp(nt(keys, extended) - lse)
                grad_weights = nt(kv[c][1, at, :], masked_grad)
                grad_scores = (weights * (grad_weights - delta)).astype(BF16)
                dv = nn(weights.astype(BF16), masked_grad)
                dk = nn(grad_scores, masked_query)
                dqt = dqt + nn(kt_scr[:, everywhere], grad_scores)
                if head == 0:
                    dv_scr[everywhere, :] = dv
                    dk_scr[everywhere, :] = dk
                elif c == 0:
                    dk_ref[at, :] = dk_scr[everywhere, :] + dk
                    dv_ref[at, :] = dv_scr[everywhere, :] + dv
                else:
                    far[c - 1][0, at, :] = (dk_scr[everywhere, :] + dk).astype(BF16)
                    far[c - 1][1, at, :] = (dv_scr[everywhere, :] + dv).astype(BF16)
        outs.append(dqt)
    row = lax.broadcasted_iota(jnp.int32, outs[0].shape, 0)
    dq_ref[...] = jnp.transpose(jnp.where(row < HD, outs[0], outs[1])).astype(BF16)


def attention_backward(plan, query, grad, o, lse, bias, kv):
    rows, width = query.shape
    chunks = len(kv)
    keys = chunks * rows
    pair_block = pl.BlockSpec((rows, PAIR), lambda p: (0, p))
    kv_block = pl.BlockSpec((2, rows, PAIR), lambda p: (0, 0, p))
    near = jax.ShapeDtypeStruct((rows, width), F32)
    return pl.pallas_call(
        functools.partial(attention_back_kernel, chunks, min(256, rows)),
        out_shape=[jax.ShapeDtypeStruct((rows, width), BF16), near, near]
        + [jax.ShapeDtypeStruct((2, rows, width), BF16)] * (chunks - 1),
        grid=(plan.pairs,),
        in_specs=[pair_block] * 3
        + [
            pl.BlockSpec((1, 8, rows), lambda p: (p, 0, 0)),
            pl.BlockSpec((keys, PAIR), lambda p: (0, 0)),
        ]
        + [kv_block] * chunks,
        out_specs=[pair_block] * 3 + [kv_block] * (chunks - 1),
        scratch_shapes=[
            pltpu.VMEM((PAIR, keys), BF16),
            pltpu.VMEM((keys, PAIR), F32),
            pltpu.VMEM((keys, PAIR), F32),
        ],
        compiler_params=params(),
        cost_estimate=cost(
            40 * rows * keys * width,
            16 * rows * width + 8 * keys * width,
            rows * keys * plan.heads,
        ),
        name="attention_backward",
    )(query, grad, o, lse, bias, *kv)


def qkv_back_kernel(
    n_dp, n_z, n_far, meta, dq_ref, dk_ref, dv_ref, du2_ref, x_ref, gain_ref, cos_ref, sin_ref, *refs
):
    far = refs[:n_far]
    qk_own, qk_other, vo_own, vo_other = (
        refs[n_far + i * n_dp : n_far + (i + 1) * n_dp] for i in range(4)
    )
    dqkv_ref, dx_ref, low_ref, dg_ref, wqk, wv, sems = refs[n_far + 4 * n_dp :]
    section = meta[0]
    count = n_dp * n_z

    def at_half(which):
        return lambda start, size: wqk.at[which, pl.ds(start, size), :]

    def at_v(start, size):
        return wv.at[pl.ds(start, size), :]

    qk = piece_copies(meta, qk_own, at_half(section), sems, 0, n_z)
    qk += piece_copies(meta, qk_other, at_half(1 - section), sems, count, n_z)
    run(qk)
    v_own = piece_copies(meta, vo_own, at_v, sems, 2 * count, n_z)
    v_other = piece_copies(meta, vo_other, at_v, sems, 2 * count, n_z)

    @pl.when(section == 0)
    def _():
        run(v_own)

    @pl.when(section != 0)
    def _():
        run(v_other)

    rows, width = x_ref.shape
    cos, sin = cos_ref[...], sin_ref[...]
    for pair in range(width // PAIR):
        lanes = slice(pair * PAIR, (pair + 1) * PAIR)
        dq = dq_ref[:, lanes].astype(F32) * HD**-0.5
        dk, dv = dk_ref[:, lanes], dv_ref[:, lanes]
        for part in far:
            dk = dk + part[0, :, lanes].astype(F32)
            dv = dv + part[1, :, lanes].astype(F32)
        dk = dk.astype(BF16).astype(F32)
        dqkv_ref[:, pair * PAIR : (pair + 1) * PAIR] = (dq * cos - swap_halves(dq) * sin).astype(BF16)
        at = width + pair * PAIR
        dqkv_ref[:, at : at + PAIR] = (dk * cos - swap_halves(dk) * sin).astype(BF16)
        at = 2 * width + pair * PAIR
        dqkv_ref[:, at : at + PAIR] = dv.astype(BF16)
    wait(qk)

    @pl.when(section == 0)
    def _():
        wait(v_own)

    @pl.when(section != 0)
    def _():
        wait(v_other)

    da = nt(dqkv_ref[:, :width], wqk[0])
    da = da + nt(dqkv_ref[:, width : 2 * width], wqk[1])
    da = da + nt(dqkv_ref[:, 2 * width :], wv[...])
    grad, dgain = norm_back(x_ref[...], gain_ref[...], da)
    dx = du2_ref[...] + grad
    dx_ref[...] = dx
    low_ref[...] = dx.astype(BF16)
    dg_ref[...] = dgain


def qkv_backward(plan, dq, dk, dv, far, du2, x, gain, cos, sin, qk, vo):
    rows, width = x.shape
    n = plan.n_dp
    return pl.pallas_call(
        functools.partial(qkv_back_kernel, n, plan.pieces_z, len(far)),
        out_shape=[
            jax.ShapeDtypeStruct((rows, 3 * width), BF16),
            jax.ShapeDtypeStruct((rows, width), F32),
            jax.ShapeDtypeStruct((rows, width), BF16),
            jax.ShapeDtypeStruct((1, width), F32),
        ],
        in_specs=[smem()] + [vmem()] * (8 + len(far)) + [anywhere()] * (4 * n),
        out_specs=[vmem()] * 4,
        scratch_shapes=[
            pltpu.VMEM((2, width, width), BF16),
            pltpu.VMEM((width, width), BF16),
            pltpu.SemaphoreType.DMA((3 * n * plan.pieces_z,)),
        ],
        compiler_params=params(),
        cost_estimate=cost(6 * rows * width * width, 30 * rows * width + 6 * width * width),
        name="qkv_backward",
    )(plan.meta, dq, dk, dv, du2, x, gain, cos, sin, *far, *qk[0], *qk[1], *vo[0], *vo[1])


def weight_kernel(n_dp, n_z, mine, half, start, chunk, meta, left_ref, right_ref, *refs):
    if mine:
        got_ref, outs, acc = refs[0], refs[1:-1], refs[-1]
    else:
        got_ref, outs, acc = None, refs[:-1], refs[-1]
    cols = acc.shape[1]
    which = meta[0] if mine else 1 - meta[0]
    lanes = pl.ds(pl.multiple_of(which * half + start, 128), cols)

    def body(i, carry):
        at = pl.ds(pl.multiple_of(i * chunk, chunk), chunk)
        acc[at, :] = tn(left_ref[:, at], right_ref[:, lanes])
        return carry

    total = acc.shape[0]
    lax.fori_loop(0, total // chunk, body, 0)
    block = total // n_dp
    for mask, row, begin, size in block_starts(meta, n_dp, n_z, block):
        rows = acc[pl.ds(pl.multiple_of(begin, 8), size), :]
        at = slice(mask * block + row, mask * block + row + size)
        if mine:
            outs[mask][row : row + size, :] = (rows + got_ref[at, :].astype(F32)).astype(BF16)
        else:
            outs[0][at, :] = rows.astype(BF16)


def weight_half(plan, left, right, half, start, cols, got):
    rows, total = left.shape
    n = plan.n_dp
    mine = got is not None
    out = jax.ShapeDtypeStruct((total // n, cols), BF16)
    result = pl.pallas_call(
        functools.partial(weight_kernel, n, plan.pieces_z, mine, half, start, 256),
        out_shape=[out] * n if mine else [jax.ShapeDtypeStruct((total, cols), BF16)],
        in_specs=[smem(), vmem(), vmem()] + ([vmem()] if mine else []),
        out_specs=[vmem()] * (n if mine else 1),
        scratch_shapes=[pltpu.VMEM((total, cols), F32)],
        compiler_params=params(),
        cost_estimate=cost(
            2 * rows * total * cols, 2 * rows * (total + cols) + 2 * total * cols * (2 if mine else 1)
        ),
        name="weight_half",
    )(plan.meta, left, right, *([got] if mine else []))
    return result if mine else result[0]


def weight_grad(plan, left, right, cols, start, low_first):
    half = right.shape[1] // 2
    theirs = weight_half(plan, left, right, half, start, cols, None)
    pieces = weight_half(plan, left, right, half, start, cols, other_core(theirs))
    return collect(plan, pieces, low_first)


def by_section(plan, first, second):
    return jnp.where(plan.section == 0, first, second)


def take_half(plan, matrix, which):
    half = matrix.shape[-1] // 2
    return lax.dynamic_slice_in_dim(matrix, which * half, half, axis=matrix.ndim - 1)


def to_sequences(plan, tokens):
    pieces = tokens.reshape(plan.n_seq, 2, plan.half, plan.width)
    mine = lax.dynamic_index_in_dim(pieces, plan.section, 1, keepdims=False)
    mine = mine.reshape(plan.n_ctx, plan.sub, plan.width)
    moved = lax.all_to_all(mine, "ctx", 0, 0, tiled=True)
    return moved.reshape(plan.rows, plan.width)


def from_sequences(plan, rows):
    pieces = rows.reshape(plan.n_ctx, plan.sub, plan.width)
    moved = lax.all_to_all(pieces, "ctx", 0, 0, tiled=True)
    return moved.reshape(plan.n_seq, plan.half, plan.width)


def to_output(plan, layers):
    own = by_section(plan, layers[0], layers[1])
    got = other_core(by_section(plan, layers[1], layers[0]))
    first = by_section(plan, own, got)
    second = by_section(plan, got, own)
    both = jnp.stack([first, second], axis=1).astype(F32)
    return both.reshape(1, plan.micro, plan.seqs, plan.span, plan.width)


def gather_gains(plan, gain_attn, gain_ffn):
    own = jnp.stack([gain_attn[0], gain_ffn[0]]).astype(BF16)
    got = other_core(own)
    both = jnp.stack([by_section(plan, own, got), by_section(plan, got, own)])
    block = both.reshape(1, -1)
    parts = [block]
    for d in range(1, plan.n_ctx):
        parts.append(xor_ctx(plan, block, d))
    block = jnp.concatenate(parts, axis=0)
    for bit in range(plan.dp_bits):
        block = jnp.concatenate([block, xor_dp(plan, block, bit)], axis=0)
    total = plan.n_ctx * plan.n_dp
    place = jnp.arange(total)
    source = (((place // plan.n_ctx) ^ plan.dp) * plan.n_ctx) + ((place % plan.n_ctx) ^ plan.ctx)
    chosen = (jnp.arange(total)[:, None] == source[None, :]).astype(F32)
    ordered = jnp.dot(chosen, block.astype(F32), precision=lax.Precision.HIGHEST)
    gains = ordered.reshape(total, 2, 2, -1).transpose(1, 2, 0, 3).reshape(2, 2, 1, plan.width)
    return gains


def sum_gains(plan, gains):
    total = gains + other_core(gains)
    for bit in range(plan.dp_bits):
        total = total + xor_dp(plan, total, bit)
    mask = 1
    while mask < plan.n_ctx:
        total = total + xor_ctx(plan, total, mask)
        mask *= 2
    layer = lax.dynamic_slice_in_dim(total, plan.section * 2, 2, axis=0)
    size = plan.width // (plan.n_dp * plan.n_ctx)
    place = (plan.dp * plan.n_ctx + plan.ctx) * size
    mine = lax.dynamic_slice_in_dim(layer, place, size, axis=1)
    return mine[0:1], mine[1:2]


def shared_keys(plan, own):
    chunks = []
    for mask in range(plan.parts):
        here = own if mask == 0 else xor_ctx(plan, own, mask)
        chunks += [here, other_core(here)]
    return chunks


def return_keys(plan, far):
    got = []
    for mask in range(plan.parts):
        for core in range(2):
            index = 2 * mask + core
            if index == 0:
                continue
            part = far[index - 1]
            if core:
                part = other_core(part)
            if mask:
                part = xor_ctx(plan, part, mask)
            got.append(part)
    return got


def positions_of(plan, section, ctx):
    part = ctx % plan.parts
    start = jnp.arange(plan.n_ctx)[:, None] * plan.span + section * plan.half + part * plan.sub
    return (start + jnp.arange(plan.sub)[None, :]).reshape(-1)


def rope_tables(positions):
    half_width = HD // 2
    frequency = jnp.power(10000.0, -(jnp.arange(half_width).astype(F32) * 2.0) / HD)
    angles = positions.astype(F32)[:, None] * frequency[None, :]
    cos, sin = jnp.cos(angles), jnp.sin(angles)
    return jnp.concatenate([cos] * 4, axis=1), jnp.concatenate([-sin, sin, -sin, sin], axis=1)


def local(tokens, upstream, lengths, w_qkv, w_out, w_in, w_back, gain_attn, gain_ffn):
    plan = Plan(tokens, w_in)
    width = plan.width
    layers = 2

    qkv_low, out_low = w_qkv[0].astype(BF16), w_out[0].astype(BF16)
    in_low, back_low = w_in[0].astype(BF16), w_back[0].astype(BF16)
    here, there = plan.section, 1 - plan.section

    def halves(which):
        return (
            take_half(plan, qkv_low[:, : 2 * width], which),
            jnp.where(which == 0, qkv_low[:, 2 * width :], out_low),
            take_half(plan, in_low, which),
            take_half(plan, back_low, which),
        )

    kept = halves(here)
    got = [other_core(value) for value in halves(there)]
    shards = [
        [by_section(plan, k, g) for k, g in zip(kept, got)],
        [by_section(plan, g, k) for k, g in zip(kept, got)],
    ]

    source = to_sequences(plan, tokens).astype(F32)
    gains = gather_gains(plan, gain_attn, gain_ffn)
    weights = []
    for layer in range(layers):
        qk, vo, first, second = shards[layer]
        weights.append(
            (
                spread(plan, qk, True),
                spread(plan, vo, False),
                spread(plan, first, True),
                spread(plan, second, False),
            )
        )
    cotangent = to_sequences(plan, upstream)

    cos, sin = rope_tables(positions_of(plan, plan.section, plan.ctx))
    sequence = plan.ctx // plan.parts
    length = lax.dynamic_index_in_dim(lengths.reshape(-1), sequence, 0, keepdims=False)
    places = []
    for mask in range(plan.parts):
        for core in range(2):
            places.append(positions_of(plan, plan.section ^ core, plan.ctx ^ mask))
    hidden_key = jnp.where(jnp.concatenate(places) < length, 0.0, MASKED)
    lane = jnp.arange(PAIR)
    bias = jnp.where(lane[None, :] == 0, hidden_key[:, None], 0.0).astype(BF16)

    saved, acts = [], []
    x = source
    for layer in range(layers):
        qk, vo, first, second = weights[layer]
        a, query, own_kv = qkv_forward(plan, x, gains[layer, 0], cos, sin, qk, vo)
        kv = shared_keys(plan, own_kv)
        o, lse = attention_forward(plan, query, kv, bias)
        u2, b = out_forward(plan, o, x, gains[layer, 1], vo)
        result, low, h, slope = ffn_forward(plan, b, u2, first, second)
        saved.append((x, a, query, kv, o, lse, u2, b, h, slope))
        acts.append(from_sequences(plan, low))
        x = result

    c = cotangent
    grads, sums, dgains = [None] * layers, [None] * layers, [None] * layers
    for layer in reversed(range(layers)):
        qk, vo, first, second = weights[layer]
        x, a, query, kv, o, lse, u2, b, h, slope = saved[layer]
        cf, dhp, du2, dz, do, dg2 = ffn_backward(
            plan, c, slope, u2, gains[layer, 1], first, second, vo
        )
        d_in = weight_grad(plan, b, dhp, plan.hidden // 2, 0, True)
        d_back = weight_grad(plan, h, cf, width // 2, 0, False)
        dq, dk, dv, *far = attention_backward(plan, query, do, o, lse, bias, kv)
        far = return_keys(plan, far)
        d_out = weight_grad(plan, o, dz, width // 2, 0, True)
        dqkv, dx, low, dg1 = qkv_backward(
            plan, dq, dk, dv, far, du2, x, gains[layer, 0], cos, sin, qk, vo
        )
        wide = 3 * width // 2
        cut = (wide // 2 + 127) // 128 * 128
        d_qkv = jnp.concatenate(
            [
                weight_grad(plan, a, dqkv, cut, 0, True),
                weight_grad(plan, a, dqkv, wide - cut, cut, False),
            ],
            axis=1,
        )
        grads[layer] = from_sequences(plan, low)
        sums[layer] = (d_qkv, d_out, d_in, d_back)
        dgains[layer] = (dg1, dg2)
        c = dx

    def to_owner(first, second):
        own = by_section(plan, first, second)
        got = other_core(by_section(plan, second, first))
        left, right = by_section(plan, own, got), by_section(plan, got, own)
        return jnp.concatenate([left, right], axis=1).astype(F32)[None]

    weight_grads = [to_owner(one, two) for one, two in zip(*sums)]
    gain_sums = sum_gains(plan, jnp.concatenate([g for pair in dgains for g in pair], axis=0))
    return (to_output(plan, acts), to_output(plan, grads), *weight_grads, *gain_sums)


def solution(mesh):
    rows = P(None, "dp", "ctx", None)
    weight = P("section", ("dp", "ctx"), None)
    gain = P("section", ("dp", "ctx"))
    out_rows = P("section", None, "dp", "ctx", None)
    return jax.shard_map(
        local,
        mesh=mesh,
        in_specs=(rows, rows, P(None, "dp"), weight, weight, weight, weight, gain, gain),
        out_specs=(out_rows, out_rows, weight, weight, weight, weight, gain, gain),
        check_vma=False,
    )
```

time: 2290 us -> 803 us (0.35)
  waiting for transfers between devices: 1300 us -> 216 us
  matrix products: 478 us -> 0.12 us
  Pallas kernels: 0 us -> 292 us
  starting transfers between devices: 12.3 us -> 226 us
  local copies, waits for them, and re-layouts: 204 us -> 23.2 us
  other arithmetic: 187 us -> 32.5 us
  blocking collectives: 71.1 us -> 0 us
    reduce_scatter x10 -> x0, waiting for transfers between devices: 807 us -> none  [the longest x1 178 us: local(): lax.psum_scatter(sum_in, ('dp', 'ctx'), scatter_dimension=0, tiled=True)]
    all_gather x16 -> x0, waiting for transfers between devices: 488 us -> none  [the longest x3 110 us: local(): lax.all_gather(forward_key_rows, 'ctx', axis=1, tiled=True)]
    dot_general x57 -> x1, matrix products: 478 us -> 0.12 us  [gather_gains(): jnp.dot(chosen, block.astype(F32), precision=lax.Precision.HIGHEST)]
    pallas_call x0 -> x34, Pallas kernels: none -> 292 us  [the longest x20 104 us: weight_half(): pl.pallas_call(functools.partial(weight_kernel, n, plan.pieces_z, mine, h...]
    ppermute x4 -> x175, waiting for transfers between devices: 5.35 us -> 216 us  [the longest x58 118 us: xor_dp(): lax.ppermute(value, 'dp', [(i, i ^ 1 << bit) for i in range(plan.n_dp)])]
    ppermute x4 -> x175, starting transfers between devices: 10 us -> 200 us  [the longest x58 85 us: other_core(): return lax.ppermute(value, 'section', [(0, 1), (1, 0)])]
    unnamed x2 -> x0, blocking collectives: 71.1 us -> none
    convert_element_type x24 -> x35, other arithmetic: 71.6 us -> 14.1 us  [the longest x20 6.11 us: collect(): (pieces[mask].astype(F32) + got[mask].astype(F32)).astype(BF16)]
  transfers between devices with their start and end apart: 30 -> 181, of which waited for: 22 -> 52; matrix products, arithmetic and copies ran while one was open for 29% -> 5% of each run, Pallas kernels for 0% -> 37%
where the time goes in v1:
time: 803 us; the launch traced here: 792 us
  Pallas kernels  292 us (36%)
  starting transfers between devices  226 us (28%)
  waiting for transfers between devices  216 us (27%)
  other arithmetic  32.5 us (4%)
  local copies, waits for them, and re-layouts  23.2 us (3%)
    ppermute x58, waiting for transfers between devices, xor_dp(): lax.ppermute(value, 'dp', [(i, i ^ 1 << bit) for i in range(plan.n_dp)])  118 us
    pallas_call x20, Pallas kernels, weight_half(): pl.pallas_call(functools.partial(weight_kernel, n, plan.pieces_z, mine, h...  104 us
    ppermute x59, waiting for transfers between devices, xor_ctx(): lax.ppermute(value, 'ctx', [(i, i ^ mask) for i in range(plan.n_ctx)])  93.7 us
    ppermute x58, starting transfers between devices, other_core(): return lax.ppermute(value, 'section', [(0, 1), (1, 0)])  85 us
    ppermute x59, starting transfers between devices, xor_ctx(): lax.ppermute(value, 'ctx', [(i, i ^ mask) for i in range(plan.n_ctx)])  68 us
    ppermute x58, starting transfers between devices, xor_dp(): lax.ppermute(value, 'dp', [(i, i ^ 1 << bit) for i in range(plan.n_dp)])  47 us
    pallas_call x2, Pallas kernels, attention_backward(): pl.pallas_call(functools.partial(attention_back_kernel, chunks, min(256,...  41.3 us
    pallas_call x2, Pallas kernels, ffn_backward(): pl.pallas_call(functools.partial(ffn_back_kernel, n, plan.pieces_z, 512),...  34.1 us
  transfers between devices with their start and end apart: 181, of which 52 were waited for; matrix products, arithmetic and copies ran while one was open for 5% of the time, Pallas kernels for 37%

profile of v1, /device:TPU:1, one launch (start us, length us, event | category | flops | bytes accessed | tf_op | source)
XLA Modules:
  0.0 791.8 jit_solution(3721645344248650224)
XLA Ops:
  15.9 12.6 %collective-permute-done.3 = bf16[1,192]{1,0:T(2,128)(2,1)S(1)} collective-permute-done((bf16[1,192]{1,0:T(2,128)(2,1)S(1)}, bf16[1,192]{1,0:T(2,128)(2,1)S(1)}, u32[]{:S(2)}, u32[]{:S(2)}) %collective-permute-start.3) | collective-permute-done | bytes 416 | tf_op jit(solution)/shard_map/ppermute | solution.py:88
  64.3 7.4 collective-permute-done.19
  86.9 7.3 collective-permute-done.83
  145.3 7.7 qkv_forward.2
  157.5 12.1 %collective-permute-done.45.refs_10_ = bf16[768,384]{1,0:T(8,128)(2,1)} collective-permute-done((bf16[768,384]{1,0:T(8,128)(2,1)}, bf16[768,384]{1,0:T(8,128)(2,1)}, u32[]{:S(2)}, u32[]{:S(2)}) %collective-permute-start.45) | collective-permute-done | bytes 589856 | tf_op jit(solution)/shard_map/ppermute | solution.py:84
  172.3 10.1 %collective-permute-done.33.refs_1_ = bf16[192,1536]{1,0:T(8,128)(2,1)} collective-permute-done((bf16[192,1536]{1,0:T(8,128)(2,1)S(1)}, bf16[192,1536]{1,0:T(8,128)(2,1)}, u32[]{:S(2)}, u32[]{:S(2)}) %collective-permute-start.33) | collective-permute-done | bytes 589856 | tf_op jit(solution)/shard_map/ppermute | solution.py:84
  198.5 14.1 %attention_forward.2 = (bf16[512,768]{1,0:T(8,128)(2,1)}, f32[6,8,512]{2,1,0:T(8,128)}) custom-call(bf16[512,768]{1,0:T(8,128)(2,1)} %get-tuple-element.96.q_ref, bf16[2,512,768]{2,1,0:T(8,128)(2,1)} %get-tuple-element.97.refs_0_, bf16[2,512,768]{2,1,0:T(8,128)(2,1)} %collective-permute-done.28.refs_1_, bf16[1024,128]{1,0:T(8,128)(2,1)} %select_convert_fusion.refs_2_.bias_ref), custom_call_target="tpu_custom_call" | custom-call | flops 6442450944 | bytes 4718592 | tf_op jit(solution)/shard_map/attention_forward/pallas_call | solution.py:320
  220.9 17.0 %ffn_forward.2 = (f32[512,768]{1,0:T(8,128)}, bf16[512,768]{1,0:T(8,128)(2,1)}, bf16[512,3072]{1,0:T(8,128)(2,1)}, bf16[512,3072]{1,0:T(8,128)(2,1)}) custom-call(s32[3]{0:T(128)} %pad_add_fusion.meta, bf16[512,768]{1,0:T(8,128)(2,1)} %get-tuple-element.99.b_ref.left_ref, f32[512,768]{1,0:T(8,128)} %get-tuple-element.100.u2_ref, ...), custom_call_target="tpu_custom_call" | custom-call | flops 4926210048 | bytes 20447232 | tf_op jit(solution)/shard_map/ffn_forward/pallas_call | solution.py:438
  239.0 7.7 qkv_forward.3
  268.4 7.3 collective-permute-done.85.refs_9_
  279.1 9.3 %collective-permute-done.75.refs_1_ = bf16[192,1536]{1,0:T(8,128)(2,1)} collective-permute-done((bf16[192,1536]{1,0:T(8,128)(2,1)S(1)}, bf16[192,1536]{1,0:T(8,128)(2,1)}, u32[]{:S(2)}, u32[]{:S(2)}) %collective-permute-start.75) | collective-permute-done | bytes 589856 | tf_op jit(solution)/shard_map/ppermute | solution.py:84
  304.4 14.1 %attention_forward.3 = (bf16[512,768]{1,0:T(8,128)(2,1)}, f32[6,8,512]{2,1,0:T(8,128)}) custom-call(bf16[512,768]{1,0:T(8,128)(2,1)} %get-tuple-element.103.q_ref, bf16[2,512,768]{2,1,0:T(8,128)(2,1)} %get-tuple-element.104.refs_0_, bf16[2,512,768]{2,1,0:T(8,128)(2,1)} %collective-permute-done.71.refs_1_, bf16[1024,128]{1,0:T(8,128)(2,1)} %select_convert_fusion.refs_2_.bias_ref), custom_call_target="tpu_custom_call" | custom-call | flops 6442450944 | bytes 4718592 | tf_op jit(solution)/shard_map/attention_forward/pallas_call | solution.py:320
  325.9 16.9 %ffn_forward.3 = (f32[512,768]{1,0:T(8,128)}, bf16[512,768]{1,0:T(8,128)(2,1)}, bf16[512,3072]{1,0:T(8,128)(2,1)}, bf16[512,3072]{1,0:T(8,128)(2,1)}) custom-call(s32[3]{0:T(128)} %pad_add_fusion.meta, bf16[512,768]{1,0:T(8,128)(2,1)} %get-tuple-element.106.b_ref.left_ref, f32[512,768]{1,0:T(8,128)} %get-tuple-element.107.u2_ref, ...), custom_call_target="tpu_custom_call" | custom-call | flops 4926210048 | bytes 20447232 | tf_op jit(solution)/shard_map/ffn_forward/pallas_call | solution.py:438
  346.5 17.0 %ffn_backward.2 = (bf16[512,768]{1,0:T(8,128)(2,1)}, bf16[512,3072]{1,0:T(8,128)(2,1)}, f32[512,768]{1,0:T(8,128)}, bf16[512,768]{1,0:T(8,128)(2,1)}, bf16[512,768]{1,0:T(8,128)(2,1)}, /*index=5*/f32[1,768]{1,0:T(1,128)}) custom-call(s32[3]{0:T(128)} %pad_add_fusion.meta, bf16[512,768]{1,0:T(8,128)(2,1)} %bitcast.91, ...), custom_call_target="tpu_custom_call" | custom-call | flops 5435817984 | bytes 23986176 | tf_op jit(solution)/shard_map/ffn_backward/pallas_call | solution.py:524
  367.3 20.6 %attention_backward.2 = (bf16[512,768]{1,0:T(8,128)(2,1)}, f32[512,768]{1,0:T(8,128)}, f32[512,768]{1,0:T(8,128)}, bf16[2,512,768]{2,1,0:T(8,128)(2,1)}) custom-call(bf16[512,768]{1,0:T(8,128)(2,1)} %get-tuple-element.103.q_ref, bf16[512,768]{1,0:T(8,128)(2,1)} %get-tuple-element.110.do_ref, bf16[512,768]{1,0:T(8,128)(2,1)} %get-tuple-element.105.o_ref.left_ref, ...), custom_call_target="tpu_custom_call" | custom-call | flops 16106127360 | bytes 12582912 | tf_op jit(solution)/shard_map/attention_backward/pallas_call | solution.py:604
  403.8 7.8 weight_half.38
  423.2 11.5 %qkv_backward.2 = (bf16[512,2304]{1,0:T(8,128)(2,1)}, f32[512,768]{1,0:T(8,128)}, bf16[512,768]{1,0:T(8,128)(2,1)}, f32[1,768]{1,0:T(1,128)}) custom-call(s32[3]{0:T(128)} %pad_add_fusion.meta, bf16[512,768]{1,0:T(8,128)(2,1)} %get-tuple-element.112.dq_ref, f32[512,768]{1,0:T(8,128)} %get-tuple-element.113.dk_ref, f32[512,768]{1,0:T(8,128)} %get-tuple-element.114.dv_ref, ...), custom_call_target="tpu_custom_call" | custom-call | flops 1811939328 | bytes 15335424 | tf_op jit(solution)/shard_map/qkv_backward/pallas_call | solution.py:700
  438.5 17.1 %ffn_backward.3 = (bf16[512,768]{1,0:T(8,128)(2,1)}, bf16[512,3072]{1,0:T(8,128)(2,1)}, f32[512,768]{1,0:T(8,128)}, bf16[512,768]{1,0:T(8,128)(2,1)}, bf16[512,768]{1,0:T(8,128)(2,1)}, /*index=5*/f32[1,768]{1,0:T(1,128)}) custom-call(s32[3]{0:T(128)} %pad_add_fusion.meta, f32[512,768]{1,0:T(8,128)} %get-tuple-element.117.c_ref, ...), custom_call_target="tpu_custom_call" | custom-call | flops 5435817984 | bytes 23986176 | tf_op jit(solution)/shard_map/ffn_backward/pallas_call | solution.py:524
  459.1 20.7 %attention_backward.3 = (bf16[512,768]{1,0:T(8,128)(2,1)}, f32[512,768]{1,0:T(8,128)}, f32[512,768]{1,0:T(8,128)}, bf16[2,512,768]{2,1,0:T(8,128)(2,1)}) custom-call(bf16[512,768]{1,0:T(8,128)(2,1)} %get-tuple-element.96.q_ref, bf16[512,768]{1,0:T(8,128)(2,1)} %get-tuple-element.119.do_ref, bf16[512,768]{1,0:T(8,128)(2,1)} %get-tuple-element.98.o_ref.left_ref, ...), custom_call_target="tpu_custom_call" | custom-call | flops 16106127360 | bytes 12582912 | tf_op jit(solution)/shard_map/attention_backward/pallas_call | solution.py:604
  493.4 8.0 %weight_half.36 = bf16[3072,384]{1,0:T(8,128)(2,1)} custom-call(s32[3]{0:T(128)} %pad_add_fusion.meta, bf16[512,3072]{1,0:T(8,128)(2,1)} %get-tuple-element.168.left_ref, bf16[512,768]{1,0:T(8,128)(2,1)} %get-tuple-element.169.right_ref), custom_call_target="tpu_custom_call" | custom-call | flops 1207959552 | bytes 5898240 | tf_op jit(solution)/shard_map/weight_half/pallas_call | solution.py:752
  516.0 8.6 %weight_half.39 = (bf16[768,384]{1,0:T(8,128)(2,1)}, bf16[768,384]{1,0:T(8,128)(2,1)}, bf16[768,384]{1,0:T(8,128)(2,1)}, bf16[768,384]{1,0:T(8,128)(2,1)}) custom-call(s32[3]{0:T(128)} %pad_add_fusion.meta, bf16[512,3072]{1,0:T(8,128)(2,1)} %get-tuple-element.174.left_ref, bf16[512,768]{1,0:T(8,128)(2,1)} %get-tuple-element.175.right_ref, ...), custom_call_target="tpu_custom_call" | custom-call | flops 1207959552 | bytes 8257536 | tf_op jit(solution)/shard_map/weight_half/pallas_call | solution.py:752
  529.6 6.9 weight_half.35
  576.0 7.6 collective-permute-done.149
  585.8 11.6 %qkv_backward.3 = (bf16[512,2304]{1,0:T(8,128)(2,1)}, f32[512,768]{1,0:T(8,128)}, bf16[512,768]{1,0:T(8,128)(2,1)}, f32[1,768]{1,0:T(1,128)}) custom-call(s32[3]{0:T(128)} %pad_add_fusion.meta, bf16[512,768]{1,0:T(8,128)(2,1)} %get-tuple-element.121.dq_ref, f32[512,768]{1,0:T(8,128)} %get-tuple-element.122.dk_ref, f32[512,768]{1,0:T(8,128)} %get-tuple-element.123.dv_ref, ...), custom_call_target="tpu_custom_call" | custom-call | flops 1811939328 | bytes 15335424 | tf_op jit(solution)/shard_map/qkv_backward/pallas_call | solution.py:700
  615.4 8.3 %collective-permute-done.172 = f32[4,768]{1,0:T(4,128)S(1)} collective-permute-done((f32[4,768]{1,0:T(4,128)S(1)}, f32[4,768]{1,0:T(4,128)S(1)}, u32[]{:S(2)}, u32[]{:S(2)}) %collective-permute-start.172) | collective-permute-done | bytes 12320 | tf_op jit(solution)/shard_map/ppermute | solution.py:84
  663.4 8.6 %weight_half.37 = (bf16[768,384]{1,0:T(8,128)(2,1)}, bf16[768,384]{1,0:T(8,128)(2,1)}, bf16[768,384]{1,0:T(8,128)(2,1)}, bf16[768,384]{1,0:T(8,128)(2,1)}) custom-call(s32[3]{0:T(128)} %pad_add_fusion.meta, bf16[512,3072]{1,0:T(8,128)(2,1)} %get-tuple-element.168.left_ref, bf16[512,768]{1,0:T(8,128)(2,1)} %get-tuple-element.169.right_ref, ...), custom_call_target="tpu_custom_call" | custom-call | flops 1207959552 | bytes 8257536 | tf_op jit(solution)/shard_map/weight_half/pallas_call | solution.py:752
  672.0 6.4 weight_half.33
  703.7 6.9 collective-permute-done.157
  726.8 10.6 %collective-permute-done.143 = bf16[192,1536]{1,0:T(8,128)(2,1)S(1)} collective-permute-done((bf16[192,1536]{1,0:T(8,128)(2,1)S(1)}, bf16[192,1536]{1,0:T(8,128)(2,1)S(1)}, u32[]{:S(2)}, u32[]{:S(2)}) %collective-permute-start.143) | collective-permute-done | bytes 589856 | tf_op jit(solution)/shard_map/ppermute | solution.py:84
  757.4 12.3 %collective-permute-done.160 = bf16[192,384]{1,0:T(8,128)(2,1)S(1)} collective-permute-done((bf16[192,384]{1,0:T(8,128)(2,1)S(1)}, bf16[192,384]{1,0:T(8,128)(2,1)S(1)}, u32[]{:S(2)}, u32[]{:S(2)}) %collective-permute-start.160) | collective-permute-done | bytes 147488 | tf_op jit(solution)/shard_map/ppermute | solution.py:88
  769.8 6.3 collective-permute-start.169
  782.1 6.3 collective-permute-done.145
  (744 shorter events, 442.6 us)
Async XLA Ops:
  4.2 35.0 %collective-permute-start.17 = (bf16[48,768]{1,0:T(8,128)(2,1)S(1)}, bf16[48,768]{1,0:T(8,128)(2,1)S(1)}, u32[]{:S(2)}, u32[]{:S(2)}) collective-permute-start(bf16[48,768]{1,0:T(8,128)(2,1)S(1)} %bitcast_select_fusion.4), channel_id=1, source_target_pairs={{0,16},{16,0},{1,17},{17,1},{2,18},{18,2},{3,19},{19,3},{4,20},{20... | collective-permute-start | bytes 221192 | tf_op jit(solution)/shard_map/ppermute | solution.py:80
  4.7 32.3 %collective-permute-start.6 = (bf16[48,768]{1,0:T(8,128)(2,1)S(1)}, bf16[48,768]{1,0:T(8,128)(2,1)}, u32[]{:S(2)}, u32[]{:S(2)}) collective-permute-start(bf16[48,768]{1,0:T(8,128)(2,1)S(1)} %constant_dynamic-slice_fusion), channel_id=1, source_target_pairs={{0,16},{16,0},{1,17},{17,1},{2,18},{18,2},{3,19},{19,3},{4,20},{20... | collective-permute-start | bytes 221192 | tf_op jit(solution)/shard_map/ppermute | solution.py:80
  5.8 135.1 %all-to-all-start = ((bf16[4,128,768]{2,1,0:T(8,128)(2,1)}), bf16[4,128,768]{2,1,0:T(8,128)(2,1)S(1)}, u32[]{:S(2)}, u32[]{:S(2)}) async-start(bf16[4,128,768]{2,1,0:T(8,128)(2,1)} %dynamic-slice_bitcast_fusion.1), calls=%async_computation | async-start | bytes 1572864 | tf_op jit(solution)/shard_map/all_to_all | solution.py:787
  153.1 45.4 %collective-permute-start.28 = (bf16[2,512,768]{2,1,0:T(8,128)(2,1)}, bf16[2,512,768]{2,1,0:T(8,128)(2,1)}, u32[]{:S(2)}, u32[]{:S(2)}) collective-permute-start(bf16[2,512,768]{2,1,0:T(8,128)(2,1)} %get-tuple-element.97.refs_0_), channel_id=1, source_target_pairs={{0,16},{16,0},{1,17},{17,1},{2,18},{18,2},{3,19},{19,3},{4,20},{20... | collective-permute-start | bytes 4718600 | tf_op jit(solution)/shard_map/ppermute | solution.py:80
  185.8 33.7 %collective-permute-start.37 = (bf16[192,1536]{1,0:T(8,128)(2,1)}, bf16[192,1536]{1,0:T(8,128)(2,1)S(1)}, u32[]{:S(2)}, u32[]{:S(2)}) collective-permute-start(bf16[192,1536]{1,0:T(8,128)(2,1)} %collective-permute-done.33.refs_1_), channel_id=1, source_target_pairs={{0,16},{16,0},{1,17},{17,1},{2,18},{18,2},{3,19},{19,3},{4,20},{20... | collective-permute-start | bytes 1769480 | tf_op jit(solution)/shard_map/ppermute | solution.py:80
  188.5 30.3 %collective-permute-start.48 = (bf16[768,384]{1,0:T(8,128)(2,1)S(1)}, bf16[768,384]{1,0:T(8,128)(2,1)S(1)}, u32[]{:S(2)}, u32[]{:S(2)}) collective-permute-start(bf16[768,384]{1,0:T(8,128)(2,1)S(1)} %copy-done.105), channel_id=1, source_target_pairs={{0,16},{16,0},{1,17},{17,1},{2,18},{18,2},{3,19},{19,3},{4,20},{20... | collective-permute-start | bytes 1769480 | tf_op jit(solution)/shard_map/ppermute | solution.py:80
  218.8 44.4 %collective-permute-start.88 = (bf16[768,384]{1,0:T(8,128)(2,1)S(1)}, bf16[768,384]{1,0:T(8,128)(2,1)S(1)}, u32[]{:S(2)}, u32[]{:S(2)}) collective-permute-start(bf16[768,384]{1,0:T(8,128)(2,1)S(1)} %pad_maximum_fusion.3.refs_8_), channel_id=1, source_target_pairs={{0,16},{16,0},{1,17},{17,1},{2,18},{18,2},{3,19},{19,3},{4,20},{20... | collective-permute-start | bytes 1769480 | tf_op jit(solution)/shard_map/ppermute | solution.py:80
  246.7 57.7 %collective-permute-start.71 = (bf16[2,512,768]{2,1,0:T(8,128)(2,1)}, bf16[2,512,768]{2,1,0:T(8,128)(2,1)}, u32[]{:S(2)}, u32[]{:S(2)}) collective-permute-start(bf16[2,512,768]{2,1,0:T(8,128)(2,1)} %get-tuple-element.104.refs_0_), channel_id=1, source_target_pairs={{0,16},{16,0},{1,17},{17,1},{2,18},{18,2},{3,19},{19,3},{4,20},{20... | collective-permute-start | bytes 4718600 | tf_op jit(solution)/shard_map/ppermute | solution.py:80
  290.2 52.5 %all-to-all-start.3 = ((bf16[4,128,768]{2,1,0:T(8,128)(2,1)}), bf16[4,128,768]{2,1,0:T(8,128)(2,1)S(1)}, u32[]{:S(2)}, u32[]{:S(2)}) async-start(bf16[4,128,768]{2,1,0:T(8,128)(2,1)} %dynamic-slice_bitcast_fusion), calls=%async_computation.3 | async-start | bytes 1572864 | tf_op jit(solution)/shard_map/all_to_all | solution.py:787
  293.9 30.4 %collective-permute-start.79 = (bf16[192,1536]{1,0:T(8,128)(2,1)}, bf16[192,1536]{1,0:T(8,128)(2,1)S(1)}, u32[]{:S(2)}, u32[]{:S(2)}) collective-permute-start(bf16[192,1536]{1,0:T(8,128)(2,1)} %collective-permute-done.75.refs_1_), channel_id=1, source_target_pairs={{0,16},{16,0},{1,17},{17,1},{2,18},{18,2},{3,19},{19,3},{4,20},{20... | collective-permute-start | bytes 1769480 | tf_op jit(solution)/shard_map/ppermute | solution.py:80
  296.5 27.8 %collective-permute-start.89 = (bf16[768,384]{1,0:T(8,128)(2,1)S(1)}, bf16[768,384]{1,0:T(8,128)(2,1)S(1)}, u32[]{:S(2)}, u32[]{:S(2)}) collective-permute-start(bf16[768,384]{1,0:T(8,128)(2,1)S(1)} %copy-done.122), channel_id=1, source_target_pairs={{0,16},{16,0},{1,17},{17,1},{2,18},{18,2},{3,19},{19,3},{4,20},{20... | collective-permute-start | bytes 1769480 | tf_op jit(solution)/shard_map/ppermute | solution.py:80
  342.8 45.2 %all-to-all-start.1 = ((bf16[4,128,768]{2,1,0:T(8,128)(2,1)}), bf16[4,128,768]{2,1,0:T(8,128)(2,1)S(1)}, u32[]{:S(2)}, u32[]{:S(2)}) async-start(bf16[4,128,768]{2,1,0:T(8,128)(2,1)} %bitcast.20), calls=%async_computation.1 | async-start | bytes 1572864 | tf_op jit(solution)/shard_map/all_to_all | solution.py:793
  387.9 35.4 %collective-permute-start.93 = (bf16[2,512,768]{2,1,0:T(8,128)(2,1)}, bf16[2,512,768]{2,1,0:T(8,128)(2,1)}, u32[]{:S(2)}, u32[]{:S(2)}) collective-permute-start(bf16[2,512,768]{2,1,0:T(8,128)(2,1)} %get-tuple-element.116), channel_id=1, source_target_pairs={{0,16},{16,0},{1,17},{17,1},{2,18},{18,2},{3,19},{19,3},{4,20},{20... | collective-permute-start | bytes 4718600 | tf_op jit(solution)/shard_map/ppermute | solution.py:80
  388.0 34.3 %all-to-all-start.2 = ((bf16[4,128,768]{2,1,0:T(8,128)(2,1)}), bf16[4,128,768]{2,1,0:T(8,128)(2,1)S(1)}, u32[]{:S(2)}, u32[]{:S(2)}) async-start(bf16[4,128,768]{2,1,0:T(8,128)(2,1)} %bitcast.23), calls=%async_computation.2 | async-start | bytes 1572864 | tf_op jit(solution)/shard_map/all_to_all | solution.py:793
  411.7 104.0 %collective-permute-start.162 = (bf16[3072,384]{1,0:T(8,128)(2,1)}, bf16[3072,384]{1,0:T(8,128)(2,1)}, u32[]{:S(2)}, u32[]{:S(2)}) collective-permute-start(bf16[3072,384]{1,0:T(8,128)(2,1)} %weight_half.38), channel_id=1, source_target_pairs={{0,16},{16,0},{1,17},{17,1},{2,18},{18,2},{3,19},{19,3},{4,20},{20... | collective-permute-start | bytes 7077896 | tf_op jit(solution)/shard_map/ppermute | solution.py:80
  420.3 109.2 %collective-permute-start.147 = (bf16[768,1536]{1,0:T(8,128)(2,1)}, bf16[768,1536]{1,0:T(8,128)(2,1)}, u32[]{:S(2)}, u32[]{:S(2)}) collective-permute-start(bf16[768,1536]{1,0:T(8,128)(2,1)} %weight_half.34), channel_id=1, source_target_pairs={{0,16},{16,0},{1,17},{17,1},{2,18},{18,2},{3,19},{19,3},{4,20},{20... | collective-permute-start | bytes 7077896 | tf_op jit(solution)/shard_map/ppermute | solution.py:80
  420.4 119.1 %collective-permute-start.136 = (bf16[48,384]{1,0:T(8,128)(2,1)S(1)}, bf16[48,384]{1,0:T(8,128)(2,1)S(1)}, u32[]{:S(2)}, u32[]{:S(2)}) collective-permute-start(bf16[48,384]{1,0:T(8,128)(2,1)S(1)} %get-tuple-element.235), channel_id=1, source_target_pairs={{0,1},{1,0},{2,3},{3,2},{4,5},{5,4},{6,7},{7,6},{8,9},{9,8},{10,11... | collective-permute-start | bytes 110600 | tf_op jit(solution)/shard_map/ppermute | solution.py:88
  422.4 79.0 %collective-permute-start.92 = (bf16[4,128,768]{2,1,0:T(8,128)(2,1)S(1)}, bf16[4,128,768]{2,1,0:T(8,128)(2,1)}, u32[]{:S(2)}, u32[]{:S(2)}) collective-permute-start(bf16[4,128,768]{2,1,0:T(8,128)(2,1)S(1)} %broadcast_select_fusion.2), channel_id=1, source_target_pairs={{0,16},{16,0},{1,17},{17,1},{2,18},{18,2},{3,19},{19,3},{4,20},{20... | collective-permute-start | bytes 2359304 | tf_op jit(solution)/shard_map/ppermute | solution.py:80
  434.7 222.0 %all-to-all-start.5 = ((bf16[4,128,768]{2,1,0:T(8,128)(2,1)}), bf16[4,128,768]{2,1,0:T(8,128)(2,1)S(1)}, u32[]{:S(2)}, u32[]{:S(2)}) async-start(bf16[4,128,768]{2,1,0:T(8,128)(2,1)} %bitcast.90), calls=%async_computation.5 | async-start | bytes 1572864 | tf_op jit(solution)/shard_map/all_to_all | solution.py:793
  458.9 44.2 %collective-permute-start.125 = (bf16[768,384]{1,0:T(8,128)(2,1)}, bf16[768,384]{1,0:T(8,128)(2,1)S(1)}, u32[]{:S(2)}, u32[]{:S(2)}) collective-permute-start(bf16[768,384]{1,0:T(8,128)(2,1)} %weight_half.28), channel_id=1, source_target_pairs={{0,16},{16,0},{1,17},{17,1},{2,18},{18,2},{3,19},{19,3},{4,20},{20... | collective-permute-start | bytes 1769480 | tf_op jit(solution)/shard_map/ppermute | solution.py:80
  512.7 27.4 %collective-permute-start.138 = (bf16[48,384]{1,0:T(8,128)(2,1)S(1)}, bf16[48,384]{1,0:T(8,128)(2,1)S(1)}, u32[]{:S(2)}, u32[]{:S(2)}) collective-permute-start(bf16[48,384]{1,0:T(8,128)(2,1)S(1)} %get-tuple-element.236), channel_id=1, source_target_pairs={{0,3},{1,2},{2,1},{3,0},{4,7},{5,6},{6,5},{7,4},{8,11},{9,10},{10,... | collective-permute-start | bytes 110600 | tf_op jit(solution)/shard_map/ppermute | solution.py:88
  547.6 37.1 %collective-permute-start.94 = (bf16[2,512,768]{2,1,0:T(8,128)(2,1)}, bf16[2,512,768]{2,1,0:T(8,128)(2,1)S(1)}, u32[]{:S(2)}, u32[]{:S(2)}) collective-permute-start(bf16[2,512,768]{2,1,0:T(8,128)(2,1)} %get-tuple-element.125), channel_id=1, source_target_pairs={{0,16},{16,0},{1,17},{17,1},{2,18},{18,2},{3,19},{19,3},{4,20},{20... | collective-permute-start | bytes 4718600 | tf_op jit(solution)/shard_map/ppermute | solution.py:80
  568.9 94.5 %collective-permute-start.155 = (bf16[3072,384]{1,0:T(8,128)(2,1)}, bf16[3072,384]{1,0:T(8,128)(2,1)}, u32[]{:S(2)}, u32[]{:S(2)}) collective-permute-start(bf16[3072,384]{1,0:T(8,128)(2,1)} %weight_half.36), channel_id=1, source_target_pairs={{0,16},{16,0},{1,17},{17,1},{2,18},{18,2},{3,19},{19,3},{4,20},{20... | collective-permute-start | bytes 7077896 | tf_op jit(solution)/shard_map/ppermute | solution.py:80
  571.0 100.9 %collective-permute-start.140 = (bf16[768,1536]{1,0:T(8,128)(2,1)}, bf16[768,1536]{1,0:T(8,128)(2,1)}, u32[]{:S(2)}, u32[]{:S(2)}) collective-permute-start(bf16[768,1536]{1,0:T(8,128)(2,1)} %weight_half.32), channel_id=1, source_target_pairs={{0,16},{16,0},{1,17},{17,1},{2,18},{18,2},{3,19},{19,3},{4,20},{20... | collective-permute-start | bytes 7077896 | tf_op jit(solution)/shard_map/ppermute | solution.py:80
  574.5 29.5 %collective-permute-start.111 = (bf16[192,640]{1,0:T(8,128)(2,1)S(1)}, bf16[192,640]{1,0:T(8,128)(2,1)S(1)}, u32[]{:S(2)}, u32[]{:S(2)}) collective-permute-start(bf16[192,640]{1,0:T(8,128)(2,1)S(1)} %copy-done.129), channel_id=1, source_target_pairs={{0,4},{4,0},{8,12},{12,8},{1,5},{5,1},{9,13},{13,9},{2,6},{6,2},{1... | collective-permute-start | bytes 737288 | tf_op jit(solution)/shard_map/ppermute | solution.py:84
  644.5 33.9 %collective-permute-start.96 = (bf16[768,640]{1,0:T(8,128)(2,1)}, bf16[768,640]{1,0:T(8,128)(2,1)}, u32[]{:S(2)}, u32[]{:S(2)}) collective-permute-start(bf16[768,640]{1,0:T(8,128)(2,1)} %weight_half.20), channel_id=1, source_target_pairs={{0,16},{16,0},{1,17},{17,1},{2,18},{18,2},{3,19},{19,3},{4,20},{20... | collective-permute-start | bytes 2949128 | tf_op jit(solution)/shard_map/ppermute | solution.py:80
  655.8 28.5 %collective-permute-start.104 = (bf16[192,512]{1,0:T(8,128)(2,1)}, bf16[192,512]{1,0:T(8,128)(2,1)S(1)}, u32[]{:S(2)}, u32[]{:S(2)}) collective-permute-start(bf16[192,512]{1,0:T(8,128)(2,1)} %get-tuple-element.135), channel_id=1, source_target_pairs={{0,8},{4,12},{8,0},{12,4},{1,9},{5,13},{9,1},{13,5},{2,10},{6,14},... | collective-permute-start | bytes 589832 | tf_op jit(solution)/shard_map/ppermute | solution.py:84
  656.8 35.9 %all-to-all-start.4 = ((bf16[4,128,768]{2,1,0:T(8,128)(2,1)}), bf16[4,128,768]{2,1,0:T(8,128)(2,1)S(1)}, u32[]{:S(2)}, u32[]{:S(2)}) async-start(bf16[4,128,768]{2,1,0:T(8,128)(2,1)} %bitcast.31), calls=%async_computation.4 | async-start | bytes 1572864 | tf_op jit(solution)/shard_map/all_to_all | solution.py:793
  693.6 53.8 %collective-permute-start.166 = (bf16[192,384]{1,0:T(8,128)(2,1)S(1)}, bf16[192,384]{1,0:T(8,128)(2,1)S(1)}, u32[]{:S(2)}, u32[]{:S(2)}) collective-permute-start(bf16[192,384]{1,0:T(8,128)(2,1)S(1)} %copy-done.86), channel_id=1, source_target_pairs={{0,1},{1,0},{2,3},{3,2},{4,5},{5,4},{6,7},{7,6},{8,9},{9,8},{10,11... | collective-permute-start | bytes 442376 | tf_op jit(solution)/shard_map/ppermute | solution.py:88
  715.1 27.0 %collective-permute-start.158 = (bf16[768,384]{1,0:T(8,128)(2,1)S(1)}, bf16[768,384]{1,0:T(8,128)(2,1)S(1)}, u32[]{:S(2)}, u32[]{:S(2)}) collective-permute-start(bf16[768,384]{1,0:T(8,128)(2,1)S(1)} %add_convert_fusion.4), channel_id=1, source_target_pairs={{0,4},{4,0},{8,12},{12,8},{1,5},{5,1},{9,13},{13,9},{2,6},{6,2},{1... | collective-permute-start | bytes 1769480 | tf_op jit(solution)/shard_map/ppermute | solution.py:84
  753.8 28.4 %collective-permute-start.152 = (bf16[48,1536]{1,0:T(8,128)(2,1)S(1)}, bf16[48,1536]{1,0:T(8,128)(2,1)S(1)}, u32[]{:S(2)}, u32[]{:S(2)}) collective-permute-start(bf16[48,1536]{1,0:T(8,128)(2,1)S(1)} %copy-done.81), channel_id=1, source_target_pairs={{0,2},{1,3},{2,0},{3,1},{4,6},{5,7},{6,4},{7,5},{8,10},{9,11},{10,... | collective-permute-start | bytes 442376 | tf_op jit(solution)/shard_map/ppermute | solution.py:88
  754.8 27.4 %collective-permute-start.144 = (bf16[48,1536]{1,0:T(8,128)(2,1)S(1)}, bf16[48,1536]{1,0:T(8,128)(2,1)S(1)}, u32[]{:S(2)}, u32[]{:S(2)}) collective-permute-start(bf16[48,1536]{1,0:T(8,128)(2,1)S(1)} %get-tuple-element.206), channel_id=1, source_target_pairs={{0,1},{1,0},{2,3},{3,2},{4,5},{5,4},{6,7},{7,6},{8,9},{9,8},{10,11... | collective-permute-start | bytes 442376 | tf_op jit(solution)/shard_map/ppermute | solution.py:88
  (283 other events, 3941.5 us)

commit v2 on v1

v2 whole, which is shorter than its diff:
```python
import functools

import jax
import jax.numpy as jnp
from jax import lax
from jax.experimental import pallas as pl
from jax.experimental.pallas import tpu as pltpu
from jax.sharding import PartitionSpec as P

HD = 64
PAIR = 2 * HD
BF16 = jnp.bfloat16
F32 = jnp.float32
MASKED = -1e30
COST_SHARE = 0.1
GAIN_LANES = 128


def nn(left, right):
    return lax.dot_general(left, right, (((1,), (0,)), ((), ())), preferred_element_type=F32)


def nt(left, right):
    return lax.dot_general(left, right, (((1,), (1,)), ((), ())), preferred_element_type=F32)


def tn(left, right):
    return lax.dot_general(left, right, (((0,), (0,)), ((), ())), preferred_element_type=F32)


def normalise(rows):
    centred = rows - jnp.mean(rows, axis=-1, keepdims=True)
    scale = lax.rsqrt(jnp.mean(centred * centred, axis=-1, keepdims=True) + 1e-05)
    return centred * scale, scale


def norm_back(rows, gain, grad):
    normed, scale = normalise(rows)
    inner = grad * gain
    mean_inner = jnp.mean(inner, axis=-1, keepdims=True)
    mean_along = jnp.mean(inner * normed, axis=-1, keepdims=True)
    grad_rows = scale * (inner - mean_inner - normed * mean_along)
    return grad_rows, jnp.sum(grad * normed, axis=0, keepdims=True)


def swap_halves(pair_block):
    lane = lax.broadcasted_iota(jnp.int32, pair_block.shape, 1)
    ahead = pltpu.roll(pair_block, PAIR - HD // 2, 1)
    behind = pltpu.roll(pair_block, HD // 2, 1)
    return jnp.where(lane % HD < HD // 2, ahead, behind)


class Plan:
    def __init__(self, tokens, w_in):
        micro, seqs, span, width = tokens.shape
        self.width = width
        self.hidden = w_in.shape[-1]
        self.heads = width // HD
        self.pairs = width // PAIR
        self.n_ctx = lax.axis_size("ctx")
        self.n_dp = lax.axis_size("dp")
        self.micro, self.seqs, self.span = micro, seqs, span
        self.n_seq = micro * seqs
        self.parts = self.n_ctx // self.n_seq
        assert self.parts * self.n_seq == self.n_ctx
        self.half = span // 2
        self.sub = self.half // self.parts
        self.rows = self.n_ctx * self.sub
        self.section = lax.axis_index("section")
        self.dp = lax.axis_index("dp")
        self.ctx = lax.axis_index("ctx")
        self.staged = w_in.shape[1] % 16 == 0 and self.n_ctx == 4 and self.n_dp == 4
        self.blocks = self.n_dp if self.staged else 1
        self.shards = self.n_dp * self.n_ctx if self.staged else 1
        self.shard_rows = width // self.shards
        self.meta = jnp.stack([self.section, self.dp]).astype(jnp.int32)


X_BIT, Y_BIT = 1, 2


def other_core(value):
    return lax.ppermute(value, "section", [(0, 1), (1, 0)])


def xor_dp(plan, value, mask):
    return lax.ppermute(value, "dp", [(i, i ^ mask) for i in range(plan.n_dp)])


def xor_ctx(plan, value, mask):
    return lax.ppermute(value, "ctx", [(i, i ^ mask) for i in range(plan.n_ctx)])


def exchange_ctx(value, dim=0):
    return lax.all_to_all(value, "ctx", dim, dim, tiled=True)


def spread_ctx(plan, shard):
    return exchange_ctx(jnp.concatenate([shard] * plan.n_ctx, axis=0))


def after(value, *earlier):
    earlier = [item for item in earlier if item is not None]
    if not earlier:
        return value
    return lax.optimization_barrier((value, *earlier))[0]


class Spread:
    def __init__(self, own, relative):
        self.own, self.relative = own, relative

    def share(self, *earlier):
        self.other = other_core(after(self.own, *earlier))

    def refs(self):
        return [self.own, self.other]


def to_lanes_of_halves(tall):
    half = tall.shape[1] // 2
    return jnp.concatenate([to_lanes(tall[:, :half]), to_lanes(tall[:, half:])], axis=1)


def to_lanes(tall):
    rows = tall.shape[0] // 4
    return jnp.concatenate([tall[i * rows : (i + 1) * rows] for i in range(4)], axis=1)


def from_lanes(wide):
    cols = wide.shape[1] // 4
    return jnp.concatenate([wide[:, i * cols : (i + 1) * cols] for i in range(4)], axis=0)


def gather_natural(plan, shard, tall=0):
    gathered = lax.all_gather(shard, ("dp", "ctx"), axis=0, tiled=True)
    if plan.staged:
        return Spread(gathered.reshape(plan.shards, plan.shard_rows, -1), False)
    if tall:
        cut = gathered.shape[1] - tall
        n = plan.n_dp * plan.n_ctx
        quarters = gathered[:, cut:].reshape(n, plan.width // n, 4, tall // 4).transpose(0, 2, 1, 3)
        gathered = jnp.concatenate([gathered[:, :cut], to_lanes(quarters.reshape(-1, tall // 4))], axis=1)
    return Spread(gathered[None], False)


class SpreadDp:
    def __init__(self, plan, block, *earlier):
        self.plan = plan
        self.block = after(block, *earlier)
        self.got = [xor_dp(plan, self.block, mask) for mask in (X_BIT, Y_BIT, X_BIT | Y_BIT)]

    def result(self, *earlier):
        plan = self.plan
        blocks = jnp.stack([after(self.block, *earlier), *self.got])
        return Spread(blocks.reshape(plan.shards, plan.shard_rows, -1), True)


class Collect:
    def __init__(self, plan, blocks):
        self.plan = plan
        self.blocks = [blocks[0]] + [xor_dp(plan, blocks[mask], mask) for mask in range(1, plan.n_dp)]

    def first(self, order):
        order.need(*self.blocks[1:])

    def second(self, order):
        plan = self.plan
        own = order.gate(self.blocks[0])
        block = sum(value.astype(F32) for value in [own, *self.blocks[1:]]).astype(BF16)
        order.mark(block)
        self.parts = exchange_ctx(block.reshape(plan.n_ctx, plan.shard_rows, -1))

    def last(self, order):
        order.need(self.parts)

    def result(self):
        return jnp.sum(self.parts.astype(F32), axis=0).astype(BF16)


def smem():
    return pl.BlockSpec(memory_space=pltpu.SMEM)


def anywhere():
    return pl.BlockSpec(memory_space=pl.ANY)


def whole(shape):
    return pl.BlockSpec(shape, lambda i: (0,) * len(shape))


def rows_of(step, width):
    return pl.BlockSpec((step, width), lambda i: (i, 0))


def params(megabytes):
    return pltpu.CompilerParams(vmem_limit_bytes=megabytes * 1024 * 1024)


def cost(flops, bytes_accessed, transcendentals=0):
    return pl.CostEstimate(
        flops=int(flops * COST_SHARE),
        bytes_accessed=int(bytes_accessed * COST_SHARE),
        transcendentals=int(transcendentals * COST_SHARE),
    )


def block_copies(meta, ref, relative, place, lanes, sems, first):
    blocks = 4 if relative else 1
    count = ref.shape[0] // blocks
    copies = []
    for mask in range(blocks):
        start = (meta[1] ^ mask) * count if relative else 0
        copies.append(
            pltpu.make_async_copy(
                ref.at[pl.ds(mask * count, count), :, lanes],
                place(pl.ds(start, count)),
                sems.at[first + mask],
            )
        )
    return copies


def run(copies):
    for copy in copies:
        copy.start()


def wait(copies):
    for copy in copies:
        copy.wait()


class Loads:
    def __init__(self, section, own, other, carrier=None):
        self.section, self.own, self.other, self.carrier = section, own, other, carrier

    def each(self, act):
        if self.carrier is None:
            act(self.own)
            act(self.other)
            return
        pl.when(self.section == self.carrier)(lambda: act(self.own))
        pl.when(self.section != self.carrier)(lambda: act(self.other))

    def start(self):
        self.each(run)

    def wait(self):
        self.each(wait)


def split_refs(refs, counts):
    out, at = [], 0
    for count in counts:
        out.append(refs[at : at + count])
        at += count
    return out


def side(which, half):
    return pl.ds(pl.multiple_of(which * half, 128), half)


def load_halves(meta, relative, refs, matrix, start, sems, first):
    half = matrix.shape[-1] // 2
    lanes = slice(start, start + half)

    def at(which):
        return lambda shards: matrix.at[shards, :, side(which, half)]

    own = block_copies(meta, refs[0], relative, at(meta[0]), lanes, sems, first)
    other = block_copies(meta, refs[1], relative, at(1 - meta[0]), lanes, sems, first + 4)
    return Loads(meta[0], own, other)


def load_tall(meta, relative, refs, matrix, start, sems, first):
    half = matrix.shape[-1] // 2
    own, other = [], []
    for quarter in range(4):
        lanes = slice(start + quarter * half, start + (quarter + 1) * half)

        def at(which, quarter=quarter):
            return lambda shards: matrix.at[shards, quarter, :, side(which, half)]

        where = first + 8 * quarter
        own += block_copies(meta, refs[0], relative, at(meta[0]), lanes, sems, where)
        other += block_copies(meta, refs[1], relative, at(1 - meta[0]), lanes, sems, where + 4)
    return Loads(meta[0], own, other)


def load_one(meta, relative, refs, matrix, start, sems, first, carrier):
    lanes = slice(start, start + matrix.shape[-1])

    def at(shards):
        return matrix.at[shards]

    own = block_copies(meta, refs[0], relative, at, lanes, sems, first)
    other = block_copies(meta, refs[1], relative, at, lanes, sems, first)
    return Loads(meta[0], own, other, carrier)


def flat(matrix):
    return matrix.reshape(-1, matrix.shape[-1])


def row_step(rows, step=128):
    return step if rows % step == 0 else rows


def qkv_kernel(relative, meta, x_ref, cos_ref, sin_ref, *refs):
    attn_refs, rest = split_refs(refs, (2, len(refs) - 2))
    a_ref, q_ref, kv_ref, gains_ref, wqk, wv, columns, sems = rest
    width = wv.shape[-1]
    qk = load_halves(meta, relative, attn_refs, wqk, 0, sems, 0)
    v = load_one(meta, relative, attn_refs, wv, width, sems, 8, 0)
    gain = load_one(meta, relative, attn_refs, columns, 2 * width, sems, 12, 0)
    first = pl.program_id(0) == 0

    @pl.when(first)
    def _():
        gain.start()
        qk.start()
        v.start()
        gain.wait()
        gains_ref[...] = jnp.transpose(flat(columns[...]).astype(F32))[:8]

    normed, _ = normalise(x_ref[...].astype(F32))
    a = (normed * gains_ref[0:1, :]).astype(BF16)
    a_ref[...] = jnp.transpose(a)

    @pl.when(first)
    def _():
        qk.wait()
        v.wait()

    cos, sin = cos_ref[...], sin_ref[...]
    for which in range(2):
        out = nn(a, flat(wqk[:, :, which * width : (which + 1) * width]))
        for pair in range(width // PAIR):
            lanes = slice(pair * PAIR, (pair + 1) * PAIR)
            block = out[:, lanes]
            turned = block * cos + swap_halves(block) * sin
            if which == 0:
                q_ref[:, lanes] = (turned * HD**-0.5).astype(BF16)
            else:
                kv_ref[0, :, lanes] = turned.astype(BF16)
    kv_ref[1] = nn(a, flat(wv[...])).astype(BF16)


def qkv_forward(plan, x, cos, sin, attn):
    rows, width = x.shape
    step = row_step(rows)
    return pl.pallas_call(
        functools.partial(qkv_kernel, attn.relative),
        out_shape=[
            jax.ShapeDtypeStruct((width, rows), BF16),
            jax.ShapeDtypeStruct((rows, width), BF16),
            jax.ShapeDtypeStruct((2, rows, width), BF16),
            jax.ShapeDtypeStruct((8, width), F32),
        ],
        grid=(rows // step,),
        in_specs=[smem(), rows_of(step, width), rows_of(step, PAIR), rows_of(step, PAIR)]
        + [anywhere()] * 2,
        out_specs=[
            pl.BlockSpec((width, step), lambda i: (0, i)),
            rows_of(step, width),
            pl.BlockSpec((2, step, width), lambda i: (0, i, 0)),
            whole((8, width)),
        ],
        scratch_shapes=[
            pltpu.VMEM((plan.shards, plan.shard_rows, 2 * width), BF16),
            pltpu.VMEM((plan.shards, plan.shard_rows, width), BF16),
            pltpu.VMEM((plan.shards, plan.shard_rows, GAIN_LANES), BF16),
            pltpu.SemaphoreType.DMA((16,)),
        ],
        compiler_params=params(56),
        cost_estimate=cost(6 * rows * width * width, 12 * rows * width + 6 * width * width),
        name="qkv_forward",
    )(plan.meta, x, cos, sin, *attn.refs())


def lane_mask(shape, head):
    lane = lax.broadcasted_iota(jnp.int32, shape, 1)
    return lane < HD if head == 0 else lane >= HD


def with_ones(query):
    lane = lax.broadcasted_iota(jnp.int32, query.shape, 1)
    return jnp.concatenate([query, jnp.where(lane == 0, 1.0, 0.0).astype(BF16)], axis=1)


def attention_kernel(chunks, key_block, q_ref, *refs):
    kv = refs[:chunks]
    bias_ref, o_ref, ot_ref, lse_ref, s_scr, vt_scr = refs[chunks:]
    rows = q_ref.shape[0]
    per_chunk = rows // key_block
    query = q_ref[...]
    for c in range(chunks):
        vt_scr[:, c * rows : (c + 1) * rows] = jnp.transpose(kv[c][1])
    outs = []
    for head in range(2):
        extended = with_ones(jnp.where(lane_mask(query.shape, head), query, jnp.zeros_like(query)))
        peak = jnp.full((1, rows), -jnp.inf, F32)
        for c in range(chunks):
            for j in range(per_chunk):
                at = slice(j * key_block, (j + 1) * key_block)
                everywhere = slice(c * rows + at.start, c * rows + at.stop)
                keys = jnp.concatenate([kv[c][0, at, :], bias_ref[everywhere, :]], axis=1)
                scores = nt(keys, extended)
                s_scr[everywhere, :] = scores
                peak = jnp.maximum(peak, jnp.max(scores, axis=0, keepdims=True))
        total = jnp.zeros((1, rows), F32)
        out = jnp.zeros((PAIR, rows), F32)
        for c in range(chunks):
            for j in range(per_chunk):
                everywhere = slice(c * rows + j * key_block, c * rows + (j + 1) * key_block)
                weights = jnp.exp(s_scr[everywhere, :] - peak)
                total = total + jnp.sum(weights, axis=0, keepdims=True)
                out = out + nn(vt_scr[:, everywhere], weights.astype(BF16))
        lse_ref[0, head : head + 1, :] = peak + jnp.log(total)
        outs.append(out / total)
    row = lax.broadcasted_iota(jnp.int32, outs[0].shape, 0)
    out = jnp.where(row < HD, outs[0], outs[1])
    o_ref[...] = jnp.transpose(out).astype(BF16)
    ot_ref[...] = out.astype(BF16)


def attention_forward(plan, query, kv, bias):
    rows, width = query.shape
    chunks = len(kv)
    keys = chunks * rows
    pair_block = pl.BlockSpec((rows, PAIR), lambda p: (0, p))
    kv_block = pl.BlockSpec((2, rows, PAIR), lambda p: (0, 0, p))
    return pl.pallas_call(
        functools.partial(attention_kernel, chunks, min(256, rows)),
        out_shape=[
            jax.ShapeDtypeStruct((rows, width), BF16),
            jax.ShapeDtypeStruct((width, rows), BF16),
            jax.ShapeDtypeStruct((plan.pairs, 8, rows), F32),
        ],
        grid=(plan.pairs,),
        in_specs=[pair_block] + [kv_block] * chunks + [pl.BlockSpec((keys, PAIR), lambda p: (0, 0))],
        out_specs=[
            pair_block,
            pl.BlockSpec((PAIR, rows), lambda p: (p, 0)),
            pl.BlockSpec((1, 8, rows), lambda p: (p, 0, 0)),
        ],
        scratch_shapes=[pltpu.VMEM((keys, rows), F32), pltpu.VMEM((PAIR, keys), BF16)],
        compiler_params=params(56),
        cost_estimate=cost(
            16 * rows * keys * width, 4 * rows * width + 4 * keys * width, rows * keys * plan.heads
        ),
        name="attention_forward",
    )(query, *kv, bias)


def layer_loads(meta, relative, attn_refs, ffn_refs, wo, w1, w2, sems):
    half = w1.shape[-1] // 2
    out = load_one(meta, relative[0], attn_refs, wo, wo.shape[-1], sems, 0, 1)
    first = load_halves(meta, relative[1], ffn_refs, w1, 0, sems, 4)
    second = load_tall(meta, relative[1], ffn_refs, w2, half, sems, 12)
    return out, first, second


def layer_scratch(plan):
    width, hidden, n, rows = plan.width, plan.hidden, plan.shards, plan.shard_rows
    return [
        pltpu.VMEM((n, rows, width), BF16),
        pltpu.VMEM((n, rows, hidden), BF16),
        pltpu.VMEM((n, 4, rows, width), BF16),
        pltpu.SemaphoreType.DMA((44,)),
    ]


def tall_chunk(w2, i):
    n = w2.shape[0]
    value = w2[pl.ds(i * (n // 4), n // 4)] if n >= 4 else w2[0, i]
    return flat(value)


def ffn_kernel(relative, meta, o_ref, x_ref, gains_ref, *refs):
    attn_refs, ffn_refs, rest = split_refs(refs, (2, 2, len(refs) - 4))
    u2_ref, bt_ref, acts_ref, low_ref, ht_ref, slope_ref, wo, w1, w2, sems, b_ref = rest
    out, first, second = layer_loads(meta, relative, attn_refs, ffn_refs, wo, w1, w2, sems)
    chunk = slope_ref.shape[1]
    i = pl.program_id(0)

    @pl.when(i == 0)
    def _():
        out.start()
        first.start()
        second.start()
        out.wait()
        u2 = x_ref[...].astype(F32) + nn(o_ref[...], flat(wo[...]))
        u2_ref[...] = u2
        acts_ref[...] = u2
        b = (normalise(u2)[0] * gains_ref[1:2, :]).astype(BF16)
        b_ref[...] = b
        bt_ref[...] = jnp.transpose(b)
        first.wait()
        second.wait()

    at = pl.ds(pl.multiple_of(i * chunk, chunk), chunk)
    hp = nn(b_ref[...], flat(w1[:, :, at]))
    cdf = 0.5 * (1.0 + lax.erf(hp * (0.5**0.5)))
    density = jnp.exp(-0.5 * hp * hp) * 0.3989422804014327
    h = (hp * cdf).astype(BF16)
    ht_ref[...] = jnp.transpose(h)
    slope_ref[...] = (cdf + hp * density).astype(BF16)
    acts_ref[...] += nn(h, tall_chunk(w2, i))

    @pl.when(i == pl.num_programs(0) - 1)
    def _():
        low_ref[...] = acts_ref[...].astype(BF16)


def ffn_forward(plan, o, x, gains, attn, ffn):
    rows, width = x.shape
    hidden = plan.hidden
    chunk = hidden // 4
    refs = [*attn.refs(), *ffn.refs()]
    relative = (attn.relative, ffn.relative)
    columns = pl.BlockSpec((rows, chunk), lambda i: (0, i))
    return pl.pallas_call(
        functools.partial(ffn_kernel, relative),
        out_shape=[
            jax.ShapeDtypeStruct((rows, width), F32),
            jax.ShapeDtypeStruct((width, rows), BF16),
            jax.ShapeDtypeStruct((rows, width), F32),
            jax.ShapeDtypeStruct((rows, width), BF16),
            jax.ShapeDtypeStruct((hidden, rows), BF16),
            jax.ShapeDtypeStruct((rows, hidden), BF16),
        ],
        grid=(hidden // chunk,),
        in_specs=[smem(), whole((rows, width)), whole((rows, width)), whole((8, width))]
        + [anywhere()] * len(refs),
        out_specs=[whole((rows, width)), whole((width, rows)), whole((rows, width)), whole((rows, width))]
        + [rows_of(chunk, rows), columns],
        scratch_shapes=[
            *layer_scratch(plan),
            pltpu.VMEM((rows, width), BF16),
        ],
        compiler_params=params(56),
        cost_estimate=cost(
            4 * rows * width * hidden + 2 * rows * width * width + 60 * rows * hidden,
            20 * rows * width + 4 * rows * hidden + 4 * width * hidden,
            2 * rows * hidden,
        ),
        name="ffn_forward",
    )(plan.meta, o, x, gains, *refs)


def ffn_back_kernel(relative, meta, c_ref, slope_ref, u2_ref, gains_ref, *refs):
    attn_refs, ffn_refs, rest = split_refs(refs, (2, 2, len(refs) - 4))
    cf_ref, dhp_ref, du2_ref, dz_ref, do_ref, dg_ref, wo, w1, w2, sems, acc = rest
    out, first, second = layer_loads(meta, relative, attn_refs, ffn_refs, wo, w1, w2, sems)
    chunk = dhp_ref.shape[1]
    i = pl.program_id(0)

    @pl.when(i == 0)
    def _():
        second.start()
        first.start()
        out.start()
        cf_ref[...] = c_ref[...].astype(BF16)
        acc[...] = jnp.zeros_like(acc)
        second.wait()
        first.wait()
        out.wait()

    at = pl.ds(pl.multiple_of(i * chunk, chunk), chunk)
    dh = nt(cf_ref[...], tall_chunk(w2, i))
    dhp = (dh * slope_ref[...].astype(F32)).astype(BF16)
    dhp_ref[...] = dhp
    acc[...] += nt(dhp, flat(w1[:, :, at]))

    @pl.when(i == pl.num_programs(0) - 1)
    def _():
        grad, dgain = norm_back(u2_ref[...], gains_ref[1:2, :], acc[...])
        du2 = c_ref[...].astype(F32) + grad
        du2_ref[...] = du2
        dg_ref[...] = dgain
        dz = du2.astype(BF16)
        dz_ref[...] = dz
        do_ref[...] = nt(dz, flat(wo[...])).astype(BF16)


def ffn_backward(plan, c, slope, u2, gains, attn, ffn):
    rows, width = u2.shape
    hidden = plan.hidden
    chunk = hidden // 4
    refs = [*attn.refs(), *ffn.refs()]
    relative = (attn.relative, ffn.relative)
    columns = pl.BlockSpec((rows, chunk), lambda i: (0, i))
    wide = jax.ShapeDtypeStruct((rows, width), BF16)
    full = whole((rows, width))
    return pl.pallas_call(
        functools.partial(ffn_back_kernel, relative),
        out_shape=[
            wide,
            jax.ShapeDtypeStruct((rows, hidden), BF16),
            jax.ShapeDtypeStruct((rows, width), F32),
            wide,
            wide,
            jax.ShapeDtypeStruct((1, width), F32),
        ],
        grid=(hidden // chunk,),
        in_specs=[smem(), full, columns, full, whole((8, width))] + [anywhere()] * len(refs),
        out_specs=[full, columns, full, full, full, whole((1, width))],
        scratch_shapes=[
            *layer_scratch(plan),
            pltpu.VMEM((rows, width), F32),
        ],
        compiler_params=params(56),
        cost_estimate=cost(
            4 * rows * width * hidden + 2 * rows * width * width,
            18 * rows * width + 4 * rows * hidden + 4 * width * hidden + 2 * width * width,
        ),
        name="ffn_backward",
    )(plan.meta, c, slope, u2, gains, *refs)


def attention_back_kernel(chunks, key_block, q_ref, do_ref, o_ref, lse_ref, bias_ref, *refs):
    kv = refs[:chunks]
    dq_ref, dk_ref, dv_ref = refs[chunks : chunks + 3]
    far = refs[chunks + 3 : 2 * chunks + 2]
    kt_scr, dk_scr, dv_scr = refs[2 * chunks + 2 :]
    rows = q_ref.shape[0]
    per_chunk = rows // key_block
    query, grad = q_ref[...], do_ref[...]
    for c in range(chunks):
        kt_scr[:, c * rows : (c + 1) * rows] = jnp.transpose(kv[c][0])
    products = jnp.transpose(grad.astype(F32) * o_ref[...].astype(F32))
    outs = []
    for head in range(2):
        mask = lane_mask(query.shape, head)
        masked_query = jnp.where(mask, query, jnp.zeros_like(query))
        masked_grad = jnp.where(mask, grad, jnp.zeros_like(grad))
        extended = with_ones(masked_query)
        delta = jnp.sum(products[head * HD : (head + 1) * HD], axis=0, keepdims=True)
        lse = lse_ref[0, head : head + 1, :]
        dqt = jnp.zeros((PAIR, rows), F32)
        for c in range(chunks):
            for j in range(per_chunk):
                at = slice(j * key_block, (j + 1) * key_block)
                everywhere = slice(c * rows + at.start, c * rows + at.stop)
                keys = jnp.concatenate([kv[c][0, at, :], bias_ref[everywhere, :]], axis=1)
                weights = jnp.exp(nt(keys, extended) - lse)
                grad_weights = nt(kv[c][1, at, :], masked_grad)
                grad_scores = (weights * (grad_weights - delta)).astype(BF16)
                dv = nn(weights.astype(BF16), masked_grad)
                dk = nn(grad_scores, masked_query)
                dqt = dqt + nn(kt_scr[:, everywhere], grad_scores)
                if head == 0:
                    dv_scr[everywhere, :] = dv
                    dk_scr[everywhere, :] = dk
                elif c == 0:
                    dk_ref[at, :] = dk_scr[everywhere, :] + dk
                    dv_ref[at, :] = dv_scr[everywhere, :] + dv
                else:
                    far[c - 1][0, at, :] = (dk_scr[everywhere, :] + dk).astype(BF16)
                    far[c - 1][1, at, :] = (dv_scr[everywhere, :] + dv).astype(BF16)
        outs.append(dqt)
    row = lax.broadcasted_iota(jnp.int32, outs[0].shape, 0)
    dq_ref[...] = jnp.transpose(jnp.where(row < HD, outs[0], outs[1])).astype(BF16)


def attention_backward(plan, query, grad, o, lse, bias, kv):
    rows, width = query.shape
    chunks = len(kv)
    keys = chunks * rows
    pair_block = pl.BlockSpec((rows, PAIR), lambda p: (0, p))
    kv_block = pl.BlockSpec((2, rows, PAIR), lambda p: (0, 0, p))
    near = jax.ShapeDtypeStruct((rows, width), F32)
    return pl.pallas_call(
        functools.partial(attention_back_kernel, chunks, min(256, rows)),
        out_shape=[jax.ShapeDtypeStruct((rows, width), BF16), near, near]
        + [jax.ShapeDtypeStruct((2, rows, width), BF16)] * (chunks - 1),
        grid=(plan.pairs,),
        in_specs=[pair_block] * 3
        + [
            pl.BlockSpec((1, 8, rows), lambda p: (p, 0, 0)),
            pl.BlockSpec((keys, PAIR), lambda p: (0, 0)),
        ]
        + [kv_block] * chunks,
        out_specs=[pair_block] * 3 + [kv_block] * (chunks - 1),
        scratch_shapes=[
            pltpu.VMEM((PAIR, keys), BF16),
            pltpu.VMEM((keys, PAIR), F32),
            pltpu.VMEM((keys, PAIR), F32),
        ],
        compiler_params=params(56),
        cost_estimate=cost(
            40 * rows * keys * width,
            16 * rows * width + 8 * keys * width,
            rows * keys * plan.heads,
        ),
        name="attention_backward",
    )(query, grad, o, lse, bias, *kv)


def qkv_back_kernel(
    spread, n_far, meta, dq_ref, dk_ref, dv_ref, du2_ref, x_ref, gains_ref, cos_ref, sin_ref, *refs
):
    far, attn_refs, rest = split_refs(refs, (n_far, len(refs) - n_far - 7, 7))
    dqkv_ref, dx_ref, low_ref, dg_ref, wqk, wv, sems = rest
    qk = load_halves(meta, spread, attn_refs, wqk, 0, sems, 0)
    v = load_one(meta, spread, attn_refs, wv, wv.shape[-1], sems, 8, 0)
    first = pl.program_id(0) == 0

    @pl.when(first)
    def _():
        qk.start()
        v.start()
        dg_ref[...] = jnp.zeros_like(dg_ref)

    width = x_ref.shape[1]
    cos, sin = cos_ref[...], sin_ref[...]
    for pair in range(width // PAIR):
        lanes = slice(pair * PAIR, (pair + 1) * PAIR)
        dq = dq_ref[:, lanes].astype(F32) * HD**-0.5
        dk, dv = dk_ref[:, lanes], dv_ref[:, lanes]
        for part in far:
            dk = dk + part[0, :, lanes].astype(F32)
            dv = dv + part[1, :, lanes].astype(F32)
        dk = dk.astype(BF16).astype(F32)
        dqkv_ref[:, pair * PAIR : (pair + 1) * PAIR] = (dq * cos - swap_halves(dq) * sin).astype(BF16)
        at = width + pair * PAIR
        dqkv_ref[:, at : at + PAIR] = (dk * cos - swap_halves(dk) * sin).astype(BF16)
        at = 2 * width + pair * PAIR
        dqkv_ref[:, at : at + PAIR] = dv.astype(BF16)

    @pl.when(first)
    def _():
        qk.wait()
        v.wait()

    da = nt(dqkv_ref[:, : 2 * width], flat(wqk[...]))
    da = da + nt(dqkv_ref[:, 2 * width :], flat(wv[...]))
    grad, dgain = norm_back(x_ref[...].astype(F32), gains_ref[0:1, :], da)
    dx = du2_ref[...] + grad
    dx_ref[...] = dx
    low_ref[...] = dx.astype(BF16)
    dg_ref[...] += dgain


def qkv_backward(plan, dq, dk, dv, far, du2, x, gains, cos, sin, attn):
    rows, width = x.shape
    step = row_step(rows)
    refs = attn.refs()
    some = rows_of(step, width)
    return pl.pallas_call(
        functools.partial(qkv_back_kernel, attn.relative, len(far)),
        out_shape=[
            jax.ShapeDtypeStruct((rows, 3 * width), BF16),
            jax.ShapeDtypeStruct((rows, width), F32),
            jax.ShapeDtypeStruct((rows, width), BF16),
            jax.ShapeDtypeStruct((1, width), F32),
        ],
        grid=(rows // step,),
        in_specs=[smem()]
        + [some] * 5
        + [whole((8, width)), rows_of(step, PAIR), rows_of(step, PAIR)]
        + [pl.BlockSpec((2, step, width), lambda i: (0, i, 0))] * len(far)
        + [anywhere()] * len(refs),
        out_specs=[rows_of(step, 3 * width), some, some, whole((1, width))],
        scratch_shapes=[
            pltpu.VMEM((plan.shards, plan.shard_rows, 2 * width), BF16),
            pltpu.VMEM((plan.shards, plan.shard_rows, width), BF16),
            pltpu.SemaphoreType.DMA((12,)),
        ],
        compiler_params=params(56),
        cost_estimate=cost(6 * rows * width * width, 30 * rows * width + 6 * width * width),
        name="qkv_backward",
    )(plan.meta, dq, dk, dv, du2, x, gains, cos, sin, *far, *refs)


class Job:
    def __init__(self, left, right, start, cols, tall=False):
        self.left, self.right, self.start, self.cols, self.tall = left, right, start, cols, tall
        self.lanes = 4 * cols if tall else cols
        self.given = right is None


def weight_kernel(jobs, n_lefts, n_rights, mine, relative, meta, *refs):
    n_got = 1 if mine else 0
    lefts, rights, got, outs, (acc,) = split_refs(
        refs, (n_lefts, n_rights, n_got, len(refs) - n_lefts - n_rights - n_got - 1, 1)
    )
    step = pl.program_id(0)
    which = meta[0] if mine else 1 - meta[0]
    block = (meta[1] ^ step) if relative else step

    shards, size = acc.shape[:2]
    lane = 0
    for job in jobs:
        left = lefts[job.left]
        if job.given:
            count = shards * size
            rows = left[pl.ds(pl.multiple_of(block * count, 16), count), :]
            acc[:, :, lane : lane + job.cols] = rows.reshape(shards, size, job.cols)
            lane += job.cols
            continue
        right = rights[job.right]
        half = right.shape[1] // 2
        columns = right[:, side(which, half)] if job.cols == half else right[
            :, pl.ds(pl.multiple_of(which * half + job.start, 128), job.cols)
        ]
        count = shards * size * (4 if job.tall else 1)
        product = nn(left[pl.ds(pl.multiple_of(block * count, 16), count), :], columns)
        if job.tall:
            product = product.reshape(shards, 4, size, job.cols)
            for quarter in range(4):
                acc[:, :, lane : lane + job.cols] = product[:, quarter]
                lane += job.cols
        else:
            acc[:, :, lane : lane + job.cols] = product.reshape(shards, size, job.cols)
            lane += job.cols
    if not mine:
        outs[0][0] = acc[...].astype(BF16)
    elif len(outs) == 1:
        outs[0][0] = (acc[...] + got[0][0].astype(F32)).astype(BF16)
    else:
        for mask, out in enumerate(outs):

            @pl.when(step == mask)
            def _(out=out):
                out[...] = (acc[...] + got[0][0].astype(F32)).astype(BF16)


def weight_call(plan, lefts, rights, jobs, got, relative):
    rows = lefts[0].shape[1]
    n = plan.blocks
    mine = got is not None
    shape = (plan.shards // n, plan.shard_rows, sum(job.lanes for job in jobs))
    block = pl.BlockSpec((1, *shape), lambda i: (i, 0, 0, 0))
    if mine and relative:
        out_shape = [jax.ShapeDtypeStruct(shape, BF16)] * n
        out_specs = [whole(shape)] * n
    else:
        out_shape = [jax.ShapeDtypeStruct((n, *shape), BF16)]
        out_specs = [block]
    flops = sum(2 * rows * lefts[job.left].shape[0] * job.cols for job in jobs if not job.given)
    moved = sum(value.size * 2 for value in [*lefts, *rights])
    moved += 2 * n * shape[0] * shape[1] * shape[2] * (2 if mine else 1)
    result = pl.pallas_call(
        functools.partial(weight_kernel, jobs, len(lefts), len(rights), mine, relative),
        out_shape=out_shape,
        grid=(n,),
        in_specs=[smem()]
        + [whole(value.shape) for value in [*lefts, *rights]]
        + ([block] if mine else []),
        out_specs=out_specs,
        scratch_shapes=[pltpu.VMEM(shape, F32)],
        compiler_params=params(56),
        cost_estimate=cost(flops, moved),
        name="weight_mine" if mine else "weight_theirs",
    )(plan.meta, *lefts, *rights, *([got] if mine else []))
    return result if mine and relative else result[0]


class WeightGrads:
    def __init__(self, plan, lefts, rights, jobs, relative):
        self.plan, self.lefts, self.rights, self.jobs = plan, lefts, rights, jobs
        self.relative = relative and plan.staged

    def theirs(self, order):
        lefts = [order.gate(self.lefts[0]), *self.lefts[1:]]
        out = weight_call(self.plan, lefts, self.rights, self.jobs, None, self.relative)
        order.mark(out)
        self.got = other_core(out)

    def mine(self, order):
        plan = self.plan
        lefts = [order.gate(self.lefts[0]), *self.lefts[1:]]
        out = weight_call(plan, lefts, self.rights, self.jobs, self.got, self.relative)
        if self.relative:
            order.mark(out[0])
            self.sums = Collect(plan, out)
            return
        order.mark(out)
        tall = sum(job.lanes for job in self.jobs if job.tall)
        out = out.reshape(plan.width, -1)
        if plan.staged:
            self.total = lax.psum_scatter(out, ("dp", "ctx"), scatter_dimension=0, tiled=True)
            return
        cut = out.shape[1] - tall
        self.total = lax.psum_scatter(out[:, :cut], ("dp", "ctx"), scatter_dimension=0, tiled=True)
        if tall:
            part = from_lanes(out[:, cut:])
            part = lax.psum_scatter(part, ("dp", "ctx"), scatter_dimension=0, tiled=True)
            self.total = jnp.concatenate([self.total, to_lanes(part)], axis=1)

    def step(self, name, order):
        if self.relative:
            getattr(self.sums, name)(order)

    def result(self):
        return self.sums.result() if self.relative else self.total


class Order:
    def __init__(self):
        self.earlier = []

    def gate(self, value):
        return after(value, *self.earlier)

    def mark(self, value):
        self.earlier = [] if value is None else [value]

    def need(self, *values):
        self.earlier += [value for value in values if value is not None]


def by_section(plan, first, second):
    return jnp.where(plan.section == 0, first, second)


def take_half(plan, matrix, which):
    half = matrix.shape[-1] // 2
    return lax.dynamic_slice_in_dim(matrix, which * half, half, axis=matrix.ndim - 1)


def to_sequences(plan, tokens):
    pieces = tokens.reshape(plan.n_seq, 2, plan.half, plan.width)
    mine = lax.dynamic_index_in_dim(pieces, plan.section, 1, keepdims=False)
    mine = mine.reshape(plan.n_ctx, plan.sub, plan.width)
    return exchange_ctx(mine).reshape(plan.rows, plan.width)


def from_sequences(plan, stack):
    return exchange_ctx(stack.reshape(stack.shape[0], plan.n_ctx, plan.sub, plan.width), 1)


def arranged(plan, moved, *earlier):
    moved = after(moved, *earlier)
    return moved.reshape(moved.shape[0], plan.n_seq, plan.half, plan.width)


def to_output(plan, layers):
    own = by_section(plan, layers[0], layers[1])
    got = other_core(by_section(plan, layers[1], layers[0]))
    first = by_section(plan, own, got)
    second = by_section(plan, got, own)
    both = jnp.stack([first, second], axis=1).astype(F32)
    return both.reshape(1, plan.micro, plan.seqs, plan.span, plan.width)


def shared_keys(plan, own):
    chunks = []
    for mask in range(plan.parts):
        here = own if mask == 0 else xor_ctx(plan, own, mask)
        chunks += [here, other_core(here)]
    return chunks


def return_keys(plan, far):
    got = []
    for mask in range(plan.parts):
        for core in range(2):
            index = 2 * mask + core
            if index == 0:
                continue
            part = far[index - 1]
            if core:
                part = other_core(part)
            if mask:
                part = xor_ctx(plan, part, mask)
            got.append(part)
    return got


def positions_of(plan, section, ctx):
    part = ctx % plan.parts
    start = jnp.arange(plan.n_ctx)[:, None] * plan.span + section * plan.half + part * plan.sub
    return (start + jnp.arange(plan.sub)[None, :]).reshape(-1)


def rope_tables(positions):
    half_width = HD // 2
    frequency = jnp.power(10000.0, -(jnp.arange(half_width).astype(F32) * 2.0) / HD)
    angles = positions.astype(F32)[:, None] * frequency[None, :]
    cos, sin = jnp.cos(angles), jnp.sin(angles)
    return jnp.concatenate([cos] * 4, axis=1), jnp.concatenate([-sin, sin, -sin, sin], axis=1)


def local(tokens, upstream, lengths, w_qkv, w_out, w_in, w_back, gain_attn, gain_ffn):
    plan = Plan(tokens, w_in)
    width = plan.width
    layers = 2

    qkv_low, out_low = w_qkv[0].astype(BF16), w_out[0].astype(BF16)
    in_low, back_low = w_in[0].astype(BF16), to_lanes_of_halves(w_back[0].astype(BF16))
    both = jnp.stack([gain_attn[0], gain_ffn[0]], axis=1).astype(BF16)
    both = jnp.pad(both, ((0, 0), (0, GAIN_LANES - 2)))
    here, there = plan.section, 1 - plan.section

    def attn_half(which):
        value = jnp.where(which == 0, qkv_low[:, 2 * width :], out_low)
        return jnp.concatenate([take_half(plan, qkv_low[:, : 2 * width], which), value, both], axis=1)

    def ffn_half(which):
        return jnp.concatenate(
            [take_half(plan, in_low, which), take_half(plan, back_low, which)], axis=1
        )

    def shards_of(half):
        kept, got = half(here), other_core(half(there))
        return by_section(plan, kept, got), by_section(plan, got, kept)

    attn_shards, ffn_shards = shards_of(attn_half), shards_of(ffn_half)
    tall = 4 * (width // 2)
    if plan.staged:
        attn0_z = spread_ctx(plan, attn_shards[0])
        attn0_dp = SpreadDp(plan, attn0_z)
        ffn0_z = spread_ctx(plan, after(ffn_shards[0], attn0_z))
        source = to_sequences(plan, after(tokens, ffn0_z))
        attn1 = gather_natural(plan, after(attn_shards[1], attn0_z), tall)
        attn0 = attn0_dp.result(ffn0_z)
        ffn0_dp = SpreadDp(plan, ffn0_z, *attn0_dp.got)
        ffn1 = gather_natural(plan, after(ffn_shards[1], attn0_z), tall)
    else:
        source = to_sequences(plan, tokens)
        attn0, attn1 = (gather_natural(plan, shard) for shard in attn_shards)
        ffn0, ffn1 = (gather_natural(plan, shard, tall) for shard in ffn_shards)
    attn0.share()

    cos, sin = rope_tables(positions_of(plan, plan.section, plan.ctx))
    sequence = plan.ctx // plan.parts
    length = lax.dynamic_index_in_dim(lengths.reshape(-1), sequence, 0, keepdims=False)
    places = []
    for mask in range(plan.parts):
        for core in range(2):
            places.append(positions_of(plan, plan.section ^ core, plan.ctx ^ mask))
    hidden_key = jnp.where(jnp.concatenate(places) < length, 0.0, MASKED)
    lane = jnp.arange(PAIR)
    bias = jnp.where(lane[None, :] == 0, hidden_key[:, None], 0.0).astype(BF16)

    order = Order()
    saved, acts, gains = [], [], []

    def forward_qkv(x, attn):
        a, query, own_kv, rows = qkv_forward(plan, order.gate(x), cos, sin, attn)
        order.mark(query)
        gains.append(rows)
        return a, query, shared_keys(plan, own_kv)

    def forward_attention(query, kv):
        out = attention_forward(plan, order.gate(query), kv, bias)
        order.mark(out[2])
        return out

    def forward_ffn(x, layer, attn, ffn, held):
        a, query, kv, o, ot, lse = held
        u2, b, result, low, h, slope = ffn_forward(
            plan, order.gate(o), x, gains[layer], attn, ffn
        )
        order.mark(low)
        saved.append((x, a, query, kv, o, ot, lse, u2, b, h, slope))
        acts.append(low)
        return result

    held = forward_qkv(source, attn0)
    held += tuple(forward_attention(*held[1:]))
    if plan.staged:
        ffn0 = ffn0_dp.result(held[5])
    ffn0.share(held[5])
    attn1.share(held[5])
    x = forward_ffn(source, 0, attn0, ffn0, held)
    held = forward_qkv(x, attn1)
    ffn1.share(held[1])
    held += tuple(forward_attention(*held[1:]))
    cotangent = to_sequences(plan, after(upstream, held[1]))
    forward_ffn(x, 1, attn1, ffn1, held)
    weights = [(attn0, ffn0), (attn1, ffn1)]

    hidden_half, width_half = plan.hidden // 2, width // 2
    grads, dgains = [None] * layers, [None] * layers

    def ffn_part(layer, c):
        attn, ffn = weights[layer]
        u2, _, _, slope = saved[layer][7:]
        out = ffn_backward(plan, order.gate(c), slope, u2, gains[layer], attn, ffn)
        order.mark(out[-1])
        return out

    def attention_part(layer, do):
        x, a, query, kv, o, ot, lse, u2, b, h, slope = saved[layer]
        dq, dk, dv, *far = attention_backward(plan, query, order.gate(do), o, lse, bias, kv)
        order.mark(dq)
        return dq, dk, dv, return_keys(plan, far)

    def qkv_part(layer, dq, dk, dv, far, du2, dg2):
        x = saved[layer][0]
        dqkv, dx, low, dg1 = qkv_backward(
            plan, order.gate(dq), dk, dv, far, du2, x, gains[layer], cos, sin, weights[layer][0]
        )
        order.mark(dg1)
        grads[layer] = low
        dgains[layer] = (dg1, dg2)
        return dqkv, dx, low

    def job_in(left, right):
        return Job(left, right, 0, hidden_half)

    def job_out(left, right):
        return Job(left, right, 0, width_half)

    def job_back(left, right):
        return Job(left, right, 0, width_half, tall=True)

    def job_qkv(left, right):
        return Job(left, right, 0, 3 * width // 2)

    a1, ot1, b1, h1 = (saved[1][i] for i in (1, 5, 8, 9))
    a0, ot0, b0, h0 = (saved[0][i] for i in (1, 5, 8, 9))

    cf, dhp, du2, dz, do, dg2 = ffn_part(1, cotangent)
    sum_ffn1 = WeightGrads(
        plan, [b1, ot1, h1], [dhp, dz, cf], [job_in(0, 0), job_out(1, 1), job_back(2, 2)], False
    )
    sum_ffn1.theirs(order)
    back = attention_part(1, do)
    sum_ffn1.mine(order)
    dqkv, c, low = qkv_part(1, *back, du2, dg2)
    early = from_sequences(plan, jnp.stack([acts[0], acts[1], grads[1]]))
    sum_mixed = WeightGrads(plan, [a1, h0], [dqkv, low], [job_qkv(0, 0), job_back(1, 1)], True)
    sum_mixed.theirs(order)
    sum_mixed.mine(order)
    cf, dhp, du2, dz, do, dg2 = ffn_part(0, c)
    sum_in0 = WeightGrads(plan, [b0, ot0], [dhp, dz], [job_in(0, 0), job_out(1, 1)], True)
    sum_in0.theirs(order)
    sum_in0.mine(order)
    sum_mixed.step("first", order)
    sum_mixed.step("second", order)
    back = attention_part(0, do)
    dqkv, c, low = qkv_part(0, *back, du2, dg2)
    rows = jnp.concatenate([row for pair in dgains for row in pair], axis=0)
    columns = jnp.pad(rows.T, ((0, 0), (0, GAIN_LANES - 2 * layers)))
    sum_qkv0 = WeightGrads(
        plan, [a0, columns], [dqkv], [job_qkv(0, 0), Job(1, None, 0, GAIN_LANES)], True
    )
    sum_qkv0.theirs(order)
    sum_qkv0.mine(order)
    late = from_sequences(plan, order.gate(grads[0])[None])
    sum_in0.step("second", order)
    sum_qkv0.step("second", order)
    early = arranged(plan, early, *order.earlier)
    late = arranged(plan, late, *order.earlier)

    cut = hidden_half + width_half
    ffn1_sum, mixed_sum = sum_ffn1.result(), sum_mixed.result()
    in0_sum, qkv0_sum = sum_in0.result(), sum_qkv0.result()
    wide = 3 * width // 2
    gain_sums = lax.dynamic_slice_in_dim(qkv0_sum[:, wide:], plan.section * 2, 2, axis=1).T.astype(F32)
    sums = [
        (qkv0_sum[:, :wide], in0_sum[:, hidden_half:], in0_sum[:, :hidden_half], from_lanes(mixed_sum[:, wide:])),
        (
            mixed_sum[:, :wide],
            ffn1_sum[:, hidden_half:cut],
            ffn1_sum[:, :hidden_half],
            from_lanes(ffn1_sum[:, cut:]),
        ),
    ]

    def to_owner(first, second):
        own = by_section(plan, first, second)
        got = other_core(by_section(plan, second, first))
        left, right = by_section(plan, own, got), by_section(plan, got, own)
        return jnp.concatenate([left, right], axis=1).astype(F32)[None]

    weight_grads = [to_owner(one, two) for one, two in zip(*sums)]
    return (
        to_output(plan, early[:2]),
        to_output(plan, [late[0], early[2]]),
        *weight_grads,
        gain_sums[0:1],
        gain_sums[1:2],
    )


def solution(mesh):
    rows = P(None, "dp", "ctx", None)
    weight = P("section", ("dp", "ctx"), None)
    gain = P("section", ("dp", "ctx"))
    out_rows = P("section", None, "dp", "ctx", None)
    return jax.shard_map(
        local,
        mesh=mesh,
        in_specs=(rows, rows, P(None, "dp"), weight, weight, weight, weight, gain, gain),
        out_specs=(out_rows, out_rows, weight, weight, weight, weight, gain, gain),
        check_vma=False,
    )
```

time: 803 us -> 635 us (0.79)
  starting transfers between devices: 226 us -> 65.8 us
  Pallas kernels: 292 us -> 239 us
  waiting for transfers between devices: 216 us -> 239 us
  other arithmetic: 32.5 us -> 51.4 us
  between operations: 2.69 us -> 14.6 us
    ppermute x117 -> x15, waiting for transfers between devices: 212 us -> 108 us  [xor_dp(): return lax.ppermute(value, 'dp', [(i, i ^ mask) for i in range(plan.n_dp)])]
    all_to_all x6 -> x9, waiting for transfers between devices: 0.02 us -> 103 us  [exchange_ctx(): return lax.all_to_all(value, 'ctx', dim, dim, tiled=True)]
    ppermute x117 -> x15, starting transfers between devices: 115 us -> 13.4 us  [xor_dp(): return lax.ppermute(value, 'dp', [(i, i ^ mask) for i in range(plan.n_dp)])]
    ppermute x58 -> x20, starting transfers between devices: 85 us -> 15 us  [other_core(): return lax.ppermute(value, 'section', [(0, 1), (1, 0)])]
    pallas_call x30 -> x16, Pallas kernels: 222 us -> 169 us  [the longest x8 62.6 us: weight_call(): pl.pallas_call(functools.partial(weight_kernel, jobs, len(lefts), len(rig...]
    ppermute x58 -> x20, waiting for transfers between devices: 4.03 us -> 28.2 us  [other_core(): return lax.ppermute(value, 'section', [(0, 1), (1, 0)])]
    all_to_all x6 -> x9, starting transfers between devices: 25.6 us -> 37.2 us  [exchange_ctx(): return lax.all_to_all(value, 'ctx', dim, dim, tiled=True)]
    another operation x6, other arithmetic: 2.13 us -> 10.9 us  [the longest x2 7.68 us: result(): blocks = jnp.stack([after(self.block, *earlier), *self.got])]
  transfers between devices with their start and end apart: 181 -> 47, of which waited for: 52 -> 21; matrix products, arithmetic and copies ran while one was open for 5% -> 8% of each run, Pallas kernels for 37% -> 31%
where the time goes in v2:
time: 635 us; the launch traced here: 630 us
  waiting for transfers between devices  239 us (38%)
  Pallas kernels  239 us (38%)
  starting transfers between devices  65.8 us (10%)
  other arithmetic  51.4 us (8%)
  local copies, waits for them, and re-layouts  20.7 us (3%)
  between operations  14.6 us (2%)
    ppermute x15, waiting for transfers between devices, xor_dp(): return lax.ppermute(value, 'dp', [(i, i ^ mask) for i in range(plan.n_dp)])  108 us
    all_to_all x9, waiting for transfers between devices, exchange_ctx(): return lax.all_to_all(value, 'ctx', dim, dim, tiled=True)  103 us
    pallas_call x8, Pallas kernels, weight_call(): pl.pallas_call(functools.partial(weight_kernel, jobs, len(lefts), len(rig...  62.6 us
    pallas_call x2, Pallas kernels, attention_backward(): pl.pallas_call(functools.partial(attention_back_kernel, chunks, min(256,...  41.2 us
    all_to_all x9, starting transfers between devices, exchange_ctx(): return lax.all_to_all(value, 'ctx', dim, dim, tiled=True)  37.2 us
    pallas_call x2, Pallas kernels, ffn_backward(): pl.pallas_call(functools.partial(ffn_back_kernel, relative), out_shape=[w...  34 us
    pallas_call x2, Pallas kernels, ffn_forward(): pl.pallas_call(functools.partial(ffn_kernel, relative), out_shape=[jax.Sh...  32.9 us
    pallas_call x2, Pallas kernels, attention_forward(): pl.pallas_call(functools.partial(attention_kernel, chunks, min(256, rows)...  28.3 us
  transfers between devices with their start and end apart: 47, of which 21 were waited for; matrix products, arithmetic and copies ran while one was open for 8% of the time, Pallas kernels for 31%

profile of v2, /device:TPU:1, one launch (start us, length us, event | category | flops | bytes accessed | tf_op | source)
XLA Modules:
  0.0 630.3 jit_solution(9446298735735569499)
XLA Ops:
  20.2 15.3 %all-to-all-done = bf16[4,48,1664]{2,1,0:T(8,128)(2,1)S(1)} async-done(((bf16[4,48,1664]{2,1,0:T(8,128)(2,1)}), bf16[4,48,1664]{2,1,0:T(8,128)(2,1)S(1)}, u32[]{:S(2)}, u32[]{:S(2)}) %all-to-all-start) | async-done | bytes 639008 | tf_op jit(solution)/shard_map/all_to_all | solution.py:95
  46.5 29.1 %all-to-all-done.1 = bf16[4,48,3072]{2,1,0:T(8,128)(2,1)S(1)} async-done(((bf16[4,48,3072]{2,1,0:T(8,128)(2,1)}), bf16[4,48,3072]{2,1,0:T(8,128)(2,1)S(1)}, u32[]{:S(2)}, u32[]{:S(2)}) %all-to-all-start.1) | async-done | bytes 1179680 | tf_op jit(solution)/shard_map/all_to_all | solution.py:95
  88.1 27.9 %all-to-all-done.2 = bf16[4,128,768]{2,1,0:T(8,128)(2,1)S(1)} async-done(((bf16[4,128,768]{2,1,0:T(8,128)(2,1)}), bf16[4,128,768]{2,1,0:T(8,128)(2,1)S(1)}, u32[]{:S(2)}, u32[]{:S(2)}) %all-to-all-start.2) | async-done | bytes 786464 | tf_op jit(solution)/shard_map/all_to_all | solution.py:95
  117.0 8.0 %qkv_forward.2 = (bf16[768,512]{1,0:T(8,128)(2,1)}, bf16[512,768]{1,0:T(8,128)(2,1)}, bf16[2,512,768]{2,1,0:T(8,128)(2,1)}, f32[8,768]{1,0:T(8,128)}) custom-call(s32[2]{0:T(128)} %pad_add_fusion.meta, bf16[512,768]{1,0:T(8,128)(2,1)} %bitcast.131, f32[512,128]{1,0:T(8,128)} %get-tuple-element.284.cos_ref, f32[512,128]{1,0:T(8,128)} %get-tuple-element.285.sin_ref, ...), custom_call_target="tpu_custom_call" | custom-call | flops 181193936 | bytes 825753 | tf_op jit(solution)/shard_map/qkv_forward/pallas_call | solution.py:355
  132.3 14.2 %attention_forward.2 = (bf16[512,768]{1,0:T(8,128)(2,1)}, bf16[768,512]{1,0:T(8,128)(2,1)}, f32[6,8,512]{2,1,0:T(8,128)}) custom-call(bf16[512,768]{1,0:T(8,128)(2,1)} %get-tuple-element.110.q_ref, bf16[2,512,768]{2,1,0:T(8,128)(2,1)} %get-tuple-element.111.refs_0_, bf16[2,512,768]{2,1,0:T(8,128)(2,1)} %copy-done.11, ...), custom_call_target="tpu_custom_call" | custom-call | flops 644245120 | bytes 471859 | tf_op jit(solution)/shard_map/attention_forward/pallas_call | solution.py:436
  146.4 10.4 %collective-permute-done.9 = bf16[192,3072]{1,0:T(8,128)(2,1)} collective-permute-done((bf16[192,3072]{1,0:T(8,128)(2,1)S(1)}, bf16[192,3072]{1,0:T(8,128)(2,1)}, u32[]{:S(2)}, u32[]{:S(2)}) %collective-permute-start.9) | collective-permute-done | bytes 1179680 | tf_op jit(solution)/shard_map/ppermute | solution.py:87
  156.8 29.8 %collective-permute-done.8 = bf16[192,3072]{1,0:T(8,128)(2,1)} collective-permute-done((bf16[192,3072]{1,0:T(8,128)(2,1)S(1)}, bf16[192,3072]{1,0:T(8,128)(2,1)}, u32[]{:S(2)}, u32[]{:S(2)}) %collective-permute-start.8) | collective-permute-done | bytes 1179680 | tf_op jit(solution)/shard_map/ppermute | solution.py:87
  194.8 11.5 %collective-permute-done.10.refs_3_ = bf16[16,48,3072]{2,1,0:T(8,128)(2,1)} collective-permute-done((bf16[16,48,3072]{2,1,0:T(8,128)(2,1)}, bf16[16,48,3072]{2,1,0:T(8,128)(2,1)}, u32[]{:S(2)}, u32[]{:S(2)}) %collective-permute-start.10) | collective-permute-done | bytes 4718624 | tf_op jit(solution)/shard_map/ppermute | solution.py:83
  206.3 16.3 %ffn_forward.2 = (f32[512,768]{1,0:T(8,128)}, bf16[768,512]{1,0:T(8,128)(2,1)}, f32[512,768]{1,0:T(8,128)}, bf16[512,768]{1,0:T(8,128)(2,1)}, bf16[3072,512]{1,0:T(8,128)(2,1)}, /*index=5*/bf16[512,3072]{1,0:T(8,128)(2,1)}) custom-call(s32[2]{0:T(128)} %pad_add_fusion.meta, bf16[512,768]{1,0:T(8,128)(2,1)} %get-tuple-element.114.o_ref, ...), custom_call_target="tpu_custom_call" | custom-call | flops 553019008 | bytes 2359296 | tf_op jit(solution)/shard_map/ffn_forward/pallas_call | solution.py:526
  224.0 8.1 %qkv_forward.3 = (bf16[768,512]{1,0:T(8,128)(2,1)}, bf16[512,768]{1,0:T(8,128)(2,1)}, bf16[2,512,768]{2,1,0:T(8,128)(2,1)}, f32[8,768]{1,0:T(8,128)}) custom-call(s32[2]{0:T(128)} %pad_add_fusion.meta, f32[512,768]{1,0:T(8,128)} %get-tuple-element.121.x_ref, f32[512,128]{1,0:T(8,128)} %get-tuple-element.284.cos_ref, f32[512,128]{1,0:T(8,128)} %get-tuple-element.285.sin_ref, ...), custom_call_target="tpu_custom_call" | custom-call | flops 181193936 | bytes 825753 | tf_op jit(solution)/shard_map/qkv_forward/pallas_call | solution.py:355
  243.5 14.1 %attention_forward.3 = (bf16[512,768]{1,0:T(8,128)(2,1)}, bf16[768,512]{1,0:T(8,128)(2,1)}, f32[6,8,512]{2,1,0:T(8,128)}) custom-call(bf16[512,768]{1,0:T(8,128)(2,1)} %get-tuple-element.125.q_ref, bf16[2,512,768]{2,1,0:T(8,128)(2,1)} %get-tuple-element.126.refs_0_, bf16[2,512,768]{2,1,0:T(8,128)(2,1)} %copy-done.12, ...), custom_call_target="tpu_custom_call" | custom-call | flops 644245120 | bytes 471859 | tf_op jit(solution)/shard_map/attention_forward/pallas_call | solution.py:436
  257.6 16.6 %ffn_forward.3 = (f32[512,768]{1,0:T(8,128)}, bf16[768,512]{1,0:T(8,128)(2,1)}, f32[512,768]{1,0:T(8,128)}, bf16[512,768]{1,0:T(8,128)(2,1)}, bf16[3072,512]{1,0:T(8,128)(2,1)}, /*index=5*/bf16[512,3072]{1,0:T(8,128)(2,1)}) custom-call(s32[2]{0:T(128)} %pad_add_fusion.meta, bf16[512,768]{1,0:T(8,128)(2,1)} %get-tuple-element.129.o_ref, ...), custom_call_target="tpu_custom_call" | custom-call | flops 553019008 | bytes 2359296 | tf_op jit(solution)/shard_map/ffn_forward/pallas_call | solution.py:526
  275.1 16.9 %ffn_backward.2 = (bf16[512,768]{1,0:T(8,128)(2,1)}, bf16[512,3072]{1,0:T(8,128)(2,1)}, f32[512,768]{1,0:T(8,128)}, bf16[512,768]{1,0:T(8,128)(2,1)}, bf16[512,768]{1,0:T(8,128)(2,1)}, /*index=5*/f32[1,768]{1,0:T(1,128)}) custom-call(s32[2]{0:T(128)} %pad_add_fusion.meta, bf16[512,768]{1,0:T(8,128)(2,1)} %bitcast.141, ...), custom_call_target="tpu_custom_call" | custom-call | flops 543581824 | bytes 2398617 | tf_op jit(solution)/shard_map/ffn_backward/pallas_call | solution.py:599
  292.1 9.0 %weight_theirs.4 = bf16[4,4,48,3456]{3,2,1,0:T(8,128)(2,1)} custom-call(s32[2]{0:T(128)} %pad_add_fusion.meta, bf16[768,512]{1,0:T(8,128)(2,1)} %get-tuple-element.149.refs_0_, bf16[768,512]{1,0:T(8,128)(2,1)} %get-tuple-element.142.refs_1_, bf16[3072,512]{1,0:T(8,128)(2,1)} %get-tuple-element.143.refs_2_, bf16[512,3072]{1,0:T(8,128)(2,1)} %get-tuple-element.144.refs_3_, ...), custom_call_target="tpu_custom_call" | custom-call | flops 271790912 | bytes 1474560 | tf_op jit(solution)/shard_map/weight_theirs/pallas_call | solution.py:848
  301.2 20.6 %attention_backward.2 = (bf16[512,768]{1,0:T(8,128)(2,1)}, f32[512,768]{1,0:T(8,128)}, f32[512,768]{1,0:T(8,128)}, bf16[2,512,768]{2,1,0:T(8,128)(2,1)}) custom-call(bf16[512,768]{1,0:T(8,128)(2,1)} %get-tuple-element.125.q_ref, bf16[512,768]{1,0:T(8,128)(2,1)} %get-tuple-element.147.do_ref, bf16[512,768]{1,0:T(8,128)(2,1)} %get-tuple-element.129.o_ref, ...), custom_call_target="tpu_custom_call" | custom-call | flops 1610612736 | bytes 1258291 | tf_op jit(solution)/shard_map/attention_backward/pallas_call | solution.py:677
  324.5 10.6 %weight_mine.4 = bf16[4,4,48,3456]{3,2,1,0:T(8,128)(2,1)} custom-call(s32[2]{0:T(128)} %pad_add_fusion.meta, bf16[768,512]{1,0:T(8,128)(2,1)} %get-tuple-element.149.refs_0_, bf16[768,512]{1,0:T(8,128)(2,1)} %get-tuple-element.142.refs_1_, bf16[3072,512]{1,0:T(8,128)(2,1)} %get-tuple-element.143.refs_2_, bf16[512,3072]{1,0:T(8,128)(2,1)} %get-tuple-element.144.refs_3_, ...), custom_call_target="tpu_custom_call" | custom-call | flops 271790912 | bytes 2005401 | tf_op jit(solution)/shard_map/weight_mine/pallas_call | solution.py:848
  336.3 11.9 %qkv_backward.2 = (bf16[512,2304]{1,0:T(8,128)(2,1)}, f32[512,768]{1,0:T(8,128)}, bf16[512,768]{1,0:T(8,128)(2,1)}, f32[1,768]{1,0:T(1,128)}) custom-call(s32[2]{0:T(128)} %pad_add_fusion.meta, bf16[512,768]{1,0:T(8,128)(2,1)} %get-tuple-element.150.dq_ref, f32[512,768]{1,0:T(8,128)} %get-tuple-element.151.dk_ref, f32[512,768]{1,0:T(8,128)} %get-tuple-element.152.dv_ref, ...), custom_call_target="tpu_custom_call" | custom-call | flops 181193936 | bytes 1533542 | tf_op jit(solution)/shard_map/qkv_backward/pallas_call | solution.py:754
  348.2 7.6 %weight_theirs.5 = bf16[4,4,48,2688]{3,2,1,0:T(8,128)(2,1)} custom-call(s32[2]{0:T(128)} %pad_add_fusion.meta, bf16[768,512]{1,0:T(8,128)(2,1)} %get-tuple-element.163.refs_0_, bf16[3072,512]{1,0:T(8,128)(2,1)} %get-tuple-element.161.refs_1_, bf16[512,2304]{1,0:T(8,128)(2,1)} %get-tuple-element.162.refs_2_, bf16[512,768]{1,0:T(8,128)(2,1)} %get-tuple-element.155.refs_3_), custom_call_target="tpu_custom_call" | custom-call | flops 211392928 | bytes 1120665 | tf_op jit(solution)/shard_map/weight_theirs/pallas_call | solution.py:848
  355.9 7.3 %collective-permute-done.16.refs_4_ = bf16[4,4,48,2688]{3,2,1,0:T(8,128)(2,1)} collective-permute-done((bf16[4,4,48,2688]{3,2,1,0:T(8,128)(2,1)}, bf16[4,4,48,2688]{3,2,1,0:T(8,128)(2,1)}, u32[]{:S(2)}, u32[]{:S(2)}) %collective-permute-start.16) | collective-permute-done | bytes 4128800 | tf_op jit(solution)/shard_map/ppermute | solution.py:83
  363.2 9.8 %weight_mine.5 = (bf16[4,48,2688]{2,1,0:T(8,128)(2,1)}, bf16[4,48,2688]{2,1,0:T(8,128)(2,1)}, bf16[4,48,2688]{2,1,0:T(8,128)(2,1)}, bf16[4,48,2688]{2,1,0:T(8,128)(2,1)}) custom-call(s32[2]{0:T(128)} %pad_add_fusion.meta, bf16[768,512]{1,0:T(8,128)(2,1)} %get-tuple-element.163.refs_0_, bf16[3072,512]{1,0:T(8,128)(2,1)} %get-tuple-element.161.refs_1_, ...), custom_call_target="tpu_custom_call" | custom-call | flops 211392928 | bytes 1533542 | tf_op jit(solution)/shard_map/weight_mine/pallas_call | solution.py:848
  373.0 17.1 %ffn_backward.3 = (bf16[512,768]{1,0:T(8,128)(2,1)}, bf16[512,3072]{1,0:T(8,128)(2,1)}, f32[512,768]{1,0:T(8,128)}, bf16[512,768]{1,0:T(8,128)(2,1)}, bf16[512,768]{1,0:T(8,128)(2,1)}, /*index=5*/f32[1,768]{1,0:T(1,128)}) custom-call(s32[2]{0:T(128)} %pad_add_fusion.meta, f32[512,768]{1,0:T(8,128)} %get-tuple-element.165.c_ref, ...), custom_call_target="tpu_custom_call" | custom-call | flops 543581824 | bytes 2398617 | tf_op jit(solution)/shard_map/ffn_backward/pallas_call | solution.py:599
  390.1 6.4 %weight_theirs.6 = bf16[4,4,48,1920]{3,2,1,0:T(8,128)(2,1)} custom-call(s32[2]{0:T(128)} %pad_add_fusion.meta, bf16[768,512]{1,0:T(8,128)(2,1)} %get-tuple-element.175.refs_0_, bf16[768,512]{1,0:T(8,128)(2,1)} %get-tuple-element.172.refs_1_, bf16[512,3072]{1,0:T(8,128)(2,1)} %get-tuple-element.173.refs_2_, bf16[512,768]{1,0:T(8,128)(2,1)} %get-tuple-element.174.refs_3_), custom_call_target="tpu_custom_call" | custom-call | flops 150994944 | bytes 845414 | tf_op jit(solution)/shard_map/weight_theirs/pallas_call | solution.py:848
  404.9 8.0 %weight_mine.6 = (bf16[4,48,1920]{2,1,0:T(8,128)(2,1)}, bf16[4,48,1920]{2,1,0:T(8,128)(2,1)}, bf16[4,48,1920]{2,1,0:T(8,128)(2,1)}, bf16[4,48,1920]{2,1,0:T(8,128)(2,1)}) custom-call(s32[2]{0:T(128)} %pad_add_fusion.meta, bf16[768,512]{1,0:T(8,128)(2,1)} %get-tuple-element.175.refs_0_, bf16[768,512]{1,0:T(8,128)(2,1)} %get-tuple-element.172.refs_1_, ...), custom_call_target="tpu_custom_call" | custom-call | flops 150994944 | bytes 1140326 | tf_op jit(solution)/shard_map/weight_mine/pallas_call | solution.py:848
  412.9 12.3 %collective-permute-done.18 = bf16[4,48,2688]{2,1,0:T(8,128)(2,1)S(1)} collective-permute-done((bf16[4,48,2688]{2,1,0:T(8,128)(2,1)}, bf16[4,48,2688]{2,1,0:T(8,128)(2,1)S(1)}, u32[]{:S(2)}, u32[]{:S(2)}) %collective-permute-start.18) | collective-permute-done | bytes 1032224 | tf_op jit(solution)/shard_map/ppermute | solution.py:87
  425.4 26.6 %collective-permute-done.20 = bf16[4,48,2688]{2,1,0:T(8,128)(2,1)} collective-permute-done((bf16[4,48,2688]{2,1,0:T(8,128)(2,1)}, bf16[4,48,2688]{2,1,0:T(8,128)(2,1)}, u32[]{:S(2)}, u32[]{:S(2)}) %collective-permute-start.20) | collective-permute-done | bytes 1032224 | tf_op jit(solution)/shard_map/ppermute | solution.py:87
  455.0 20.6 %attention_backward.3 = (bf16[512,768]{1,0:T(8,128)(2,1)}, f32[512,768]{1,0:T(8,128)}, f32[512,768]{1,0:T(8,128)}, bf16[2,512,768]{2,1,0:T(8,128)(2,1)}) custom-call(bf16[512,768]{1,0:T(8,128)(2,1)} %get-tuple-element.110.q_ref, bf16[512,768]{1,0:T(8,128)(2,1)} %get-tuple-element.181.do_ref, bf16[512,768]{1,0:T(8,128)(2,1)} %get-tuple-element.114.o_ref, ...), custom_call_target="tpu_custom_call" | custom-call | flops 1610612736 | bytes 1258291 | tf_op jit(solution)/shard_map/attention_backward/pallas_call | solution.py:677
  481.6 11.9 %qkv_backward.3 = (bf16[512,2304]{1,0:T(8,128)(2,1)}, f32[512,768]{1,0:T(8,128)}, bf16[512,768]{1,0:T(8,128)(2,1)}, f32[1,768]{1,0:T(1,128)}) custom-call(s32[2]{0:T(128)} %pad_add_fusion.meta, bf16[512,768]{1,0:T(8,128)(2,1)} %get-tuple-element.182.dq_ref, f32[512,768]{1,0:T(8,128)} %get-tuple-element.183.dk_ref, f32[512,768]{1,0:T(8,128)} %get-tuple-element.184.dv_ref, ...), custom_call_target="tpu_custom_call" | custom-call | flops 181193936 | bytes 1533542 | tf_op jit(solution)/shard_map/qkv_backward/pallas_call | solution.py:754
  514.3 9.0 %collective-permute-done.23 = bf16[4,48,1920]{2,1,0:T(8,128)(2,1)S(1)} collective-permute-done((bf16[4,48,1920]{2,1,0:T(8,128)(2,1)}, bf16[4,48,1920]{2,1,0:T(8,128)(2,1)S(1)}, u32[]{:S(2)}, u32[]{:S(2)}) %collective-permute-start.23) | collective-permute-done | bytes 737312 | tf_op jit(solution)/shard_map/ppermute | solution.py:87
  524.1 15.9 %collective-permute-done.25 = bf16[4,48,1920]{2,1,0:T(8,128)(2,1)S(1)} collective-permute-done((bf16[4,48,1920]{2,1,0:T(8,128)(2,1)}, bf16[4,48,1920]{2,1,0:T(8,128)(2,1)S(1)}, u32[]{:S(2)}, u32[]{:S(2)}) %collective-permute-start.25) | collective-permute-done | bytes 737312 | tf_op jit(solution)/shard_map/ppermute | solution.py:87
  549.9 14.2 %all-to-all-done.8 = bf16[4,48,1920]{2,1,0:T(8,128)(2,1)} async-done(((bf16[4,48,1920]{2,1,0:T(8,128)(2,1)}), bf16[4,48,1920]{2,1,0:T(8,128)(2,1)}, u32[]{:S(2)}, u32[]{:S(2)}) %all-to-all-start.8) | async-done | bytes 737312 | tf_op jit(solution)/shard_map/all_to_all | solution.py:95
  577.8 9.4 %all-to-all-done.5 = bf16[1,4,128,768]{3,2,0,1:T(8,128)(2,1)S(1)} async-done(((bf16[1,4,128,768]{3,2,0,1:T(8,128)(2,1)}), bf16[1,4,128,768]{3,2,0,1:T(8,128)(2,1)S(1)}, u32[]{:S(2)}, u32[]{:S(2)}) %all-to-all-start.5) | async-done | bytes 786464 | tf_op jit(solution)/shard_map/all_to_all | solution.py:95
  598.0 6.8 %all-to-all-done.6 = bf16[4,48,1280]{2,1,0:T(8,128)(2,1)} async-done(((bf16[4,48,1280]{2,1,0:T(8,128)(2,1)}), bf16[4,48,1280]{2,1,0:T(8,128)(2,1)}, u32[]{:S(2)}, u32[]{:S(2)}) %all-to-all-start.6) | async-done | bytes 491552 | tf_op jit(solution)/shard_map/all_to_all | solution.py:95
  (210 shorter events, 162.5 us)
Async XLA Ops:
  13.2 22.2 %all-to-all-start = ((bf16[4,48,1664]{2,1,0:T(8,128)(2,1)}), bf16[4,48,1664]{2,1,0:T(8,128)(2,1)S(1)}, u32[]{:S(2)}, u32[]{:S(2)}) async-start(bf16[4,48,1664]{2,1,0:T(8,128)(2,1)} %bitcast.10), calls=%async_computation | async-start | bytes 1277952 | tf_op jit(solution)/shard_map/all_to_all | solution.py:95
  19.0 175.8 %all-gather.3.cloned.1.call-start = ((), (), s32[]{:S(2)}) async-start(), calls=%async_computation.10 | async-start | bytes 2715648 | tf_op jit(solution)/shard_map/all_gather | solution.py:136
  40.2 35.4 %all-to-all-start.1 = ((bf16[4,48,3072]{2,1,0:T(8,128)(2,1)}), bf16[4,48,3072]{2,1,0:T(8,128)(2,1)S(1)}, u32[]{:S(2)}, u32[]{:S(2)}) async-start(bf16[4,48,3072]{2,1,0:T(8,128)(2,1)} %bitcast.140), calls=%async_computation.1 | async-start | bytes 2359296 | tf_op jit(solution)/shard_map/all_to_all | solution.py:95
  43.8 188.4 %all-gather.5.cloned.1.call-start = ((), (), s32[]{:S(2)}) async-start(), calls=%async_computation.11 | async-start | bytes 5013504 | tf_op jit(solution)/shard_map/all_gather | solution.py:136
  43.8 31.8 %collective-permute-start.4 = (bf16[192,1664]{1,0:T(8,128)(2,1)S(1)}, bf16[192,1664]{1,0:T(8,128)(2,1)}, u32[]{:S(2)}, u32[]{:S(2)}) collective-permute-start(bf16[192,1664]{1,0:T(8,128)(2,1)S(1)} %bitcast.143), channel_id=1, source_target_pairs={{0,12},{4,8},{8,4},{12,0},{1,13},{5,9},{9,5},{13,1},{2,14},{6,10},... | collective-permute-start | bytes 1916936 | tf_op jit(solution)/shard_map/ppermute | solution.py:87
  46.1 29.6 %collective-permute-start.3 = (bf16[192,1664]{1,0:T(8,128)(2,1)S(1)}, bf16[192,1664]{1,0:T(8,128)(2,1)}, u32[]{:S(2)}, u32[]{:S(2)}) collective-permute-start(bf16[192,1664]{1,0:T(8,128)(2,1)S(1)} %bitcast.144), channel_id=1, source_target_pairs={{0,8},{4,12},{8,0},{12,4},{1,9},{5,13},{9,1},{13,5},{2,10},{6,14},... | collective-permute-start | bytes 1916936 | tf_op jit(solution)/shard_map/ppermute | solution.py:87
  46.3 29.4 %collective-permute-start.2 = (bf16[192,1664]{1,0:T(8,128)(2,1)S(1)}, bf16[192,1664]{1,0:T(8,128)(2,1)}, u32[]{:S(2)}, u32[]{:S(2)}) collective-permute-start(bf16[192,1664]{1,0:T(8,128)(2,1)S(1)} %bitcast.145), channel_id=1, source_target_pairs={{0,4},{4,0},{8,12},{12,8},{1,5},{5,1},{9,13},{13,9},{2,6},{6,2},{1... | collective-permute-start | bytes 1916936 | tf_op jit(solution)/shard_map/ppermute | solution.py:87
  79.4 36.6 %collective-permute-start.5 = (bf16[16,48,1664]{2,1,0:T(8,128)(2,1)}, bf16[16,48,1664]{2,1,0:T(8,128)(2,1)}, u32[]{:S(2)}, u32[]{:S(2)}) collective-permute-start(bf16[16,48,1664]{2,1,0:T(8,128)(2,1)} %bitcast.22.refs_0_.refs_1_), channel_id=1, source_target_pairs={{0,16},{16,0},{1,17},{17,1},{2,18},{18,2},{3,19},{19,3},{4,20},{20... | collective-permute-start | bytes 7667720 | tf_op jit(solution)/shard_map/ppermute | solution.py:83
  81.5 34.6 %all-to-all-start.2 = ((bf16[4,128,768]{2,1,0:T(8,128)(2,1)}), bf16[4,128,768]{2,1,0:T(8,128)(2,1)S(1)}, u32[]{:S(2)}, u32[]{:S(2)}) async-start(bf16[4,128,768]{2,1,0:T(8,128)(2,1)} %dynamic-slice_bitcast_fusion.1), calls=%async_computation.2 | async-start | bytes 1572864 | tf_op jit(solution)/shard_map/all_to_all | solution.py:95
  126.2 30.7 %collective-permute-start.9 = (bf16[192,3072]{1,0:T(8,128)(2,1)S(1)}, bf16[192,3072]{1,0:T(8,128)(2,1)}, u32[]{:S(2)}, u32[]{:S(2)}) collective-permute-start(bf16[192,3072]{1,0:T(8,128)(2,1)S(1)} %bitcast.136), channel_id=1, source_target_pairs={{0,12},{4,8},{8,4},{12,0},{1,13},{5,9},{9,5},{13,1},{2,14},{6,10},... | collective-permute-start | bytes 3538952 | tf_op jit(solution)/shard_map/ppermute | solution.py:87
  127.4 59.3 %collective-permute-start.8 = (bf16[192,3072]{1,0:T(8,128)(2,1)S(1)}, bf16[192,3072]{1,0:T(8,128)(2,1)}, u32[]{:S(2)}, u32[]{:S(2)}) collective-permute-start(bf16[192,3072]{1,0:T(8,128)(2,1)S(1)} %bitcast.137), channel_id=1, source_target_pairs={{0,8},{4,12},{8,0},{12,4},{1,9},{5,13},{9,1},{13,5},{2,10},{6,14},... | collective-permute-start | bytes 3538952 | tf_op jit(solution)/shard_map/ppermute | solution.py:87
  127.6 62.1 %collective-permute-start.7 = (bf16[192,3072]{1,0:T(8,128)(2,1)S(1)}, bf16[192,3072]{1,0:T(8,128)(2,1)}, u32[]{:S(2)}, u32[]{:S(2)}) collective-permute-start(bf16[192,3072]{1,0:T(8,128)(2,1)S(1)} %bitcast.138), channel_id=1, source_target_pairs={{0,4},{4,0},{8,12},{12,8},{1,5},{5,1},{9,13},{13,9},{2,6},{6,2},{1... | collective-permute-start | bytes 3538952 | tf_op jit(solution)/shard_map/ppermute | solution.py:87
  194.7 27.8 %collective-permute-start.11 = (bf16[16,48,1664]{2,1,0:T(8,128)(2,1)}, bf16[16,48,1664]{2,1,0:T(8,128)(2,1)S(1)}, u32[]{:S(2)}, u32[]{:S(2)}) collective-permute-start(bf16[16,48,1664]{2,1,0:T(8,128)(2,1)} %bitcast.122), channel_id=1, source_target_pairs={{0,16},{16,0},{1,17},{17,1},{2,18},{18,2},{3,19},{19,3},{4,20},{20... | collective-permute-start | bytes 7667720 | tf_op jit(solution)/shard_map/ppermute | solution.py:83
  232.1 25.5 %collective-permute-start.13 = (bf16[16,48,3072]{2,1,0:T(8,128)(2,1)}, bf16[16,48,3072]{2,1,0:T(8,128)(2,1)}, u32[]{:S(2)}, u32[]{:S(2)}) collective-permute-start(bf16[16,48,3072]{2,1,0:T(8,128)(2,1)} %bitcast.128), channel_id=1, source_target_pairs={{0,16},{16,0},{1,17},{17,1},{2,18},{18,2},{3,19},{19,3},{4,20},{20... | collective-permute-start | bytes 14155784 | tf_op jit(solution)/shard_map/ppermute | solution.py:83
  234.8 39.4 %all-to-all-start.3 = ((bf16[4,128,768]{2,1,0:T(8,128)(2,1)}), bf16[4,128,768]{2,1,0:T(8,128)(2,1)S(1)}, u32[]{:S(2)}, u32[]{:S(2)}) async-start(bf16[4,128,768]{2,1,0:T(8,128)(2,1)} %dynamic-slice_bitcast_fusion), calls=%async_computation.3 | async-start | bytes 1572864 | tf_op jit(solution)/shard_map/all_to_all | solution.py:95
  238.3 333.1 %reduce-scatter.4.cloned.1.call-start = ((), (), s32[]{:S(2)}) async-start(), calls=%async_computation.12 | async-start | bytes 5640192 | tf_op jit(solution)/shard_map/reduce_scatter | solution.py:887
  301.0 21.3 %collective-permute-start.14 = (bf16[4,4,48,3456]{3,2,1,0:T(8,128)(2,1)}, bf16[4,4,48,3456]{3,2,1,0:T(8,128)(2,1)S(1)}, u32[]{:S(2)}, u32[]{:S(2)}) collective-permute-start(bf16[4,4,48,3456]{3,2,1,0:T(8,128)(2,1)} %weight_theirs.4), channel_id=1, source_target_pairs={{0,16},{16,0},{1,17},{17,1},{2,18},{18,2},{3,19},{19,3},{4,20},{20... | collective-permute-start | bytes 15925256 | tf_op jit(solution)/shard_map/ppermute | solution.py:83
  396.7 28.6 %collective-permute-start.18 = (bf16[4,48,2688]{2,1,0:T(8,128)(2,1)}, bf16[4,48,2688]{2,1,0:T(8,128)(2,1)S(1)}, u32[]{:S(2)}, u32[]{:S(2)}) collective-permute-start(bf16[4,48,2688]{2,1,0:T(8,128)(2,1)} %get-tuple-element.177), channel_id=1, source_target_pairs={{0,4},{4,0},{8,12},{12,8},{1,5},{5,1},{9,13},{13,9},{2,6},{6,2},{1... | collective-permute-start | bytes 3096584 | tf_op jit(solution)/shard_map/ppermute | solution.py:87
  397.6 27.7 %collective-permute-start.19 = (bf16[4,48,2688]{2,1,0:T(8,128)(2,1)}, bf16[4,48,2688]{2,1,0:T(8,128)(2,1)}, u32[]{:S(2)}, u32[]{:S(2)}) collective-permute-start(bf16[4,48,2688]{2,1,0:T(8,128)(2,1)} %get-tuple-element.178), channel_id=1, source_target_pairs={{0,8},{4,12},{8,0},{12,4},{1,9},{5,13},{9,1},{13,5},{2,10},{6,14},... | collective-permute-start | bytes 3096584 | tf_op jit(solution)/shard_map/ppermute | solution.py:87
  398.2 53.8 %collective-permute-start.20 = (bf16[4,48,2688]{2,1,0:T(8,128)(2,1)}, bf16[4,48,2688]{2,1,0:T(8,128)(2,1)}, u32[]{:S(2)}, u32[]{:S(2)}) collective-permute-start(bf16[4,48,2688]{2,1,0:T(8,128)(2,1)} %get-tuple-element.179), channel_id=1, source_target_pairs={{0,12},{4,8},{8,4},{12,0},{1,13},{5,9},{9,5},{13,1},{2,14},{6,10},... | collective-permute-start | bytes 3096584 | tf_op jit(solution)/shard_map/ppermute | solution.py:87
  401.1 99.5 %all-to-all-start.4 = ((bf16[3,4,128,768]{3,2,0,1:T(8,128)(2,1)}), bf16[3,4,128,768]{3,2,0,1:T(8,128)(2,1)S(1)}, u32[]{:S(2)}, u32[]{:S(2)}) async-start(bf16[3,4,128,768]{3,2,0,1:T(8,128)(2,1)} %pad_maximum_fusion.2), calls=%async_computation.4 | async-start | bytes 4718592 | tf_op jit(solution)/shard_map/all_to_all | solution.py:95
  500.5 40.7 %all-to-all-start.7 = ((bf16[4,48,2688]{2,1,0:T(8,128)(2,1)}), bf16[4,48,2688]{2,1,0:T(8,128)(2,1)S(1)}, u32[]{:S(2)}, u32[]{:S(2)}) async-start(bf16[4,48,2688]{2,1,0:T(8,128)(2,1)} %add_convert_fusion), calls=%async_computation.7 | async-start | bytes 2064384 | tf_op jit(solution)/shard_map/all_to_all | solution.py:95
  507.5 32.5 %collective-permute-start.25 = (bf16[4,48,1920]{2,1,0:T(8,128)(2,1)}, bf16[4,48,1920]{2,1,0:T(8,128)(2,1)S(1)}, u32[]{:S(2)}, u32[]{:S(2)}) collective-permute-start(bf16[4,48,1920]{2,1,0:T(8,128)(2,1)} %get-tuple-element.195), channel_id=1, source_target_pairs={{0,12},{4,8},{8,4},{12,0},{1,13},{5,9},{9,5},{13,1},{2,14},{6,10},... | collective-permute-start | bytes 2211848 | tf_op jit(solution)/shard_map/ppermute | solution.py:87
  541.2 22.9 %all-to-all-start.8 = ((bf16[4,48,1920]{2,1,0:T(8,128)(2,1)}), bf16[4,48,1920]{2,1,0:T(8,128)(2,1)}, u32[]{:S(2)}, u32[]{:S(2)}) async-start(bf16[4,48,1920]{2,1,0:T(8,128)(2,1)} %add_convert_fusion.1), calls=%async_computation.8 | async-start | bytes 1474560 | tf_op jit(solution)/shard_map/all_to_all | solution.py:95
  545.5 22.2 %collective-permute-start.26 = (bf16[4,48,1280]{2,1,0:T(8,128)(2,1)}, bf16[4,48,1280]{2,1,0:T(8,128)(2,1)}, u32[]{:S(2)}, u32[]{:S(2)}) collective-permute-start(bf16[4,48,1280]{2,1,0:T(8,128)(2,1)} %get-tuple-element.197), channel_id=1, source_target_pairs={{0,4},{4,0},{8,12},{12,8},{1,5},{5,1},{9,13},{13,9},{2,6},{6,2},{1... | collective-permute-start | bytes 1474568 | tf_op jit(solution)/shard_map/ppermute | solution.py:87
  546.4 21.2 %collective-permute-start.27 = (bf16[4,48,1280]{2,1,0:T(8,128)(2,1)}, bf16[4,48,1280]{2,1,0:T(8,128)(2,1)}, u32[]{:S(2)}, u32[]{:S(2)}) collective-permute-start(bf16[4,48,1280]{2,1,0:T(8,128)(2,1)} %get-tuple-element.198), channel_id=1, source_target_pairs={{0,8},{4,12},{8,0},{12,4},{1,9},{5,13},{9,1},{13,5},{2,10},{6,14},... | collective-permute-start | bytes 1474568 | tf_op jit(solution)/shard_map/ppermute | solution.py:87
  546.9 20.7 %collective-permute-start.28 = (bf16[4,48,1280]{2,1,0:T(8,128)(2,1)}, bf16[4,48,1280]{2,1,0:T(8,128)(2,1)}, u32[]{:S(2)}, u32[]{:S(2)}) collective-permute-start(bf16[4,48,1280]{2,1,0:T(8,128)(2,1)} %get-tuple-element.199), channel_id=1, source_target_pairs={{0,12},{4,8},{8,4},{12,0},{1,13},{5,9},{9,5},{13,1},{2,14},{6,10},... | collective-permute-start | bytes 1474568 | tf_op jit(solution)/shard_map/ppermute | solution.py:87
  564.1 23.1 %all-to-all-start.5 = ((bf16[1,4,128,768]{3,2,0,1:T(8,128)(2,1)}), bf16[1,4,128,768]{3,2,0,1:T(8,128)(2,1)S(1)}, u32[]{:S(2)}, u32[]{:S(2)}) async-start(bf16[1,4,128,768]{3,2,0,1:T(8,128)(2,1)} %bitcast.150), calls=%async_computation.5 | async-start | bytes 1572864 | tf_op jit(solution)/shard_map/all_to_all | solution.py:95
  573.0 38.7 %collective-permute-start.33 = (bf16[48,1536]{1,0:T(8,128)(2,1)}, bf16[48,1536]{1,0:T(8,128)(2,1)}, u32[]{:S(2)}, u32[]{:S(2)}) collective-permute-start(bf16[48,1536]{1,0:T(8,128)(2,1)} %broadcast_select_fusion.7), channel_id=1, source_target_pairs={{0,16},{16,0},{1,17},{17,1},{2,18},{18,2},{3,19},{19,3},{4,20},{20... | collective-permute-start | bytes 442376 | tf_op jit(solution)/shard_map/ppermute | solution.py:83
  593.1 20.5 %collective-permute-start.34 = (bf16[192,384]{1,0:T(8,128)(2,1)}, bf16[192,384]{1,0:T(8,128)(2,1)}, u32[]{:S(2)}, u32[]{:S(2)}) collective-permute-start(bf16[192,384]{1,0:T(8,128)(2,1)} %broadcast_select_fusion.5), channel_id=1, source_target_pairs={{0,16},{16,0},{1,17},{17,1},{2,18},{18,2},{3,19},{19,3},{4,20},{20... | collective-permute-start | bytes 442376 | tf_op jit(solution)/shard_map/ppermute | solution.py:83
  597.5 19.6 %collective-permute-start.30 = (bf16[4,128,768]{2,1,0:T(8,128)(2,1)}, bf16[4,128,768]{2,1,0:T(8,128)(2,1)}, u32[]{:S(2)}, u32[]{:S(2)}) collective-permute-start(bf16[4,128,768]{2,1,0:T(8,128)(2,1)} %get-tuple-element.242), channel_id=1, source_target_pairs={{0,16},{16,0},{1,17},{17,1},{2,18},{18,2},{3,19},{19,3},{4,20},{20... | collective-permute-start | bytes 2359304 | tf_op jit(solution)/shard_map/ppermute | solution.py:83
  597.5 19.6 %collective-permute-start.29 = (bf16[4,128,768]{2,1,0:T(8,128)(2,1)}, bf16[4,128,768]{2,1,0:T(8,128)(2,1)}, u32[]{:S(2)}, u32[]{:S(2)}) collective-permute-start(bf16[4,128,768]{2,1,0:T(8,128)(2,1)} %get-tuple-element.243), channel_id=1, source_target_pairs={{0,16},{16,0},{1,17},{17,1},{2,18},{18,2},{3,19},{19,3},{4,20},{20... | collective-permute-start | bytes 2359304 | tf_op jit(solution)/shard_map/ppermute | solution.py:83
  (40 other events, 508.9 us)
Sparse Core Ops, SparseCore 0:
  35.6 85.9 all-gather.2
  124.9 105.8 all-gather.4
  356.1 166.6 reduce-scatter.3

commit v3 on v2

--- a/solution.py
+++ b/solution.py
@@ -554,7 +554,7 @@
 
 def ffn_back_kernel(relative, meta, c_ref, slope_ref, u2_ref, gains_ref, *refs):
     attn_refs, ffn_refs, rest = split_refs(refs, (2, 2, len(refs) - 4))
-    cf_ref, dhp_ref, du2_ref, dz_ref, do_ref, dg_ref, wo, w1, w2, sems, acc = rest
+    cf_ref, dhp_ref, du2_ref, dz_ref, do_ref, dg_ref, send_ref, wo, w1, w2, sems, acc = rest
     out, first, second = layer_loads(meta, relative, attn_refs, ffn_refs, wo, w1, w2, sems)
     chunk = dhp_ref.shape[1]
     i = pl.program_id(0)
@@ -574,6 +574,12 @@
     dh = nt(cf_ref[...], tall_chunk(w2, i))
     dhp = (dh * slope_ref[...].astype(F32)).astype(BF16)
     dhp_ref[...] = dhp
+    there = 1 - meta[0]
+    steps = pl.num_programs(0) // 2
+
+    @pl.when(i // steps == there)
+    def _():
+        send_ref[:, pl.ds(pl.multiple_of((i % steps) * chunk, 128), chunk)] = dhp
     acc[...] += nt(dhp, flat(w1[:, :, at]))
 
     @pl.when(i == pl.num_programs(0) - 1)
@@ -585,6 +591,10 @@
         dz = du2.astype(BF16)
         dz_ref[...] = dz
         do_ref[...] = nt(dz, flat(wo[...])).astype(BF16)
+        half = dz.shape[1] // 2
+        begin = send_ref.shape[1] - 2 * half
+        send_ref[:, begin : begin + half] = dz_ref[:, side(there, half)]
+        send_ref[:, begin + half :] = cf_ref[:, side(there, half)]
 
 
 def ffn_backward(plan, c, slope, u2, gains, attn, ffn):
@@ -605,10 +615,11 @@
             wide,
             wide,
             jax.ShapeDtypeStruct((1, width), F32),
+            jax.ShapeDtypeStruct((rows, hidden // 2 + width), BF16),
         ],
         grid=(hidden // chunk,),
         in_specs=[smem(), full, columns, full, whole((8, width))] + [anywhere()] * len(refs),
-        out_specs=[full, columns, full, full, full, whole((1, width))],
+        out_specs=[full, columns, full, full, full, whole((1, width)), whole((rows, hidden // 2 + width))],
         scratch_shapes=[
             *layer_scratch(plan),
             pltpu.VMEM((rows, width), F32),
@@ -704,8 +715,8 @@
 def qkv_back_kernel(
     spread, n_far, meta, dq_ref, dk_ref, dv_ref, du2_ref, x_ref, gains_ref, cos_ref, sin_ref, *refs
 ):
-    far, attn_refs, rest = split_refs(refs, (n_far, len(refs) - n_far - 7, 7))
-    dqkv_ref, dx_ref, low_ref, dg_ref, wqk, wv, sems = rest
+    far, attn_refs, rest = split_refs(refs, (n_far, len(refs) - n_far - 8, 8))
+    dqkv_ref, dx_ref, low_ref, dg_ref, send_ref, wqk, wv, sems = rest
     qk = load_halves(meta, spread, attn_refs, wqk, 0, sems, 0)
     v = load_one(meta, spread, attn_refs, wv, wv.shape[-1], sems, 8, 0)
     first = pl.program_id(0) == 0
@@ -744,6 +755,10 @@
     dx_ref[...] = dx
     low_ref[...] = dx.astype(BF16)
     dg_ref[...] += dgain
+    there = 1 - meta[0]
+    wide = 3 * width // 2
+    send_ref[:, :wide] = dqkv_ref[:, side(there, wide)]
+    send_ref[:, wide:] = low_ref[:, side(there, width // 2)]
 
 
 def qkv_backward(plan, dq, dk, dv, far, du2, x, gains, cos, sin, attn):
@@ -758,6 +773,7 @@
             jax.ShapeDtypeStruct((rows, width), F32),
             jax.ShapeDtypeStruct((rows, width), BF16),
             jax.ShapeDtypeStruct((1, width), F32),
+            jax.ShapeDtypeStruct((rows, 2 * width), BF16),
         ],
         grid=(rows // step,),
         in_specs=[smem()]
@@ -765,7 +781,7 @@
         + [whole((8, width)), rows_of(step, PAIR), rows_of(step, PAIR)]
         + [pl.BlockSpec((2, step, width), lambda i: (0, i, 0))] * len(far)
         + [anywhere()] * len(refs),
-        out_specs=[rows_of(step, 3 * width), some, some, whole((1, width))],
+        out_specs=[rows_of(step, 3 * width), some, some, whole((1, width)), rows_of(step, 2 * width)],
         scratch_shapes=[
             pltpu.VMEM((plan.shards, plan.shard_rows, 2 * width), BF16),
             pltpu.VMEM((plan.shards, plan.shard_rows, width), BF16),
@@ -778,38 +794,26 @@
 
 
 class Job:
-    def __init__(self, left, right, start, cols, tall=False):
-        self.left, self.right, self.start, self.cols, self.tall = left, right, start, cols, tall
+    def __init__(self, left, right, cols, at=0, tall=False):
+        self.left, self.right, self.cols, self.at, self.tall = left, right, cols, at, tall
         self.lanes = 4 * cols if tall else cols
-        self.given = right is None
-
-
-def weight_kernel(jobs, n_lefts, n_rights, mine, relative, meta, *refs):
-    n_got = 1 if mine else 0
-    lefts, rights, got, outs, (acc,) = split_refs(
-        refs, (n_lefts, n_rights, n_got, len(refs) - n_lefts - n_rights - n_got - 1, 1)
+
+
+def weight_kernel(jobs, n_lefts, n_rights, relative, meta, *refs):
+    lefts, rights, (got,), outs, (acc,) = split_refs(
+        refs, (n_lefts, n_rights, 1, len(refs) - n_lefts - n_rights - 2, 1)
     )
     step = pl.program_id(0)
-    which = meta[0] if mine else 1 - meta[0]
-    block = (meta[1] ^ step) if relative else step
-
     shards, size = acc.shape[:2]
     lane = 0
     for job in jobs:
-        left = lefts[job.left]
-        if job.given:
-            count = shards * size
-            rows = left[pl.ds(pl.multiple_of(block * count, 16), count), :]
-            acc[:, :, lane : lane + job.cols] = rows.reshape(shards, size, job.cols)
-            lane += job.cols
-            continue
-        right = rights[job.right]
-        half = right.shape[1] // 2
-        columns = right[:, side(which, half)] if job.cols == half else right[
-            :, pl.ds(pl.multiple_of(which * half + job.start, 128), job.cols)
-        ]
-        count = shards * size * (4 if job.tall else 1)
-        product = nn(left[pl.ds(pl.multiple_of(block * count, 16), count), :], columns)
+        own, other = lefts[job.left], lefts[job.left + 1]
+        if job.right is None:
+            product = own[...] + other[...]
+        else:
+            columns = rights[job.right][:, side(meta[0], rights[job.right].shape[1] // 2)]
+            product = nn(own[...], columns)
+            product = product + nn(other[...], got[:, job.at : job.at + job.cols])
         if job.tall:
             product = product.reshape(shards, 4, size, job.cols)
             for quarter in range(4):
@@ -818,74 +822,71 @@
         else:
             acc[:, :, lane : lane + job.cols] = product.reshape(shards, size, job.cols)
             lane += job.cols
-    if not mine:
+    if not relative:
         outs[0][0] = acc[...].astype(BF16)
-    elif len(outs) == 1:
-        outs[0][0] = (acc[...] + got[0][0].astype(F32)).astype(BF16)
-    else:
-        for mask, out in enumerate(outs):
-
-            @pl.when(step == mask)
-            def _(out=out):
-                out[...] = (acc[...] + got[0][0].astype(F32)).astype(BF16)
+        return
+    for mask, out in enumerate(outs):
+
+        @pl.when(step == mask)
+        def _(out=out):
+            out[...] = acc[...].astype(BF16)
 
 
 def weight_call(plan, lefts, rights, jobs, got, relative):
-    rows = lefts[0].shape[1]
+    rows = rights[0].shape[0]
     n = plan.blocks
-    mine = got is not None
     shape = (plan.shards // n, plan.shard_rows, sum(job.lanes for job in jobs))
-    block = pl.BlockSpec((1, *shape), lambda i: (i, 0, 0, 0))
-    if mine and relative:
+    if relative:
         out_shape = [jax.ShapeDtypeStruct(shape, BF16)] * n
-        out_specs = [whole(shape)] * n
+        out_specs = [pl.BlockSpec(shape, lambda i, meta: (0, 0, 0))] * n
     else:
         out_shape = [jax.ShapeDtypeStruct((n, *shape), BF16)]
-        out_specs = [block]
-    flops = sum(2 * rows * lefts[job.left].shape[0] * job.cols for job in jobs if not job.given)
-    moved = sum(value.size * 2 for value in [*lefts, *rights])
-    moved += 2 * n * shape[0] * shape[1] * shape[2] * (2 if mine else 1)
+        out_specs = [pl.BlockSpec((1, *shape), lambda i, meta: (i, 0, 0, 0))]
+
+    def block_of(i, meta):
+        return (meta[1] ^ i if relative else i, 0)
+
+    def all_of(value):
+        return pl.BlockSpec(value.shape, lambda i, meta: (0, 0))
+
+    moved = sum(value.size * 2 for value in [*lefts, *rights, got])
+    moved += 2 * n * shape[0] * shape[1] * shape[2]
+    flops = sum(
+        4 * rows * lefts[job.left].shape[0] * job.cols for job in jobs if job.right is not None
+    )
     result = pl.pallas_call(
-        functools.partial(weight_kernel, jobs, len(lefts), len(rights), mine, relative),
+        functools.partial(weight_kernel, jobs, len(lefts), len(rights), relative),
         out_shape=out_shape,
-        grid=(n,),
-        in_specs=[smem()]
-        + [whole(value.shape) for value in [*lefts, *rights]]
-        + ([block] if mine else []),
-        out_specs=out_specs,
-        scratch_shapes=[pltpu.VMEM(shape, F32)],
+        grid_spec=pltpu.PrefetchScalarGridSpec(
+            num_scalar_prefetch=1,
+            grid=(n,),
+            in_specs=[
+                pl.BlockSpec((value.shape[0] // n, value.shape[1]), block_of) for value in lefts
+            ]
+            + [all_of(value) for value in [*rights, got]],
+            out_specs=out_specs,
+            scratch_shapes=[pltpu.VMEM(shape, F32)],
+        ),
         compiler_params=params(56),
         cost_estimate=cost(flops, moved),
-        name="weight_mine" if mine else "weight_theirs",
-    )(plan.meta, *lefts, *rights, *([got] if mine else []))
-    return result if mine and relative else result[0]
+        name="weight_grads",
+    )(plan.meta, *lefts, *rights, got)
+    return result if relative else result[0]
 
 
 class WeightGrads:
-    def __init__(self, plan, lefts, rights, jobs, relative):
-        self.plan, self.lefts, self.rights, self.jobs = plan, lefts, rights, jobs
-        self.relative = relative and plan.staged
-
-    def theirs(self, order):
-        lefts = [order.gate(self.lefts[0]), *self.lefts[1:]]
-        out = weight_call(self.plan, lefts, self.rights, self.jobs, None, self.relative)
-        order.mark(out)
-        self.got = other_core(out)
-
-    def mine(self, order):
-        plan = self.plan
-        lefts = [order.gate(self.lefts[0]), *self.lefts[1:]]
-        out = weight_call(plan, lefts, self.rights, self.jobs, self.got, self.relative)
+    def __init__(self, plan, order, lefts, rights, jobs, got, ahead=None):
+        self.plan, self.relative = plan, plan.staged
+        lefts = [order.gate(lefts[0]), *lefts[1:]]
+        out = weight_call(plan, lefts, rights, jobs, got, self.relative)
         if self.relative:
             order.mark(out[0])
-            self.sums = Collect(plan, out)
+            earlier = ahead.sums.blocks[1:] if ahead else []
+            self.sums = Collect(plan, [after(block, *earlier) for block in out])
             return
         order.mark(out)
-        tall = sum(job.lanes for job in self.jobs if job.tall)
+        tall = sum(job.lanes for job in jobs if job.tall)
         out = out.reshape(plan.width, -1)
-        if plan.staged:
-            self.total = lax.psum_scatter(out, ("dp", "ctx"), scatter_dimension=0, tiled=True)
-            return
         cut = out.shape[1] - tall
         self.total = lax.psum_scatter(out[:, :cut], ("dp", "ctx"), scatter_dimension=0, tiled=True)
         if tall:
@@ -1040,7 +1041,7 @@
     bias = jnp.where(lane[None, :] == 0, hidden_key[:, None], 0.0).astype(BF16)
 
     order = Order()
-    saved, acts, gains = [], [], []
+    saved, acts, gains, others = [], [], [], []
 
     def forward_qkv(x, attn):
         a, query, own_kv, rows = qkv_forward(plan, order.gate(x), cos, sin, attn)
@@ -1061,8 +1062,11 @@
         order.mark(low)
         saved.append((x, a, query, kv, o, ot, lse, u2, b, h, slope))
         acts.append(low)
+        others.append([other_core(value) for value in (a, ot, b, h)])
         return result
 
+    if plan.staged:
+        order.need(*ffn0_dp.got[:2])
     held = forward_qkv(source, attn0)
     held += tuple(forward_attention(*held[1:]))
     if plan.staged:
@@ -1071,8 +1075,8 @@
     attn1.share(held[5])
     x = forward_ffn(source, 0, attn0, ffn0, held)
     held = forward_qkv(x, attn1)
-    ffn1.share(held[1])
     held += tuple(forward_attention(*held[1:]))
+    ffn1.share(held[5])
     cotangent = to_sequences(plan, after(upstream, held[1]))
     forward_ffn(x, 1, attn1, ffn1, held)
     weights = [(attn0, ffn0), (attn1, ffn1)]
@@ -1084,7 +1088,7 @@
         attn, ffn = weights[layer]
         u2, _, _, slope = saved[layer][7:]
         out = ffn_backward(plan, order.gate(c), slope, u2, gains[layer], attn, ffn)
-        order.mark(out[-1])
+        order.mark(out[5])
         return out
 
     def attention_part(layer, do):
@@ -1095,66 +1099,88 @@
 
     def qkv_part(layer, dq, dk, dv, far, du2, dg2):
         x = saved[layer][0]
-        dqkv, dx, low, dg1 = qkv_backward(
+        dqkv, dx, low, dg1, send = qkv_backward(
             plan, order.gate(dq), dk, dv, far, du2, x, gains[layer], cos, sin, weights[layer][0]
         )
         order.mark(dg1)
         grads[layer] = low
         dgains[layer] = (dg1, dg2)
-        return dqkv, dx, low
-
-    def job_in(left, right):
-        return Job(left, right, 0, hidden_half)
-
-    def job_out(left, right):
-        return Job(left, right, 0, width_half)
-
-    def job_back(left, right):
-        return Job(left, right, 0, width_half, tall=True)
-
-    def job_qkv(left, right):
-        return Job(left, right, 0, 3 * width // 2)
-
+        return dqkv, dx, low, send
+
+    wide = 3 * width // 2
     a1, ot1, b1, h1 = (saved[1][i] for i in (1, 5, 8, 9))
     a0, ot0, b0, h0 = (saved[0][i] for i in (1, 5, 8, 9))
-
-    cf, dhp, du2, dz, do, dg2 = ffn_part(1, cotangent)
+    (far_a0, far_ot0, far_b0, far_h0), (far_a1, far_ot1, far_b1, far_h1) = others
+
+    cf, dhp, du2, dz, do, dg2, send = ffn_part(1, cotangent)
+    got = other_core(send)
+    acts_back = from_sequences(plan, jnp.stack(acts))
+    back = attention_part(1, do)
     sum_ffn1 = WeightGrads(
-        plan, [b1, ot1, h1], [dhp, dz, cf], [job_in(0, 0), job_out(1, 1), job_back(2, 2)], False
+        plan,
+        order,
+        [b1, far_b1, ot1, far_ot1, h1, far_h1],
+        [dhp, dz, cf],
+        [
+            Job(0, 0, hidden_half),
+            Job(2, 1, width_half, hidden_half),
+            Job(4, 2, width_half, hidden_half + width_half, tall=True),
+        ],
+        got,
     )
-    sum_ffn1.theirs(order)
-    back = attention_part(1, do)
-    sum_ffn1.mine(order)
-    dqkv, c, low = qkv_part(1, *back, du2, dg2)
-    early = from_sequences(plan, jnp.stack([acts[0], acts[1], grads[1]]))
-    sum_mixed = WeightGrads(plan, [a1, h0], [dqkv, low], [job_qkv(0, 0), job_back(1, 1)], True)
-    sum_mixed.theirs(order)
-    sum_mixed.mine(order)
-    cf, dhp, du2, dz, do, dg2 = ffn_part(0, c)
-    sum_in0 = WeightGrads(plan, [b0, ot0], [dhp, dz], [job_in(0, 0), job_out(1, 1)], True)
-    sum_in0.theirs(order)
-    sum_in0.mine(order)
+    order.need(acts_back)
+    dqkv, c, low, send = qkv_part(1, *back, du2, dg2)
+    got = other_core(send)
+    grads1_back = from_sequences(plan, grads[1][None])
+    cf, dhp, du2, dz, do, dg2, send = ffn_part(0, c)
+    got_ffn = other_core(send)
+    sum_ffn1.step("first", order)
+    order.need(grads1_back)
+    sum_ffn1.step("second", order)
+    sum_mixed = WeightGrads(
+        plan,
+        order,
+        [a1, far_a1, h0, far_h0],
+        [dqkv, low],
+        [Job(0, 0, wide), Job(2, 1, width_half, wide, tall=True)],
+        got,
+    )
+    sum_in0 = WeightGrads(
+        plan,
+        order,
+        [b0, far_b0, ot0, far_ot0],
+        [dhp, dz],
+        [Job(0, 0, hidden_half), Job(2, 1, width_half, hidden_half)],
+        got_ffn,
+        sum_mixed,
+    )
+    back = attention_part(0, do)
     sum_mixed.step("first", order)
     sum_mixed.step("second", order)
-    back = attention_part(0, do)
-    dqkv, c, low = qkv_part(0, *back, du2, dg2)
+    dqkv, c, low, send = qkv_part(0, *back, du2, dg2)
+    got = other_core(send)
     rows = jnp.concatenate([row for pair in dgains for row in pair], axis=0)
     columns = jnp.pad(rows.T, ((0, 0), (0, GAIN_LANES - 2 * layers)))
+    sum_in0.step("first", order)
     sum_qkv0 = WeightGrads(
-        plan, [a0, columns], [dqkv], [job_qkv(0, 0), Job(1, None, 0, GAIN_LANES)], True
+        plan,
+        order,
+        [a0, far_a0, columns, other_core(columns)],
+        [dqkv],
+        [Job(0, 0, wide), Job(2, None, GAIN_LANES)],
+        got,
     )
-    sum_qkv0.theirs(order)
-    sum_qkv0.mine(order)
-    late = from_sequences(plan, order.gate(grads[0])[None])
     sum_in0.step("second", order)
+    grads0_back = from_sequences(plan, order.gate(grads[0])[None])
+    acts_back = arranged(plan, acts_back, *order.earlier)
+    acts_out = to_output(plan, acts_back)
     sum_qkv0.step("second", order)
-    early = arranged(plan, early, *order.earlier)
-    late = arranged(plan, late, *order.earlier)
+    grads0_back = arranged(plan, grads0_back, *order.earlier)
+    grads1_back = arranged(plan, grads1_back, *order.earlier)
 
     cut = hidden_half + width_half
     ffn1_sum, mixed_sum = sum_ffn1.result(), sum_mixed.result()
     in0_sum, qkv0_sum = sum_in0.result(), sum_qkv0.result()
-    wide = 3 * width // 2
     gain_sums = lax.dynamic_slice_in_dim(qkv0_sum[:, wide:], plan.section * 2, 2, axis=1).T.astype(F32)
     sums = [
         (qkv0_sum[:, :wide], in0_sum[:, hidden_half:], in0_sum[:, :hidden_half], from_lanes(mixed_sum[:, wide:])),
@@ -1174,8 +1200,8 @@
 
     weight_grads = [to_owner(one, two) for one, two in zip(*sums)]
     return (
-        to_output(plan, early[:2]),
-        to_output(plan, [late[0], early[2]]),
+        acts_out,
+        to_output(plan, [grads0_back[0], grads1_back[0]]),
         *weight_grads,
         gain_sums[0:1],
         gain_sums[1:2],

time: 635 us -> 593 us (0.934)
  waiting for transfers between devices: 239 us -> 192 us
  starting transfers between devices: 65.8 us -> 84.2 us
  Pallas kernels: 239 us -> 228 us
    ppermute x15 -> x18, waiting for transfers between devices: 108 us -> 68.5 us  [xor_dp(): return lax.ppermute(value, 'dp', [(i, i ^ mask) for i in range(plan.n_dp)])]
    pallas_call x8 -> x4, Pallas kernels: 62.6 us -> 45.8 us  [weight_call(): pl.pallas_call(functools.partial(weight_kernel, jobs, len(lefts), len(rig...]
    ppermute x20 -> x29, waiting for transfers between devices: 28.2 us -> 17.9 us  [other_core(): return lax.ppermute(value, 'section', [(0, 1), (1, 0)])]
    all_to_all x9 -> x11, starting transfers between devices: 37.2 us -> 45.9 us  [exchange_ctx(): return lax.all_to_all(value, 'ctx', dim, dim, tiled=True)]
    ppermute x20 -> x29, starting transfers between devices: 15 us -> 21.8 us  [other_core(): return lax.ppermute(value, 'section', [(0, 1), (1, 0)])]
    convert_element_type x3 -> x4, other arithmetic: 6.75 us -> 12.9 us  [second(): sum((value.astype(F32) for value in [own, *self.blocks[1:]])).astype(BF16)]
    ppermute x15 -> x18, starting transfers between devices: 13.4 us -> 16.4 us  [xor_dp(): return lax.ppermute(value, 'dp', [(i, i ^ mask) for i in range(plan.n_dp)])]
    all_to_all x9 -> x11, waiting for transfers between devices: 103 us -> 102 us  [exchange_ctx(): return lax.all_to_all(value, 'ctx', dim, dim, tiled=True)]
  transfers between devices with their start and end apart: 47 -> 60, of which waited for: 21 -> 22; matrix products, arithmetic and copies ran while one was open for 8% -> 9% of each run, Pallas kernels for 31% -> 39%
where the time goes in v3:
time: 593 us; the launch traced here: 587 us
  Pallas kernels  228 us (38%)
  waiting for transfers between devices  192 us (32%)
  starting transfers between devices  84.2 us (14%)
  other arithmetic  50.3 us (8%)
  local copies, waits for them, and re-layouts  18 us (3%)
  between operations  14.9 us (3%)
    all_to_all x11, waiting for transfers between devices, exchange_ctx(): return lax.all_to_all(value, 'ctx', dim, dim, tiled=True)  102 us
    ppermute x18, waiting for transfers between devices, xor_dp(): return lax.ppermute(value, 'dp', [(i, i ^ mask) for i in range(plan.n_dp)])  68.5 us
    all_to_all x11, starting transfers between devices, exchange_ctx(): return lax.all_to_all(value, 'ctx', dim, dim, tiled=True)  45.9 us
    pallas_call x4, Pallas kernels, weight_call(): pl.pallas_call(functools.partial(weight_kernel, jobs, len(lefts), len(rig...  45.8 us
    pallas_call x2, Pallas kernels, attention_backward(): pl.pallas_call(functools.partial(attention_back_kernel, chunks, min(256,...  41.2 us
    pallas_call x2, Pallas kernels, ffn_backward(): pl.pallas_call(functools.partial(ffn_back_kernel, relative), out_shape=[w...  39.5 us
    pallas_call x2, Pallas kernels, ffn_forward(): pl.pallas_call(functools.partial(ffn_kernel, relative), out_shape=[jax.Sh...  32.9 us
    pallas_call x2, Pallas kernels, attention_forward(): pl.pallas_call(functools.partial(attention_kernel, chunks, min(256, rows)...  28.2 us
  transfers between devices with their start and end apart: 60, of which 22 were waited for; matrix products, arithmetic and copies ran while one was open for 9% of the time, Pallas kernels for 39%

profile of v3, /device:TPU:1, one launch (start us, length us, event | category | flops | bytes accessed | tf_op | source)
XLA Modules:
  0.0 587.3 jit_solution(15412414879281351826)
XLA Ops:
  13.2 5.7 all-to-all-start
  19.8 15.6 %all-to-all-done = bf16[4,48,1664]{2,1,0:T(8,128)(2,1)S(1)} async-done(((bf16[4,48,1664]{2,1,0:T(8,128)(2,1)}), bf16[4,48,1664]{2,1,0:T(8,128)(2,1)S(1)}, u32[]{:S(2)}, u32[]{:S(2)}) %all-to-all-start) | async-done | bytes 639008 | tf_op jit(solution)/shard_map/all_to_all | solution.py:95
  43.7 28.8 %all-to-all-done.1 = bf16[4,48,3072]{2,1,0:T(8,128)(2,1)S(1)} async-done(((bf16[4,48,3072]{2,1,0:T(8,128)(2,1)}), bf16[4,48,3072]{2,1,0:T(8,128)(2,1)S(1)}, u32[]{:S(2)}, u32[]{:S(2)}) %all-to-all-start.1) | async-done | bytes 1179680 | tf_op jit(solution)/shard_map/all_to_all | solution.py:95
  87.4 23.6 %all-to-all-done.2 = bf16[4,128,768]{2,1,0:T(8,128)(2,1)S(1)} async-done(((bf16[4,128,768]{2,1,0:T(8,128)(2,1)}), bf16[4,128,768]{2,1,0:T(8,128)(2,1)S(1)}, u32[]{:S(2)}, u32[]{:S(2)}) %all-to-all-start.2) | async-done | bytes 786464 | tf_op jit(solution)/shard_map/all_to_all | solution.py:95
  111.0 8.4 %collective-permute-done.5 = bf16[192,3072]{1,0:T(8,128)(2,1)S(1)} collective-permute-done((bf16[192,3072]{1,0:T(8,128)(2,1)S(1)}, bf16[192,3072]{1,0:T(8,128)(2,1)S(1)}, u32[]{:S(2)}, u32[]{:S(2)}) %collective-permute-start.5) | collective-permute-done | bytes 1179680 | tf_op jit(solution)/shard_map/ppermute | solution.py:87
  120.1 8.0 %qkv_forward.2 = (bf16[768,512]{1,0:T(8,128)(2,1)}, bf16[512,768]{1,0:T(8,128)(2,1)}, bf16[2,512,768]{2,1,0:T(8,128)(2,1)}, f32[8,768]{1,0:T(8,128)}) custom-call(s32[2]{0:T(128)} %pad_add_fusion.meta, bf16[512,768]{1,0:T(8,128)(2,1)} %bitcast.135, f32[512,128]{1,0:T(8,128)} %get-tuple-element.304.cos_ref, f32[512,128]{1,0:T(8,128)} %get-tuple-element.305.sin_ref, ...), custom_call_target="tpu_custom_call" | custom-call | flops 181193936 | bytes 825753 | tf_op jit(solution)/shard_map/qkv_forward/pallas_call | solution.py:355
  134.5 14.1 %attention_forward.2 = (bf16[512,768]{1,0:T(8,128)(2,1)}, bf16[768,512]{1,0:T(8,128)(2,1)}, f32[6,8,512]{2,1,0:T(8,128)}) custom-call(bf16[512,768]{1,0:T(8,128)(2,1)} %get-tuple-element.124.q_ref, bf16[2,512,768]{2,1,0:T(8,128)(2,1)} %get-tuple-element.125.refs_0_, bf16[2,512,768]{2,1,0:T(8,128)(2,1)} %copy-done.7, ...), custom_call_target="tpu_custom_call" | custom-call | flops 644245120 | bytes 471859 | tf_op jit(solution)/shard_map/attention_forward/pallas_call | solution.py:436
  148.6 11.6 %collective-permute-done.9 = bf16[192,3072]{1,0:T(8,128)(2,1)} collective-permute-done((bf16[192,3072]{1,0:T(8,128)(2,1)S(1)}, bf16[192,3072]{1,0:T(8,128)(2,1)}, u32[]{:S(2)}, u32[]{:S(2)}) %collective-permute-start.9) | collective-permute-done | bytes 1179680 | tf_op jit(solution)/shard_map/ppermute | solution.py:87
  164.8 11.5 %collective-permute-done.10.refs_3_ = bf16[16,48,3072]{2,1,0:T(8,128)(2,1)} collective-permute-done((bf16[16,48,3072]{2,1,0:T(8,128)(2,1)}, bf16[16,48,3072]{2,1,0:T(8,128)(2,1)}, u32[]{:S(2)}, u32[]{:S(2)}) %collective-permute-start.10) | collective-permute-done | bytes 4718624 | tf_op jit(solution)/shard_map/ppermute | solution.py:83
  176.2 16.3 %ffn_forward.2 = (f32[512,768]{1,0:T(8,128)}, bf16[768,512]{1,0:T(8,128)(2,1)}, f32[512,768]{1,0:T(8,128)}, bf16[512,768]{1,0:T(8,128)(2,1)}, bf16[3072,512]{1,0:T(8,128)(2,1)}, /*index=5*/bf16[512,3072]{1,0:T(8,128)(2,1)}) custom-call(s32[2]{0:T(128)} %pad_add_fusion.meta, bf16[512,768]{1,0:T(8,128)(2,1)} %get-tuple-element.128.o_ref, ...), custom_call_target="tpu_custom_call" | custom-call | flops 553019008 | bytes 2359296 | tf_op jit(solution)/shard_map/ffn_forward/pallas_call | solution.py:526
  194.1 8.2 %qkv_forward.3 = (bf16[768,512]{1,0:T(8,128)(2,1)}, bf16[512,768]{1,0:T(8,128)(2,1)}, bf16[2,512,768]{2,1,0:T(8,128)(2,1)}, f32[8,768]{1,0:T(8,128)}) custom-call(s32[2]{0:T(128)} %pad_add_fusion.meta, f32[512,768]{1,0:T(8,128)} %get-tuple-element.134.x_ref, f32[512,128]{1,0:T(8,128)} %get-tuple-element.304.cos_ref, f32[512,128]{1,0:T(8,128)} %get-tuple-element.305.sin_ref, ...), custom_call_target="tpu_custom_call" | custom-call | flops 181193936 | bytes 825753 | tf_op jit(solution)/shard_map/qkv_forward/pallas_call | solution.py:355
  207.1 14.1 %attention_forward.3 = (bf16[512,768]{1,0:T(8,128)(2,1)}, bf16[768,512]{1,0:T(8,128)(2,1)}, f32[6,8,512]{2,1,0:T(8,128)}) custom-call(bf16[512,768]{1,0:T(8,128)(2,1)} %get-tuple-element.138.q_ref, bf16[2,512,768]{2,1,0:T(8,128)(2,1)} %get-tuple-element.139.refs_0_, bf16[2,512,768]{2,1,0:T(8,128)(2,1)} %copy-done.8, ...), custom_call_target="tpu_custom_call" | custom-call | flops 644245120 | bytes 471859 | tf_op jit(solution)/shard_map/attention_forward/pallas_call | solution.py:436
  233.9 16.6 %ffn_forward.3 = (f32[512,768]{1,0:T(8,128)}, bf16[768,512]{1,0:T(8,128)(2,1)}, f32[512,768]{1,0:T(8,128)}, bf16[512,768]{1,0:T(8,128)(2,1)}, bf16[3072,512]{1,0:T(8,128)(2,1)}, /*index=5*/bf16[512,3072]{1,0:T(8,128)(2,1)}) custom-call(s32[2]{0:T(128)} %pad_add_fusion.meta, bf16[512,768]{1,0:T(8,128)(2,1)} %get-tuple-element.142.o_ref, ...), custom_call_target="tpu_custom_call" | custom-call | flops 553019008 | bytes 2359296 | tf_op jit(solution)/shard_map/ffn_forward/pallas_call | solution.py:526
  253.2 19.7 %ffn_backward.2 = (bf16[512,768]{1,0:T(8,128)(2,1)}, bf16[512,3072]{1,0:T(8,128)(2,1)}, f32[512,768]{1,0:T(8,128)}, bf16[512,768]{1,0:T(8,128)(2,1)}, bf16[512,7...) custom-call(s32[2]{0:T(128)} %pad_add_fusion.meta, bf16[512,768]{1,0:T(8,128)(2,1)} %bitcast.144, ...), custom_call_target="tpu_custom_call" | custom-call | flops 543581824 | bytes 2398617 | tf_op jit(solution)/shard_map/ffn_backward/pallas_call | solution.py:609
  279.4 20.6 %attention_backward.2 = (bf16[512,768]{1,0:T(8,128)(2,1)}, f32[512,768]{1,0:T(8,128)}, f32[512,768]{1,0:T(8,128)}, bf16[2,512,768]{2,1,0:T(8,128)(2,1)}) custom-call(bf16[512,768]{1,0:T(8,128)(2,1)} %get-tuple-element.138.q_ref, bf16[512,768]{1,0:T(8,128)(2,1)} %get-tuple-element.156.do_ref, bf16[512,768]{1,0:T(8,128)(2,1)} %get-tuple-element.142.o_ref, ...), custom_call_target="tpu_custom_call" | custom-call | flops 1610612736 | bytes 1258291 | tf_op jit(solution)/shard_map/attention_backward/pallas_call | solution.py:688
  301.3 15.1 %weight_grads.4 = (bf16[4,48,3456]{2,1,0:T(8,128)(2,1)}, bf16[4,48,3456]{2,1,0:T(8,128)(2,1)}, bf16[4,48,3456]{2,1,0:T(8,128)(2,1)}, bf16[4,48,3456]{2,1,0:T(8,128)(2,1)}) custom-call(s32[2]{0:T(128)} %pad_add_fusion.meta, bf16[768,512]{1,0:T(8,128)(2,1)} %get-tuple-element.158.refs_0_, bf16[768,512]{1,0:T(8,128)(2,1)} %copy-done.16, ...), custom_call_target="tpu_custom_call" | custom-call | flops 543581824 | bytes 2182348 | tf_op jit(solution)/shard_map/weight_grads/pallas_call | solution.py:857
  319.7 12.3 %qkv_backward.2 = (bf16[512,2304]{1,0:T(8,128)(2,1)}, f32[512,768]{1,0:T(8,128)}, bf16[512,768]{1,0:T(8,128)(2,1)}, f32[1,768]{1,0:T(1,128)}, bf16[512,1536]{1,0:T(8,128)(2,1)}) custom-call(s32[2]{0:T(128)} %pad_add_fusion.meta, bf16[512,768]{1,0:T(8,128)(2,1)} %get-tuple-element.166.dq_ref, f32[512,768]{1,0:T(8,128)} %get-tuple-element.167.dk_ref, ...), custom_call_target="tpu_custom_call" | custom-call | flops 181193936 | bytes 1533542 | tf_op jit(solution)/shard_map/qkv_backward/pallas_call | solution.py:769
  336.6 19.8 %ffn_backward.3 = (bf16[512,768]{1,0:T(8,128)(2,1)}, bf16[512,3072]{1,0:T(8,128)(2,1)}, f32[512,768]{1,0:T(8,128)}, bf16[512,768]{1,0:T(8,128)(2,1)}, bf16[512,7...) custom-call(s32[2]{0:T(128)} %pad_add_fusion.meta, f32[512,768]{1,0:T(8,128)} %get-tuple-element.173.c_ref, ...), custom_call_target="tpu_custom_call" | custom-call | flops 543581824 | bytes 2398617 | tf_op jit(solution)/shard_map/ffn_backward/pallas_call | solution.py:609
  357.6 19.6 %collective-permute-done.20 = bf16[4,48,3456]{2,1,0:T(8,128)(2,1)} collective-permute-done((bf16[4,48,3456]{2,1,0:T(8,128)(2,1)}, bf16[4,48,3456]{2,1,0:T(8,128)(2,1)}, u32[]{:S(2)}, u32[]{:S(2)}) %collective-permute-start.20) | collective-permute-done | bytes 1327136 | tf_op jit(solution)/shard_map/ppermute | solution.py:87
  382.5 12.5 %weight_grads.5 = (bf16[4,48,2688]{2,1,0:T(8,128)(2,1)}, bf16[4,48,2688]{2,1,0:T(8,128)(2,1)}, bf16[4,48,2688]{2,1,0:T(8,128)(2,1)}, bf16[4,48,2688]{2,1,0:T(8,128)(2,1)}) custom-call(s32[2]{0:T(128)} %pad_add_fusion.meta, bf16[768,512]{1,0:T(8,128)(2,1)} %get-tuple-element.182.refs_0_, bf16[768,512]{1,0:T(8,128)(2,1)} %collective-permute-done.22.refs_1_, ...), custom_call_target="tpu_custom_call" | custom-call | flops 422785856 | bytes 1671168 | tf_op jit(solution)/shard_map/weight_grads/pallas_call | solution.py:857
  398.5 10.2 %weight_grads.6 = (bf16[4,48,1920]{2,1,0:T(8,128)(2,1)}, bf16[4,48,1920]{2,1,0:T(8,128)(2,1)}, bf16[4,48,1920]{2,1,0:T(8,128)(2,1)}, bf16[4,48,1920]{2,1,0:T(8,128)(2,1)}) custom-call(s32[2]{0:T(128)} %pad_add_fusion.meta, bf16[768,512]{1,0:T(8,128)(2,1)} %get-tuple-element.187.refs_0_, bf16[768,512]{1,0:T(8,128)(2,1)} %copy-done.18, ...), custom_call_target="tpu_custom_call" | custom-call | flops 301989888 | bytes 1238630 | tf_op jit(solution)/shard_map/weight_grads/pallas_call | solution.py:857
  408.7 20.6 %attention_backward.3 = (bf16[512,768]{1,0:T(8,128)(2,1)}, f32[512,768]{1,0:T(8,128)}, f32[512,768]{1,0:T(8,128)}, bf16[2,512,768]{2,1,0:T(8,128)(2,1)}) custom-call(bf16[512,768]{1,0:T(8,128)(2,1)} %get-tuple-element.124.q_ref, bf16[512,768]{1,0:T(8,128)(2,1)} %get-tuple-element.199.do_ref, bf16[512,768]{1,0:T(8,128)(2,1)} %get-tuple-element.128.o_ref, ...), custom_call_target="tpu_custom_call" | custom-call | flops 1610612736 | bytes 1258291 | tf_op jit(solution)/shard_map/attention_backward/pallas_call | solution.py:688
  430.5 4.8 all-to-all-start.10
  435.3 7.1 %collective-permute-done.30 = bf16[4,48,2688]{2,1,0:T(8,128)(2,1)} collective-permute-done((bf16[4,48,2688]{2,1,0:T(8,128)(2,1)}, bf16[4,48,2688]{2,1,0:T(8,128)(2,1)}, u32[]{:S(2)}, u32[]{:S(2)}) %collective-permute-start.30) | collective-permute-done | bytes 1032224 | tf_op jit(solution)/shard_map/ppermute | solution.py:87
  445.8 12.2 %qkv_backward.3 = (bf16[512,2304]{1,0:T(8,128)(2,1)}, f32[512,768]{1,0:T(8,128)}, bf16[512,768]{1,0:T(8,128)(2,1)}, f32[1,768]{1,0:T(1,128)}, bf16[512,1536]{1,0:T(8,128)(2,1)}) custom-call(s32[2]{0:T(128)} %pad_add_fusion.meta, bf16[512,768]{1,0:T(8,128)(2,1)} %get-tuple-element.202.dq_ref, f32[512,768]{1,0:T(8,128)} %get-tuple-element.203.dk_ref, ...), custom_call_target="tpu_custom_call" | custom-call | flops 181193936 | bytes 1533542 | tf_op jit(solution)/shard_map/qkv_backward/pallas_call | solution.py:769
  460.7 6.1 %all-to-all-done.10 = bf16[4,48,3456]{2,1,0:T(8,128)(2,1)} async-done(((bf16[4,48,3456]{2,1,0:T(8,128)(2,1)}), bf16[4,48,3456]{2,1,0:T(8,128)(2,1)}, u32[]{:S(2)}, u32[]{:S(2)}) %all-to-all-start.10) | async-done | bytes 1327136 | tf_op jit(solution)/shard_map/all_to_all | solution.py:95
  480.1 14.9 %collective-permute-done.33 = bf16[4,48,1920]{2,1,0:T(8,128)(2,1)} collective-permute-done((bf16[4,48,1920]{2,1,0:T(8,128)(2,1)}, bf16[4,48,1920]{2,1,0:T(8,128)(2,1)}, u32[]{:S(2)}, u32[]{:S(2)}) %collective-permute-start.33) | collective-permute-done | bytes 737312 | tf_op jit(solution)/shard_map/ppermute | solution.py:87
  495.7 8.1 %weight_grads.7 = (bf16[4,48,1280]{2,1,0:T(8,128)(2,1)}, bf16[4,48,1280]{2,1,0:T(8,128)(2,1)}, bf16[4,48,1280]{2,1,0:T(8,128)(2,1)}, bf16[4,48,1280]{2,1,0:T(8,128)(2,1)}) custom-call(s32[2]{0:T(128)} %pad_add_fusion.meta, bf16[768,512]{1,0:T(8,128)(2,1)} %get-tuple-element.214.refs_0_, bf16[768,512]{1,0:T(8,128)(2,1)} %collective-permute-done.35.refs_1_, ...), custom_call_target="tpu_custom_call" | custom-call | flops 181193936 | bytes 786432 | tf_op jit(solution)/shard_map/weight_grads/pallas_call | solution.py:857
  506.5 4.7 all-to-all-start.9
  521.1 8.8 %all-to-all-done.9 = bf16[4,48,1920]{2,1,0:T(8,128)(2,1)} async-done(((bf16[4,48,1920]{2,1,0:T(8,128)(2,1)}), bf16[4,48,1920]{2,1,0:T(8,128)(2,1)}, u32[]{:S(2)}, u32[]{:S(2)}) %all-to-all-start.9) | async-done | bytes 737312 | tf_op jit(solution)/shard_map/all_to_all | solution.py:95
  544.7 8.2 %all-to-all-done.6 = bf16[1,4,128,768]{3,2,0,1:T(8,128)(2,1)S(1)} async-done(((bf16[1,4,128,768]{3,2,0,1:T(8,128)(2,1)}), bf16[1,4,128,768]{3,2,0,1:T(8,128)(2,1)S(1)}, u32[]{:S(2)}, u32[]{:S(2)}) %all-to-all-start.6) | async-done | bytes 786464 | tf_op jit(solution)/shard_map/all_to_all | solution.py:95
  560.3 9.4 %all-to-all-done.7 = bf16[4,48,1280]{2,1,0:T(8,128)(2,1)S(1)} async-done(((bf16[4,48,1280]{2,1,0:T(8,128)(2,1)}), bf16[4,48,1280]{2,1,0:T(8,128)(2,1)S(1)}, u32[]{:S(2)}, u32[]{:S(2)}) %all-to-all-start.7) | async-done | bytes 491552 | tf_op jit(solution)/shard_map/all_to_all | solution.py:95
  (249 shorter events, 155.4 us)
Async XLA Ops:
  19.0 145.7 %all-gather.3.cloned.1.call-start = ((), (), s32[]{:S(2)}) async-start(), calls=%async_computation.11 | async-start | bytes 2715648 | tf_op jit(solution)/shard_map/all_gather | solution.py:136
  37.5 35.1 %all-to-all-start.1 = ((bf16[4,48,3072]{2,1,0:T(8,128)(2,1)}), bf16[4,48,3072]{2,1,0:T(8,128)(2,1)S(1)}, u32[]{:S(2)}, u32[]{:S(2)}) async-start(bf16[4,48,3072]{2,1,0:T(8,128)(2,1)} %bitcast.143), calls=%async_computation.1 | async-start | bytes 2359296 | tf_op jit(solution)/shard_map/all_to_all | solution.py:95
  41.0 31.5 %collective-permute-start.2 = (bf16[192,1664]{1,0:T(8,128)(2,1)S(1)}, bf16[192,1664]{1,0:T(8,128)(2,1)}, u32[]{:S(2)}, u32[]{:S(2)}) collective-permute-start(bf16[192,1664]{1,0:T(8,128)(2,1)S(1)} %bitcast.147), channel_id=1, source_target_pairs={{0,4},{4,0},{8,12},{12,8},{1,5},{5,1},{9,13},{13,9},{2,6},{6,2},{1... | collective-permute-start | bytes 1916936 | tf_op jit(solution)/shard_map/ppermute | solution.py:87
  42.3 30.2 %collective-permute-start.3 = (bf16[192,1664]{1,0:T(8,128)(2,1)S(1)}, bf16[192,1664]{1,0:T(8,128)(2,1)}, u32[]{:S(2)}, u32[]{:S(2)}) collective-permute-start(bf16[192,1664]{1,0:T(8,128)(2,1)S(1)} %bitcast.148), channel_id=1, source_target_pairs={{0,8},{4,12},{8,0},{12,4},{1,9},{5,13},{9,1},{13,5},{2,10},{6,14},... | collective-permute-start | bytes 1916936 | tf_op jit(solution)/shard_map/ppermute | solution.py:87
  43.5 29.0 %collective-permute-start.4 = (bf16[192,1664]{1,0:T(8,128)(2,1)S(1)}, bf16[192,1664]{1,0:T(8,128)(2,1)}, u32[]{:S(2)}, u32[]{:S(2)}) collective-permute-start(bf16[192,1664]{1,0:T(8,128)(2,1)S(1)} %bitcast.149), channel_id=1, source_target_pairs={{0,12},{4,8},{8,4},{12,0},{1,13},{5,9},{9,5},{13,1},{2,14},{6,10},... | collective-permute-start | bytes 1916936 | tf_op jit(solution)/shard_map/ppermute | solution.py:87
  75.8 44.3 %collective-permute-start.7 = (bf16[16,48,1664]{2,1,0:T(8,128)(2,1)}, bf16[16,48,1664]{2,1,0:T(8,128)(2,1)}, u32[]{:S(2)}, u32[]{:S(2)}) collective-permute-start(bf16[16,48,1664]{2,1,0:T(8,128)(2,1)} %bitcast.21.refs_0_.refs_1_), channel_id=1, source_target_pairs={{0,16},{16,0},{1,17},{17,1},{2,18},{18,2},{3,19},{19,3},{4,20},{20... | collective-permute-start | bytes 7667720 | tf_op jit(solution)/shard_map/ppermute | solution.py:83
  78.2 32.8 %all-to-all-start.2 = ((bf16[4,128,768]{2,1,0:T(8,128)(2,1)}), bf16[4,128,768]{2,1,0:T(8,128)(2,1)S(1)}, u32[]{:S(2)}, u32[]{:S(2)}) async-start(bf16[4,128,768]{2,1,0:T(8,128)(2,1)} %dynamic-slice_bitcast_fusion.1), calls=%async_computation.2 | async-start | bytes 1572864 | tf_op jit(solution)/shard_map/all_to_all | solution.py:95
  82.7 141.9 %all-gather.5.cloned.1.call-start = ((), (), s32[]{:S(2)}) async-start(), calls=%async_computation.12 | async-start | bytes 5013504 | tf_op jit(solution)/shard_map/all_gather | solution.py:136
  82.8 36.6 %collective-permute-start.5 = (bf16[192,3072]{1,0:T(8,128)(2,1)S(1)}, bf16[192,3072]{1,0:T(8,128)(2,1)S(1)}, u32[]{:S(2)}, u32[]{:S(2)}) collective-permute-start(bf16[192,3072]{1,0:T(8,128)(2,1)S(1)} %bitcast.139), channel_id=1, source_target_pairs={{0,4},{4,0},{8,12},{12,8},{1,5},{5,1},{9,13},{13,9},{2,6},{6,2},{1... | collective-permute-start | bytes 3538952 | tf_op jit(solution)/shard_map/ppermute | solution.py:87
  83.9 36.2 %collective-permute-start.6 = (bf16[192,3072]{1,0:T(8,128)(2,1)S(1)}, bf16[192,3072]{1,0:T(8,128)(2,1)}, u32[]{:S(2)}, u32[]{:S(2)}) collective-permute-start(bf16[192,3072]{1,0:T(8,128)(2,1)S(1)} %bitcast.140), channel_id=1, source_target_pairs={{0,8},{4,12},{8,0},{12,4},{1,9},{5,13},{9,1},{13,5},{2,10},{6,14},... | collective-permute-start | bytes 3538952 | tf_op jit(solution)/shard_map/ppermute | solution.py:87
  129.5 30.7 %collective-permute-start.9 = (bf16[192,3072]{1,0:T(8,128)(2,1)S(1)}, bf16[192,3072]{1,0:T(8,128)(2,1)}, u32[]{:S(2)}, u32[]{:S(2)}) collective-permute-start(bf16[192,3072]{1,0:T(8,128)(2,1)S(1)} %bitcast.141), channel_id=1, source_target_pairs={{0,12},{4,8},{8,4},{12,0},{1,13},{5,9},{9,5},{13,1},{2,14},{6,10},... | collective-permute-start | bytes 3538952 | tf_op jit(solution)/shard_map/ppermute | solution.py:87
  164.7 27.9 %collective-permute-start.11 = (bf16[16,48,1664]{2,1,0:T(8,128)(2,1)}, bf16[16,48,1664]{2,1,0:T(8,128)(2,1)S(1)}, u32[]{:S(2)}, u32[]{:S(2)}) collective-permute-start(bf16[16,48,1664]{2,1,0:T(8,128)(2,1)} %bitcast.127), channel_id=1, source_target_pairs={{0,16},{16,0},{1,17},{17,1},{2,18},{18,2},{3,19},{19,3},{4,20},{20... | collective-permute-start | bytes 7667720 | tf_op jit(solution)/shard_map/ppermute | solution.py:83
  228.1 24.1 %all-to-all-start.4 = ((bf16[4,128,768]{2,1,0:T(8,128)(2,1)}), bf16[4,128,768]{2,1,0:T(8,128)(2,1)S(1)}, u32[]{:S(2)}, u32[]{:S(2)}) async-start(bf16[4,128,768]{2,1,0:T(8,128)(2,1)} %dynamic-slice_bitcast_fusion), calls=%async_computation.4 | async-start | bytes 1572864 | tf_op jit(solution)/shard_map/all_to_all | solution.py:95
  250.5 49.7 %collective-permute-start.16 = (bf16[3072,512]{1,0:T(8,128)(2,1)}, bf16[3072,512]{1,0:T(8,128)(2,1)}, u32[]{:S(2)}, u32[]{:S(2)}) collective-permute-start(bf16[3072,512]{1,0:T(8,128)(2,1)} %get-tuple-element.160.refs_4_), channel_id=1, source_target_pairs={{0,16},{16,0},{1,17},{17,1},{2,18},{18,2},{3,19},{19,3},{4,20},{20... | collective-permute-start | bytes 9437192 | tf_op jit(solution)/shard_map/ppermute | solution.py:83
  272.9 27.3 %collective-permute-start.17 = (bf16[512,2304]{1,0:T(8,128)(2,1)}, bf16[512,2304]{1,0:T(8,128)(2,1)}, u32[]{:S(2)}, u32[]{:S(2)}) collective-permute-start(bf16[512,2304]{1,0:T(8,128)(2,1)} %get-tuple-element.164), channel_id=1, source_target_pairs={{0,16},{16,0},{1,17},{17,1},{2,18},{18,2},{3,19},{19,3},{4,20},{20... | collective-permute-start | bytes 7077896 | tf_op jit(solution)/shard_map/ppermute | solution.py:83
  275.1 44.6 %all-to-all-start.3 = ((bf16[2,4,128,768]{3,2,0,1:T(8,128)(2,1)}), bf16[2,4,128,768]{3,2,0,1:T(8,128)(2,1)S(1)}, u32[]{:S(2)}, u32[]{:S(2)}) async-start(bf16[2,4,128,768]{3,2,0,1:T(8,128)(2,1)} %pad_maximum_fusion.2), calls=%async_computation.3 | async-start | bytes 3145728 | tf_op jit(solution)/shard_map/all_to_all | solution.py:95
  316.4 41.1 %collective-permute-start.21 = (bf16[4,48,3456]{2,1,0:T(8,128)(2,1)}, bf16[4,48,3456]{2,1,0:T(8,128)(2,1)}, u32[]{:S(2)}, u32[]{:S(2)}) collective-permute-start(bf16[4,48,3456]{2,1,0:T(8,128)(2,1)} %get-tuple-element.179), channel_id=1, source_target_pairs={{0,12},{4,8},{8,4},{12,0},{1,13},{5,9},{9,5},{13,1},{2,14},{6,10},... | collective-permute-start | bytes 3981320 | tf_op jit(solution)/shard_map/ppermute | solution.py:87
  317.6 64.8 %collective-permute-start.23 = (bf16[3072,512]{1,0:T(8,128)(2,1)}, bf16[3072,512]{1,0:T(8,128)(2,1)}, u32[]{:S(2)}, u32[]{:S(2)}) collective-permute-start(bf16[3072,512]{1,0:T(8,128)(2,1)} %get-tuple-element.183.refs_2_), channel_id=1, source_target_pairs={{0,16},{16,0},{1,17},{17,1},{2,18},{18,2},{3,19},{19,3},{4,20},{20... | collective-permute-start | bytes 9437192 | tf_op jit(solution)/shard_map/ppermute | solution.py:83
  318.3 58.9 %collective-permute-start.20 = (bf16[4,48,3456]{2,1,0:T(8,128)(2,1)}, bf16[4,48,3456]{2,1,0:T(8,128)(2,1)}, u32[]{:S(2)}, u32[]{:S(2)}) collective-permute-start(bf16[4,48,3456]{2,1,0:T(8,128)(2,1)} %get-tuple-element.178), channel_id=1, source_target_pairs={{0,8},{4,12},{8,0},{12,4},{1,9},{5,13},{9,1},{13,5},{2,10},{6,14},... | collective-permute-start | bytes 3981320 | tf_op jit(solution)/shard_map/ppermute | solution.py:87
  319.4 58.2 %collective-permute-start.19 = (bf16[4,48,3456]{2,1,0:T(8,128)(2,1)}, bf16[4,48,3456]{2,1,0:T(8,128)(2,1)}, u32[]{:S(2)}, u32[]{:S(2)}) collective-permute-start(bf16[4,48,3456]{2,1,0:T(8,128)(2,1)} %get-tuple-element.177), channel_id=1, source_target_pairs={{0,4},{4,0},{8,12},{12,8},{1,5},{5,1},{9,13},{13,9},{2,6},{6,2},{1... | collective-permute-start | bytes 3981320 | tf_op jit(solution)/shard_map/ppermute | solution.py:87
  332.0 45.7 %all-to-all-start.5 = ((bf16[1,4,128,768]{3,2,0,1:T(8,128)(2,1)}), bf16[1,4,128,768]{3,2,0,1:T(8,128)(2,1)S(1)}, u32[]{:S(2)}, u32[]{:S(2)}) async-start(bf16[1,4,128,768]{3,2,0,1:T(8,128)(2,1)} %bitcast.145), calls=%async_computation.5 | async-start | bytes 1572864 | tf_op jit(solution)/shard_map/all_to_all | solution.py:95
  356.5 41.2 %collective-permute-start.27 = (bf16[512,2304]{1,0:T(8,128)(2,1)}, bf16[512,2304]{1,0:T(8,128)(2,1)}, u32[]{:S(2)}, u32[]{:S(2)}) collective-permute-start(bf16[512,2304]{1,0:T(8,128)(2,1)} %get-tuple-element.191), channel_id=1, source_target_pairs={{0,16},{16,0},{1,17},{17,1},{2,18},{18,2},{3,19},{19,3},{4,20},{20... | collective-permute-start | bytes 7077896 | tf_op jit(solution)/shard_map/ppermute | solution.py:83
  395.0 40.3 %collective-permute-start.28 = (bf16[4,48,2688]{2,1,0:T(8,128)(2,1)}, bf16[4,48,2688]{2,1,0:T(8,128)(2,1)}, u32[]{:S(2)}, u32[]{:S(2)}) collective-permute-start(bf16[4,48,2688]{2,1,0:T(8,128)(2,1)} %get-tuple-element.193), channel_id=1, source_target_pairs={{0,4},{4,0},{8,12},{12,8},{1,5},{5,1},{9,13},{13,9},{2,6},{6,2},{1... | collective-permute-start | bytes 3096584 | tf_op jit(solution)/shard_map/ppermute | solution.py:87
  396.1 39.2 %collective-permute-start.29 = (bf16[4,48,2688]{2,1,0:T(8,128)(2,1)}, bf16[4,48,2688]{2,1,0:T(8,128)(2,1)}, u32[]{:S(2)}, u32[]{:S(2)}) collective-permute-start(bf16[4,48,2688]{2,1,0:T(8,128)(2,1)} %get-tuple-element.194), channel_id=1, source_target_pairs={{0,8},{4,12},{8,0},{12,4},{1,9},{5,13},{9,1},{13,5},{2,10},{6,14},... | collective-permute-start | bytes 3096584 | tf_op jit(solution)/shard_map/ppermute | solution.py:87
  396.4 46.0 %collective-permute-start.30 = (bf16[4,48,2688]{2,1,0:T(8,128)(2,1)}, bf16[4,48,2688]{2,1,0:T(8,128)(2,1)}, u32[]{:S(2)}, u32[]{:S(2)}) collective-permute-start(bf16[4,48,2688]{2,1,0:T(8,128)(2,1)} %get-tuple-element.195), channel_id=1, source_target_pairs={{0,12},{4,8},{8,4},{12,0},{1,13},{5,9},{9,5},{13,1},{2,14},{6,10},... | collective-permute-start | bytes 3096584 | tf_op jit(solution)/shard_map/ppermute | solution.py:87
  430.5 36.3 %all-to-all-start.10 = ((bf16[4,48,3456]{2,1,0:T(8,128)(2,1)}), bf16[4,48,3456]{2,1,0:T(8,128)(2,1)}, u32[]{:S(2)}, u32[]{:S(2)}) async-start(bf16[4,48,3456]{2,1,0:T(8,128)(2,1)} %add_convert_fusion), calls=%async_computation.10 | async-start | bytes 2654208 | tf_op jit(solution)/shard_map/all_to_all | solution.py:95
  458.0 36.9 %collective-permute-start.37 = (bf16[512,1536]{1,0:T(8,128)(2,1)}, bf16[512,1536]{1,0:T(8,128)(2,1)}, u32[]{:S(2)}, u32[]{:S(2)}) collective-permute-start(bf16[512,1536]{1,0:T(8,128)(2,1)} %get-tuple-element.216), channel_id=1, source_target_pairs={{0,16},{16,0},{1,17},{17,1},{2,18},{18,2},{3,19},{19,3},{4,20},{20... | collective-permute-start | bytes 4718600 | tf_op jit(solution)/shard_map/ppermute | solution.py:83
  466.8 39.8 %all-to-all-start.8 = ((bf16[4,48,2688]{2,1,0:T(8,128)(2,1)}), bf16[4,48,2688]{2,1,0:T(8,128)(2,1)S(1)}, u32[]{:S(2)}, u32[]{:S(2)}) async-start(bf16[4,48,2688]{2,1,0:T(8,128)(2,1)} %add_convert_fusion.1), calls=%async_computation.8 | async-start | bytes 2064384 | tf_op jit(solution)/shard_map/all_to_all | solution.py:95
  470.3 24.6 %collective-permute-start.35 = (bf16[768,512]{1,0:T(8,128)(2,1)}, bf16[768,512]{1,0:T(8,128)(2,1)}, u32[]{:S(2)}, u32[]{:S(2)}) collective-permute-start(bf16[768,512]{1,0:T(8,128)(2,1)} %get-tuple-element.214.refs_0_), channel_id=1, source_target_pairs={{0,16},{16,0},{1,17},{17,1},{2,18},{18,2},{3,19},{19,3},{4,20},{20... | collective-permute-start | bytes 2359304 | tf_op jit(solution)/shard_map/ppermute | solution.py:83
  512.4 23.7 %collective-permute-start.40 = (bf16[4,48,1280]{2,1,0:T(8,128)(2,1)}, bf16[4,48,1280]{2,1,0:T(8,128)(2,1)}, u32[]{:S(2)}, u32[]{:S(2)}) collective-permute-start(bf16[4,48,1280]{2,1,0:T(8,128)(2,1)} %get-tuple-element.224), channel_id=1, source_target_pairs={{0,8},{4,12},{8,0},{12,4},{1,9},{5,13},{9,1},{13,5},{2,10},{6,14},... | collective-permute-start | bytes 1474568 | tf_op jit(solution)/shard_map/ppermute | solution.py:87
  514.9 23.7 %collective-permute-start.38 = (bf16[4,128,768]{2,1,0:T(8,128)(2,1)}, bf16[4,128,768]{2,1,0:T(8,128)(2,1)}, u32[]{:S(2)}, u32[]{:S(2)}) collective-permute-start(bf16[4,128,768]{2,1,0:T(8,128)(2,1)} %select_bitcast_fusion), channel_id=1, source_target_pairs={{0,16},{16,0},{1,17},{17,1},{2,18},{18,2},{3,19},{19,3},{4,20},{20... | collective-permute-start | bytes 2359304 | tf_op jit(solution)/shard_map/ppermute | solution.py:83
  544.7 28.5 %collective-permute-start.45 = (bf16[48,1536]{1,0:T(8,128)(2,1)}, bf16[48,1536]{1,0:T(8,128)(2,1)S(1)}, u32[]{:S(2)}, u32[]{:S(2)}) collective-permute-start(bf16[48,1536]{1,0:T(8,128)(2,1)} %broadcast_select_fusion.7), channel_id=1, source_target_pairs={{0,16},{16,0},{1,17},{17,1},{2,18},{18,2},{3,19},{19,3},{4,20},{20... | collective-permute-start | bytes 442376 | tf_op jit(solution)/shard_map/ppermute | solution.py:83
  (60 other events, 838.2 us)
Sparse Core Ops, SparseCore 0:
  35.6 83.9 all-gather.2
  123.0 101.5 all-gather.4

commit v4 on v3

--- a/solution.py
+++ b/solution.py
@@ -758,10 +758,11 @@
     there = 1 - meta[0]
     wide = 3 * width // 2
     send_ref[:, :wide] = dqkv_ref[:, side(there, wide)]
-    send_ref[:, wide:] = low_ref[:, side(there, width // 2)]
-
-
-def qkv_backward(plan, dq, dk, dv, far, du2, x, gains, cos, sin, attn):
+    if send_ref.shape[1] > wide:
+        send_ref[:, wide:] = low_ref[:, side(there, width // 2)]
+
+
+def qkv_backward(plan, dq, dk, dv, far, du2, x, gains, cos, sin, attn, sent):
     rows, width = x.shape
     step = row_step(rows)
     refs = attn.refs()
@@ -773,7 +774,7 @@
             jax.ShapeDtypeStruct((rows, width), F32),
             jax.ShapeDtypeStruct((rows, width), BF16),
             jax.ShapeDtypeStruct((1, width), F32),
-            jax.ShapeDtypeStruct((rows, 2 * width), BF16),
+            jax.ShapeDtypeStruct((rows, sent), BF16),
         ],
         grid=(rows // step,),
         in_specs=[smem()]
@@ -781,7 +782,7 @@
         + [whole((8, width)), rows_of(step, PAIR), rows_of(step, PAIR)]
         + [pl.BlockSpec((2, step, width), lambda i: (0, i, 0))] * len(far)
         + [anywhere()] * len(refs),
-        out_specs=[rows_of(step, 3 * width), some, some, whole((1, width)), rows_of(step, 2 * width)],
+        out_specs=[rows_of(step, 3 * width), some, some, whole((1, width)), rows_of(step, sent)],
         scratch_shapes=[
             pltpu.VMEM((plan.shards, plan.shard_rows, 2 * width), BF16),
             pltpu.VMEM((plan.shards, plan.shard_rows, width), BF16),
@@ -946,7 +947,7 @@
     got = other_core(by_section(plan, layers[1], layers[0]))
     first = by_section(plan, own, got)
     second = by_section(plan, got, own)
-    both = jnp.stack([first, second], axis=1).astype(F32)
+    both = jnp.concatenate([first.astype(F32), second.astype(F32)], axis=1)
     return both.reshape(1, plan.micro, plan.seqs, plan.span, plan.width)
 
 
@@ -1100,7 +1101,7 @@
     def qkv_part(layer, dq, dk, dv, far, du2, dg2):
         x = saved[layer][0]
         dqkv, dx, low, dg1, send = qkv_backward(
-            plan, order.gate(dq), dk, dv, far, du2, x, gains[layer], cos, sin, weights[layer][0]
+            plan, order.gate(dq), dk, dv, far, du2, x, gains[layer], cos, sin, weights[layer][0], wide + layer * width_half
         )
         order.mark(dg1)
         grads[layer] = low

time: 593 us -> 593 us (level)
    ppermute x18, waiting for transfers between devices: 68.5 us -> 74.9 us  [xor_dp(): return lax.ppermute(value, 'dp', [(i, i ^ mask) for i in range(plan.n_dp)])]
    all_to_all x11, waiting for transfers between devices: 102 us -> 95.6 us  [exchange_ctx(): return lax.all_to_all(value, 'ctx', dim, dim, tiled=True)]
  transfers between devices with their start and end apart: 60 -> 60, of which waited for: 22 -> 20; matrix products, arithmetic and copies ran while one was open for 9% -> 9% of each run, Pallas kernels for 39% -> 39%
where the time goes in v4:
time: 593 us; the launch traced here: 588 us
  Pallas kernels  228 us (38%)
  waiting for transfers between devices  192 us (32%)
  starting transfers between devices  84.9 us (14%)
  other arithmetic  51.8 us (9%)
  local copies, waits for them, and re-layouts  16.3 us (3%)
  between operations  14.9 us (3%)
    all_to_all x11, waiting for transfers between devices, exchange_ctx(): return lax.all_to_all(value, 'ctx', dim, dim, tiled=True)  95.6 us
    ppermute x18, waiting for transfers between devices, xor_dp(): return lax.ppermute(value, 'dp', [(i, i ^ mask) for i in range(plan.n_dp)])  74.9 us
    all_to_all x11, starting transfers between devices, exchange_ctx(): return lax.all_to_all(value, 'ctx', dim, dim, tiled=True)  47.6 us
    pallas_call x4, Pallas kernels, weight_call(): pl.pallas_call(functools.partial(weight_kernel, jobs, len(lefts), len(rig...  45.6 us
    pallas_call x2, Pallas kernels, attention_backward(): pl.pallas_call(functools.partial(attention_back_kernel, chunks, min(256,...  41.3 us
    pallas_call x2, Pallas kernels, ffn_backward(): pl.pallas_call(functools.partial(ffn_back_kernel, relative), out_shape=[w...  39.6 us
    pallas_call x2, Pallas kernels, ffn_forward(): pl.pallas_call(functools.partial(ffn_kernel, relative), out_shape=[jax.Sh...  32.9 us
    pallas_call x2, Pallas kernels, attention_forward(): pl.pallas_call(functools.partial(attention_kernel, chunks, min(256, rows)...  28.2 us
  transfers between devices with their start and end apart: 60, of which 20 were waited for; matrix products, arithmetic and copies ran while one was open for 9% of the time, Pallas kernels for 39%

profile of v4, /device:TPU:1, one launch (start us, length us, event | category | flops | bytes accessed | tf_op | source)
XLA Modules:
  0.0 587.7 jit_solution(2367351833115898429)
XLA Ops:
  13.2 5.7 all-to-all-start
  19.8 15.6 %all-to-all-done = bf16[4,48,1664]{2,1,0:T(8,128)(2,1)S(1)} async-done(((bf16[4,48,1664]{2,1,0:T(8,128)(2,1)}), bf16[4,48,1664]{2,1,0:T(8,128)(2,1)S(1)}, u32[]{:S(2)}, u32[]{:S(2)}) %all-to-all-start) | async-done | bytes 639008 | tf_op jit(solution)/shard_map/all_to_all | solution.py:95
  43.7 28.8 %all-to-all-done.1 = bf16[4,48,3072]{2,1,0:T(8,128)(2,1)S(1)} async-done(((bf16[4,48,3072]{2,1,0:T(8,128)(2,1)}), bf16[4,48,3072]{2,1,0:T(8,128)(2,1)S(1)}, u32[]{:S(2)}, u32[]{:S(2)}) %all-to-all-start.1) | async-done | bytes 1179680 | tf_op jit(solution)/shard_map/all_to_all | solution.py:95
  87.4 23.6 %all-to-all-done.2 = bf16[4,128,768]{2,1,0:T(8,128)(2,1)S(1)} async-done(((bf16[4,128,768]{2,1,0:T(8,128)(2,1)}), bf16[4,128,768]{2,1,0:T(8,128)(2,1)S(1)}, u32[]{:S(2)}, u32[]{:S(2)}) %all-to-all-start.2) | async-done | bytes 786464 | tf_op jit(solution)/shard_map/all_to_all | solution.py:95
  111.0 8.4 %collective-permute-done.5 = bf16[192,3072]{1,0:T(8,128)(2,1)S(1)} collective-permute-done((bf16[192,3072]{1,0:T(8,128)(2,1)S(1)}, bf16[192,3072]{1,0:T(8,128)(2,1)S(1)}, u32[]{:S(2)}, u32[]{:S(2)}) %collective-permute-start.5) | collective-permute-done | bytes 1179680 | tf_op jit(solution)/shard_map/ppermute | solution.py:87
  120.1 8.0 %qkv_forward.2 = (bf16[768,512]{1,0:T(8,128)(2,1)}, bf16[512,768]{1,0:T(8,128)(2,1)}, bf16[2,512,768]{2,1,0:T(8,128)(2,1)}, f32[8,768]{1,0:T(8,128)}) custom-call(s32[2]{0:T(128)} %pad_add_fusion.meta, bf16[512,768]{1,0:T(8,128)(2,1)} %bitcast.130, f32[512,128]{1,0:T(8,128)} %get-tuple-element.296.cos_ref, f32[512,128]{1,0:T(8,128)} %get-tuple-element.297.sin_ref, ...), custom_call_target="tpu_custom_call" | custom-call | flops 181193936 | bytes 825753 | tf_op jit(solution)/shard_map/qkv_forward/pallas_call | solution.py:355
  134.5 14.1 %attention_forward.2 = (bf16[512,768]{1,0:T(8,128)(2,1)}, bf16[768,512]{1,0:T(8,128)(2,1)}, f32[6,8,512]{2,1,0:T(8,128)}) custom-call(bf16[512,768]{1,0:T(8,128)(2,1)} %get-tuple-element.124.q_ref, bf16[2,512,768]{2,1,0:T(8,128)(2,1)} %get-tuple-element.125.refs_0_, bf16[2,512,768]{2,1,0:T(8,128)(2,1)} %copy-done.8, ...), custom_call_target="tpu_custom_call" | custom-call | flops 644245120 | bytes 471859 | tf_op jit(solution)/shard_map/attention_forward/pallas_call | solution.py:436
  148.6 11.6 %collective-permute-done.9 = bf16[192,3072]{1,0:T(8,128)(2,1)} collective-permute-done((bf16[192,3072]{1,0:T(8,128)(2,1)S(1)}, bf16[192,3072]{1,0:T(8,128)(2,1)}, u32[]{:S(2)}, u32[]{:S(2)}) %collective-permute-start.9) | collective-permute-done | bytes 1179680 | tf_op jit(solution)/shard_map/ppermute | solution.py:87
  164.8 11.5 %collective-permute-done.10.refs_3_ = bf16[16,48,3072]{2,1,0:T(8,128)(2,1)} collective-permute-done((bf16[16,48,3072]{2,1,0:T(8,128)(2,1)}, bf16[16,48,3072]{2,1,0:T(8,128)(2,1)}, u32[]{:S(2)}, u32[]{:S(2)}) %collective-permute-start.10) | collective-permute-done | bytes 4718624 | tf_op jit(solution)/shard_map/ppermute | solution.py:83
  176.2 16.3 %ffn_forward.2 = (f32[512,768]{1,0:T(8,128)}, bf16[768,512]{1,0:T(8,128)(2,1)}, f32[512,768]{1,0:T(8,128)}, bf16[512,768]{1,0:T(8,128)(2,1)}, bf16[3072,512]{1,0:T(8,128)(2,1)}, /*index=5*/bf16[512,3072]{1,0:T(8,128)(2,1)}) custom-call(s32[2]{0:T(128)} %pad_add_fusion.meta, bf16[512,768]{1,0:T(8,128)(2,1)} %get-tuple-element.128.o_ref, ...), custom_call_target="tpu_custom_call" | custom-call | flops 553019008 | bytes 2359296 | tf_op jit(solution)/shard_map/ffn_forward/pallas_call | solution.py:526
  194.0 8.2 %qkv_forward.3 = (bf16[768,512]{1,0:T(8,128)(2,1)}, bf16[512,768]{1,0:T(8,128)(2,1)}, bf16[2,512,768]{2,1,0:T(8,128)(2,1)}, f32[8,768]{1,0:T(8,128)}) custom-call(s32[2]{0:T(128)} %pad_add_fusion.meta, f32[512,768]{1,0:T(8,128)} %get-tuple-element.134.x_ref, f32[512,128]{1,0:T(8,128)} %get-tuple-element.296.cos_ref, f32[512,128]{1,0:T(8,128)} %get-tuple-element.297.sin_ref, ...), custom_call_target="tpu_custom_call" | custom-call | flops 181193936 | bytes 825753 | tf_op jit(solution)/shard_map/qkv_forward/pallas_call | solution.py:355
  207.1 14.1 %attention_forward.3 = (bf16[512,768]{1,0:T(8,128)(2,1)}, bf16[768,512]{1,0:T(8,128)(2,1)}, f32[6,8,512]{2,1,0:T(8,128)}) custom-call(bf16[512,768]{1,0:T(8,128)(2,1)} %get-tuple-element.138.q_ref, bf16[2,512,768]{2,1,0:T(8,128)(2,1)} %get-tuple-element.139.refs_0_, bf16[2,512,768]{2,1,0:T(8,128)(2,1)} %copy-done.9, ...), custom_call_target="tpu_custom_call" | custom-call | flops 644245120 | bytes 471859 | tf_op jit(solution)/shard_map/attention_forward/pallas_call | solution.py:436
  233.9 16.6 %ffn_forward.3 = (f32[512,768]{1,0:T(8,128)}, bf16[768,512]{1,0:T(8,128)(2,1)}, f32[512,768]{1,0:T(8,128)}, bf16[512,768]{1,0:T(8,128)(2,1)}, bf16[3072,512]{1,0:T(8,128)(2,1)}, /*index=5*/bf16[512,3072]{1,0:T(8,128)(2,1)}) custom-call(s32[2]{0:T(128)} %pad_add_fusion.meta, bf16[512,768]{1,0:T(8,128)(2,1)} %get-tuple-element.142.o_ref, ...), custom_call_target="tpu_custom_call" | custom-call | flops 553019008 | bytes 2359296 | tf_op jit(solution)/shard_map/ffn_forward/pallas_call | solution.py:526
  253.0 19.7 %ffn_backward.2 = (bf16[512,768]{1,0:T(8,128)(2,1)}, bf16[512,3072]{1,0:T(8,128)(2,1)}, f32[512,768]{1,0:T(8,128)}, bf16[512,768]{1,0:T(8,128)(2,1)}, bf16[512,7...) custom-call(s32[2]{0:T(128)} %pad_add_fusion.meta, bf16[512,768]{1,0:T(8,128)(2,1)} %bitcast.140, ...), custom_call_target="tpu_custom_call" | custom-call | flops 543581824 | bytes 2398617 | tf_op jit(solution)/shard_map/ffn_backward/pallas_call | solution.py:609
  279.4 20.6 %attention_backward.2 = (bf16[512,768]{1,0:T(8,128)(2,1)}, f32[512,768]{1,0:T(8,128)}, f32[512,768]{1,0:T(8,128)}, bf16[2,512,768]{2,1,0:T(8,128)(2,1)}) custom-call(bf16[512,768]{1,0:T(8,128)(2,1)} %get-tuple-element.138.q_ref, bf16[512,768]{1,0:T(8,128)(2,1)} %get-tuple-element.156.do_ref, bf16[512,768]{1,0:T(8,128)(2,1)} %get-tuple-element.142.o_ref, ...), custom_call_target="tpu_custom_call" | custom-call | flops 1610612736 | bytes 1258291 | tf_op jit(solution)/shard_map/attention_backward/pallas_call | solution.py:688
  301.4 15.1 %weight_grads.4 = (bf16[4,48,3456]{2,1,0:T(8,128)(2,1)}, bf16[4,48,3456]{2,1,0:T(8,128)(2,1)}, bf16[4,48,3456]{2,1,0:T(8,128)(2,1)}, bf16[4,48,3456]{2,1,0:T(8,128)(2,1)}) custom-call(s32[2]{0:T(128)} %pad_add_fusion.meta, bf16[768,512]{1,0:T(8,128)(2,1)} %get-tuple-element.158.refs_0_, bf16[768,512]{1,0:T(8,128)(2,1)} %copy-done.17, ...), custom_call_target="tpu_custom_call" | custom-call | flops 543581824 | bytes 2182348 | tf_op jit(solution)/shard_map/weight_grads/pallas_call | solution.py:858
  319.8 12.3 %qkv_backward.2 = (bf16[512,2304]{1,0:T(8,128)(2,1)}, f32[512,768]{1,0:T(8,128)}, bf16[512,768]{1,0:T(8,128)(2,1)}, f32[1,768]{1,0:T(1,128)}, bf16[512,1536]{1,0:T(8,128)(2,1)}) custom-call(s32[2]{0:T(128)} %pad_add_fusion.meta, bf16[512,768]{1,0:T(8,128)(2,1)} %get-tuple-element.166.dq_ref, f32[512,768]{1,0:T(8,128)} %get-tuple-element.167.dk_ref, ...), custom_call_target="tpu_custom_call" | custom-call | flops 181193936 | bytes 1533542 | tf_op jit(solution)/shard_map/qkv_backward/pallas_call | solution.py:770
  332.1 5.0 all-to-all-start.5
  337.1 19.8 %ffn_backward.3 = (bf16[512,768]{1,0:T(8,128)(2,1)}, bf16[512,3072]{1,0:T(8,128)(2,1)}, f32[512,768]{1,0:T(8,128)}, bf16[512,768]{1,0:T(8,128)(2,1)}, bf16[512,7...) custom-call(s32[2]{0:T(128)} %pad_add_fusion.meta, f32[512,768]{1,0:T(8,128)} %get-tuple-element.173.c_ref, ...), custom_call_target="tpu_custom_call" | custom-call | flops 543581824 | bytes 2398617 | tf_op jit(solution)/shard_map/ffn_backward/pallas_call | solution.py:609
  358.0 19.2 %collective-permute-done.20 = bf16[4,48,3456]{2,1,0:T(8,128)(2,1)} collective-permute-done((bf16[4,48,3456]{2,1,0:T(8,128)(2,1)}, bf16[4,48,3456]{2,1,0:T(8,128)(2,1)}, u32[]{:S(2)}, u32[]{:S(2)}) %collective-permute-start.20) | collective-permute-done | bytes 1327136 | tf_op jit(solution)/shard_map/ppermute | solution.py:87
  382.4 12.4 %weight_grads.5 = (bf16[4,48,2688]{2,1,0:T(8,128)(2,1)}, bf16[4,48,2688]{2,1,0:T(8,128)(2,1)}, bf16[4,48,2688]{2,1,0:T(8,128)(2,1)}, bf16[4,48,2688]{2,1,0:T(8,128)(2,1)}) custom-call(s32[2]{0:T(128)} %pad_add_fusion.meta, bf16[768,512]{1,0:T(8,128)(2,1)} %get-tuple-element.182.refs_0_, bf16[768,512]{1,0:T(8,128)(2,1)} %collective-permute-done.22.refs_1_, ...), custom_call_target="tpu_custom_call" | custom-call | flops 422785856 | bytes 1671168 | tf_op jit(solution)/shard_map/weight_grads/pallas_call | solution.py:858
  397.5 4.9 all-to-all-start.10
  402.4 10.1 %weight_grads.6 = (bf16[4,48,1920]{2,1,0:T(8,128)(2,1)}, bf16[4,48,1920]{2,1,0:T(8,128)(2,1)}, bf16[4,48,1920]{2,1,0:T(8,128)(2,1)}, bf16[4,48,1920]{2,1,0:T(8,128)(2,1)}) custom-call(s32[2]{0:T(128)} %pad_add_fusion.meta, bf16[768,512]{1,0:T(8,128)(2,1)} %get-tuple-element.187.refs_0_, bf16[768,512]{1,0:T(8,128)(2,1)} %collective-permute-done.25.refs_1_, ...), custom_call_target="tpu_custom_call" | custom-call | flops 301989888 | bytes 1238630 | tf_op jit(solution)/shard_map/weight_grads/pallas_call | solution.py:858
  412.5 20.7 %attention_backward.3 = (bf16[512,768]{1,0:T(8,128)(2,1)}, f32[512,768]{1,0:T(8,128)}, f32[512,768]{1,0:T(8,128)}, bf16[2,512,768]{2,1,0:T(8,128)(2,1)}) custom-call(bf16[512,768]{1,0:T(8,128)(2,1)} %get-tuple-element.124.q_ref, bf16[512,768]{1,0:T(8,128)(2,1)} %get-tuple-element.199.do_ref, bf16[512,768]{1,0:T(8,128)(2,1)} %get-tuple-element.128.o_ref, ...), custom_call_target="tpu_custom_call" | custom-call | flops 1610612736 | bytes 1258291 | tf_op jit(solution)/shard_map/attention_backward/pallas_call | solution.py:688
  434.4 8.2 %collective-permute-done.30 = bf16[4,48,2688]{2,1,0:T(8,128)(2,1)} collective-permute-done((bf16[4,48,2688]{2,1,0:T(8,128)(2,1)}, bf16[4,48,2688]{2,1,0:T(8,128)(2,1)}, u32[]{:S(2)}, u32[]{:S(2)}) %collective-permute-start.30) | collective-permute-done | bytes 1032224 | tf_op jit(solution)/shard_map/ppermute | solution.py:87
  446.8 12.0 %qkv_backward.3 = (bf16[512,2304]{1,0:T(8,128)(2,1)}, f32[512,768]{1,0:T(8,128)}, bf16[512,768]{1,0:T(8,128)(2,1)}, f32[1,768]{1,0:T(1,128)}, bf16[512,1152]{1,0:T(8,128)(2,1)}) custom-call(s32[2]{0:T(128)} %pad_add_fusion.meta, bf16[512,768]{1,0:T(8,128)(2,1)} %get-tuple-element.202.dq_ref, f32[512,768]{1,0:T(8,128)} %get-tuple-element.203.dk_ref, ...), custom_call_target="tpu_custom_call" | custom-call | flops 181193936 | bytes 1533542 | tf_op jit(solution)/shard_map/qkv_backward/pallas_call | solution.py:770
  470.1 9.3 %collective-permute-done.34 = bf16[4,48,1920]{2,1,0:T(8,128)(2,1)} collective-permute-done((bf16[4,48,1920]{2,1,0:T(8,128)(2,1)}, bf16[4,48,1920]{2,1,0:T(8,128)(2,1)}, u32[]{:S(2)}, u32[]{:S(2)}) %collective-permute-start.34) | collective-permute-done | bytes 737312 | tf_op jit(solution)/shard_map/ppermute | solution.py:87
  480.6 14.9 %collective-permute-done.33 = bf16[4,48,1920]{2,1,0:T(8,128)(2,1)} collective-permute-done((bf16[4,48,1920]{2,1,0:T(8,128)(2,1)}, bf16[4,48,1920]{2,1,0:T(8,128)(2,1)}, u32[]{:S(2)}, u32[]{:S(2)}) %collective-permute-start.33) | collective-permute-done | bytes 737312 | tf_op jit(solution)/shard_map/ppermute | solution.py:87
  496.3 7.9 %weight_grads.7 = (bf16[4,48,1280]{2,1,0:T(8,128)(2,1)}, bf16[4,48,1280]{2,1,0:T(8,128)(2,1)}, bf16[4,48,1280]{2,1,0:T(8,128)(2,1)}, bf16[4,48,1280]{2,1,0:T(8,128)(2,1)}) custom-call(s32[2]{0:T(128)} %pad_add_fusion.meta, bf16[768,512]{1,0:T(8,128)(2,1)} %get-tuple-element.214.refs_0_, bf16[768,512]{1,0:T(8,128)(2,1)} %collective-permute-done.35.refs_1_, ...), custom_call_target="tpu_custom_call" | custom-call | flops 181193936 | bytes 747110 | tf_op jit(solution)/shard_map/weight_grads/pallas_call | solution.py:858
  521.7 8.8 %all-to-all-done.9 = bf16[4,48,1920]{2,1,0:T(8,128)(2,1)} async-done(((bf16[4,48,1920]{2,1,0:T(8,128)(2,1)}), bf16[4,48,1920]{2,1,0:T(8,128)(2,1)}, u32[]{:S(2)}, u32[]{:S(2)}) %all-to-all-start.9) | async-done | bytes 737312 | tf_op jit(solution)/shard_map/all_to_all | solution.py:95
  545.2 8.3 %all-to-all-done.6 = bf16[1,4,128,768]{3,2,0,1:T(8,128)(2,1)S(1)} async-done(((bf16[1,4,128,768]{3,2,0,1:T(8,128)(2,1)}), bf16[1,4,128,768]{3,2,0,1:T(8,128)(2,1)S(1)}, u32[]{:S(2)}, u32[]{:S(2)}) %all-to-all-start.6) | async-done | bytes 786464 | tf_op jit(solution)/shard_map/all_to_all | solution.py:95
  560.9 9.4 %all-to-all-done.7 = bf16[4,48,1280]{2,1,0:T(8,128)(2,1)S(1)} async-done(((bf16[4,48,1280]{2,1,0:T(8,128)(2,1)}), bf16[4,48,1280]{2,1,0:T(8,128)(2,1)S(1)}, u32[]{:S(2)}, u32[]{:S(2)}) %all-to-all-start.7) | async-done | bytes 491552 | tf_op jit(solution)/shard_map/all_to_all | solution.py:95
  (249 shorter events, 151.7 us)
Async XLA Ops:
  19.0 145.7 %all-gather.3.cloned.1.call-start = ((), (), s32[]{:S(2)}) async-start(), calls=%async_computation.11 | async-start | bytes 2715648 | tf_op jit(solution)/shard_map/all_gather | solution.py:136
  37.5 35.1 %all-to-all-start.1 = ((bf16[4,48,3072]{2,1,0:T(8,128)(2,1)}), bf16[4,48,3072]{2,1,0:T(8,128)(2,1)S(1)}, u32[]{:S(2)}, u32[]{:S(2)}) async-start(bf16[4,48,3072]{2,1,0:T(8,128)(2,1)} %bitcast.139), calls=%async_computation.1 | async-start | bytes 2359296 | tf_op jit(solution)/shard_map/all_to_all | solution.py:95
  41.0 31.5 %collective-permute-start.2 = (bf16[192,1664]{1,0:T(8,128)(2,1)S(1)}, bf16[192,1664]{1,0:T(8,128)(2,1)}, u32[]{:S(2)}, u32[]{:S(2)}) collective-permute-start(bf16[192,1664]{1,0:T(8,128)(2,1)S(1)} %bitcast.142), channel_id=1, source_target_pairs={{0,4},{4,0},{8,12},{12,8},{1,5},{5,1},{9,13},{13,9},{2,6},{6,2},{1... | collective-permute-start | bytes 1916936 | tf_op jit(solution)/shard_map/ppermute | solution.py:87
  42.3 30.2 %collective-permute-start.3 = (bf16[192,1664]{1,0:T(8,128)(2,1)S(1)}, bf16[192,1664]{1,0:T(8,128)(2,1)}, u32[]{:S(2)}, u32[]{:S(2)}) collective-permute-start(bf16[192,1664]{1,0:T(8,128)(2,1)S(1)} %bitcast.143), channel_id=1, source_target_pairs={{0,8},{4,12},{8,0},{12,4},{1,9},{5,13},{9,1},{13,5},{2,10},{6,14},... | collective-permute-start | bytes 1916936 | tf_op jit(solution)/shard_map/ppermute | solution.py:87
  43.5 29.0 %collective-permute-start.4 = (bf16[192,1664]{1,0:T(8,128)(2,1)S(1)}, bf16[192,1664]{1,0:T(8,128)(2,1)}, u32[]{:S(2)}, u32[]{:S(2)}) collective-permute-start(bf16[192,1664]{1,0:T(8,128)(2,1)S(1)} %bitcast.144), channel_id=1, source_target_pairs={{0,12},{4,8},{8,4},{12,0},{1,13},{5,9},{9,5},{13,1},{2,14},{6,10},... | collective-permute-start | bytes 1916936 | tf_op jit(solution)/shard_map/ppermute | solution.py:87
  75.8 44.2 %collective-permute-start.7 = (bf16[16,48,1664]{2,1,0:T(8,128)(2,1)}, bf16[16,48,1664]{2,1,0:T(8,128)(2,1)}, u32[]{:S(2)}, u32[]{:S(2)}) collective-permute-start(bf16[16,48,1664]{2,1,0:T(8,128)(2,1)} %bitcast.21.refs_0_.refs_1_), channel_id=1, source_target_pairs={{0,16},{16,0},{1,17},{17,1},{2,18},{18,2},{3,19},{19,3},{4,20},{20... | collective-permute-start | bytes 7667720 | tf_op jit(solution)/shard_map/ppermute | solution.py:83
  78.2 32.8 %all-to-all-start.2 = ((bf16[4,128,768]{2,1,0:T(8,128)(2,1)}), bf16[4,128,768]{2,1,0:T(8,128)(2,1)S(1)}, u32[]{:S(2)}, u32[]{:S(2)}) async-start(bf16[4,128,768]{2,1,0:T(8,128)(2,1)} %dynamic-slice_bitcast_fusion.1), calls=%async_computation.2 | async-start | bytes 1572864 | tf_op jit(solution)/shard_map/all_to_all | solution.py:95
  82.7 141.9 %all-gather.5.cloned.1.call-start = ((), (), s32[]{:S(2)}) async-start(), calls=%async_computation.12 | async-start | bytes 5013504 | tf_op jit(solution)/shard_map/all_gather | solution.py:136
  82.8 36.6 %collective-permute-start.5 = (bf16[192,3072]{1,0:T(8,128)(2,1)S(1)}, bf16[192,3072]{1,0:T(8,128)(2,1)S(1)}, u32[]{:S(2)}, u32[]{:S(2)}) collective-permute-start(bf16[192,3072]{1,0:T(8,128)(2,1)S(1)} %bitcast.135), channel_id=1, source_target_pairs={{0,4},{4,0},{8,12},{12,8},{1,5},{5,1},{9,13},{13,9},{2,6},{6,2},{1... | collective-permute-start | bytes 3538952 | tf_op jit(solution)/shard_map/ppermute | solution.py:87
  83.9 36.2 %collective-permute-start.6 = (bf16[192,3072]{1,0:T(8,128)(2,1)S(1)}, bf16[192,3072]{1,0:T(8,128)(2,1)}, u32[]{:S(2)}, u32[]{:S(2)}) collective-permute-start(bf16[192,3072]{1,0:T(8,128)(2,1)S(1)} %bitcast.136), channel_id=1, source_target_pairs={{0,8},{4,12},{8,0},{12,4},{1,9},{5,13},{9,1},{13,5},{2,10},{6,14},... | collective-permute-start | bytes 3538952 | tf_op jit(solution)/shard_map/ppermute | solution.py:87
  129.5 30.7 %collective-permute-start.9 = (bf16[192,3072]{1,0:T(8,128)(2,1)S(1)}, bf16[192,3072]{1,0:T(8,128)(2,1)}, u32[]{:S(2)}, u32[]{:S(2)}) collective-permute-start(bf16[192,3072]{1,0:T(8,128)(2,1)S(1)} %bitcast.137), channel_id=1, source_target_pairs={{0,12},{4,8},{8,4},{12,0},{1,13},{5,9},{9,5},{13,1},{2,14},{6,10},... | collective-permute-start | bytes 3538952 | tf_op jit(solution)/shard_map/ppermute | solution.py:87
  164.7 27.9 %collective-permute-start.11 = (bf16[16,48,1664]{2,1,0:T(8,128)(2,1)}, bf16[16,48,1664]{2,1,0:T(8,128)(2,1)S(1)}, u32[]{:S(2)}, u32[]{:S(2)}) collective-permute-start(bf16[16,48,1664]{2,1,0:T(8,128)(2,1)} %bitcast.122), channel_id=1, source_target_pairs={{0,16},{16,0},{1,17},{17,1},{2,18},{18,2},{3,19},{19,3},{4,20},{20... | collective-permute-start | bytes 7667720 | tf_op jit(solution)/shard_map/ppermute | solution.py:83
  250.5 49.8 %collective-permute-start.16 = (bf16[3072,512]{1,0:T(8,128)(2,1)}, bf16[3072,512]{1,0:T(8,128)(2,1)}, u32[]{:S(2)}, u32[]{:S(2)}) collective-permute-start(bf16[3072,512]{1,0:T(8,128)(2,1)} %get-tuple-element.160.refs_4_), channel_id=1, source_target_pairs={{0,16},{16,0},{1,17},{17,1},{2,18},{18,2},{3,19},{19,3},{4,20},{20... | collective-permute-start | bytes 9437192 | tf_op jit(solution)/shard_map/ppermute | solution.py:83
  272.7 27.6 %collective-permute-start.17 = (bf16[512,2304]{1,0:T(8,128)(2,1)}, bf16[512,2304]{1,0:T(8,128)(2,1)}, u32[]{:S(2)}, u32[]{:S(2)}) collective-permute-start(bf16[512,2304]{1,0:T(8,128)(2,1)} %get-tuple-element.164), channel_id=1, source_target_pairs={{0,16},{16,0},{1,17},{17,1},{2,18},{18,2},{3,19},{19,3},{4,20},{20... | collective-permute-start | bytes 7077896 | tf_op jit(solution)/shard_map/ppermute | solution.py:83
  274.9 44.9 %all-to-all-start.3 = ((bf16[2,4,128,768]{3,2,0,1:T(8,128)(2,1)}), bf16[2,4,128,768]{3,2,0,1:T(8,128)(2,1)S(1)}, u32[]{:S(2)}, u32[]{:S(2)}) async-start(bf16[2,4,128,768]{3,2,0,1:T(8,128)(2,1)} %pad_maximum_fusion.2), calls=%async_computation.3 | async-start | bytes 3145728 | tf_op jit(solution)/shard_map/all_to_all | solution.py:95
  316.5 41.4 %collective-permute-start.21 = (bf16[4,48,3456]{2,1,0:T(8,128)(2,1)}, bf16[4,48,3456]{2,1,0:T(8,128)(2,1)}, u32[]{:S(2)}, u32[]{:S(2)}) collective-permute-start(bf16[4,48,3456]{2,1,0:T(8,128)(2,1)} %get-tuple-element.179), channel_id=1, source_target_pairs={{0,12},{4,8},{8,4},{12,0},{1,13},{5,9},{9,5},{13,1},{2,14},{6,10},... | collective-permute-start | bytes 3981320 | tf_op jit(solution)/shard_map/ppermute | solution.py:87
  317.6 64.8 %collective-permute-start.23 = (bf16[3072,512]{1,0:T(8,128)(2,1)}, bf16[3072,512]{1,0:T(8,128)(2,1)}, u32[]{:S(2)}, u32[]{:S(2)}) collective-permute-start(bf16[3072,512]{1,0:T(8,128)(2,1)} %get-tuple-element.183.refs_2_), channel_id=1, source_target_pairs={{0,16},{16,0},{1,17},{17,1},{2,18},{18,2},{3,19},{19,3},{4,20},{20... | collective-permute-start | bytes 9437192 | tf_op jit(solution)/shard_map/ppermute | solution.py:83
  318.3 58.9 %collective-permute-start.20 = (bf16[4,48,3456]{2,1,0:T(8,128)(2,1)}, bf16[4,48,3456]{2,1,0:T(8,128)(2,1)}, u32[]{:S(2)}, u32[]{:S(2)}) collective-permute-start(bf16[4,48,3456]{2,1,0:T(8,128)(2,1)} %get-tuple-element.178), channel_id=1, source_target_pairs={{0,8},{4,12},{8,0},{12,4},{1,9},{5,13},{9,1},{13,5},{2,10},{6,14},... | collective-permute-start | bytes 3981320 | tf_op jit(solution)/shard_map/ppermute | solution.py:87
  319.5 58.2 %collective-permute-start.19 = (bf16[4,48,3456]{2,1,0:T(8,128)(2,1)}, bf16[4,48,3456]{2,1,0:T(8,128)(2,1)}, u32[]{:S(2)}, u32[]{:S(2)}) collective-permute-start(bf16[4,48,3456]{2,1,0:T(8,128)(2,1)} %get-tuple-element.177), channel_id=1, source_target_pairs={{0,4},{4,0},{8,12},{12,8},{1,5},{5,1},{9,13},{13,9},{2,6},{6,2},{1... | collective-permute-start | bytes 3981320 | tf_op jit(solution)/shard_map/ppermute | solution.py:87
  332.1 45.7 %all-to-all-start.5 = ((bf16[1,4,128,768]{3,2,0,1:T(8,128)(2,1)}), bf16[1,4,128,768]{3,2,0,1:T(8,128)(2,1)S(1)}, u32[]{:S(2)}, u32[]{:S(2)}) async-start(bf16[1,4,128,768]{3,2,0,1:T(8,128)(2,1)} %bitcast.141), calls=%async_computation.5 | async-start | bytes 1572864 | tf_op jit(solution)/shard_map/all_to_all | solution.py:95
  357.0 45.4 %collective-permute-start.27 = (bf16[512,2304]{1,0:T(8,128)(2,1)}, bf16[512,2304]{1,0:T(8,128)(2,1)}, u32[]{:S(2)}, u32[]{:S(2)}) collective-permute-start(bf16[512,2304]{1,0:T(8,128)(2,1)} %get-tuple-element.191), channel_id=1, source_target_pairs={{0,16},{16,0},{1,17},{17,1},{2,18},{18,2},{3,19},{19,3},{4,20},{20... | collective-permute-start | bytes 7077896 | tf_op jit(solution)/shard_map/ppermute | solution.py:83
  377.8 24.6 %collective-permute-start.25 = (bf16[768,512]{1,0:T(8,128)(2,1)}, bf16[768,512]{1,0:T(8,128)(2,1)}, u32[]{:S(2)}, u32[]{:S(2)}) collective-permute-start(bf16[768,512]{1,0:T(8,128)(2,1)} %get-tuple-element.187.refs_0_), channel_id=1, source_target_pairs={{0,16},{16,0},{1,17},{17,1},{2,18},{18,2},{3,19},{19,3},{4,20},{20... | collective-permute-start | bytes 2359304 | tf_op jit(solution)/shard_map/ppermute | solution.py:83
  394.9 39.6 %collective-permute-start.28 = (bf16[4,48,2688]{2,1,0:T(8,128)(2,1)}, bf16[4,48,2688]{2,1,0:T(8,128)(2,1)S(1)}, u32[]{:S(2)}, u32[]{:S(2)}) collective-permute-start(bf16[4,48,2688]{2,1,0:T(8,128)(2,1)} %get-tuple-element.193), channel_id=1, source_target_pairs={{0,4},{4,0},{8,12},{12,8},{1,5},{5,1},{9,13},{13,9},{2,6},{6,2},{1... | collective-permute-start | bytes 3096584 | tf_op jit(solution)/shard_map/ppermute | solution.py:87
  396.0 38.4 %collective-permute-start.29 = (bf16[4,48,2688]{2,1,0:T(8,128)(2,1)}, bf16[4,48,2688]{2,1,0:T(8,128)(2,1)}, u32[]{:S(2)}, u32[]{:S(2)}) collective-permute-start(bf16[4,48,2688]{2,1,0:T(8,128)(2,1)} %get-tuple-element.194), channel_id=1, source_target_pairs={{0,8},{4,12},{8,0},{12,4},{1,9},{5,13},{9,1},{13,5},{2,10},{6,14},... | collective-permute-start | bytes 3096584 | tf_op jit(solution)/shard_map/ppermute | solution.py:87
  396.3 46.4 %collective-permute-start.30 = (bf16[4,48,2688]{2,1,0:T(8,128)(2,1)}, bf16[4,48,2688]{2,1,0:T(8,128)(2,1)}, u32[]{:S(2)}, u32[]{:S(2)}) collective-permute-start(bf16[4,48,2688]{2,1,0:T(8,128)(2,1)} %get-tuple-element.195), channel_id=1, source_target_pairs={{0,12},{4,8},{8,4},{12,0},{1,13},{5,9},{9,5},{13,1},{2,14},{6,10},... | collective-permute-start | bytes 3096584 | tf_op jit(solution)/shard_map/ppermute | solution.py:87
  397.5 63.7 %all-to-all-start.10 = ((bf16[4,48,3456]{2,1,0:T(8,128)(2,1)}), bf16[4,48,3456]{2,1,0:T(8,128)(2,1)}, u32[]{:S(2)}, u32[]{:S(2)}) async-start(bf16[4,48,3456]{2,1,0:T(8,128)(2,1)} %add_convert_fusion), calls=%async_computation.10 | async-start | bytes 2654208 | tf_op jit(solution)/shard_map/all_to_all | solution.py:95
  458.9 36.6 %collective-permute-start.37 = (bf16[512,1152]{1,0:T(8,128)(2,1)}, bf16[512,1152]{1,0:T(8,128)(2,1)}, u32[]{:S(2)}, u32[]{:S(2)}) collective-permute-start(bf16[512,1152]{1,0:T(8,128)(2,1)} %get-tuple-element.216), channel_id=1, source_target_pairs={{0,16},{16,0},{1,17},{17,1},{2,18},{18,2},{3,19},{19,3},{4,20},{20... | collective-permute-start | bytes 3538952 | tf_op jit(solution)/shard_map/ppermute | solution.py:83
  461.2 45.8 %all-to-all-start.8 = ((bf16[4,48,2688]{2,1,0:T(8,128)(2,1)}), bf16[4,48,2688]{2,1,0:T(8,128)(2,1)S(1)}, u32[]{:S(2)}, u32[]{:S(2)}) async-start(bf16[4,48,2688]{2,1,0:T(8,128)(2,1)} %add_convert_fusion.1), calls=%async_computation.8 | async-start | bytes 2064384 | tf_op jit(solution)/shard_map/all_to_all | solution.py:95
  465.9 29.6 %collective-permute-start.35 = (bf16[768,512]{1,0:T(8,128)(2,1)}, bf16[768,512]{1,0:T(8,128)(2,1)}, u32[]{:S(2)}, u32[]{:S(2)}) collective-permute-start(bf16[768,512]{1,0:T(8,128)(2,1)} %get-tuple-element.214.refs_0_), channel_id=1, source_target_pairs={{0,16},{16,0},{1,17},{17,1},{2,18},{18,2},{3,19},{19,3},{4,20},{20... | collective-permute-start | bytes 2359304 | tf_op jit(solution)/shard_map/ppermute | solution.py:83
  466.5 29.0 %collective-permute-start.33 = (bf16[4,48,1920]{2,1,0:T(8,128)(2,1)}, bf16[4,48,1920]{2,1,0:T(8,128)(2,1)}, u32[]{:S(2)}, u32[]{:S(2)}) collective-permute-start(bf16[4,48,1920]{2,1,0:T(8,128)(2,1)} %get-tuple-element.211), channel_id=1, source_target_pairs={{0,8},{4,12},{8,0},{12,4},{1,9},{5,13},{9,1},{13,5},{2,10},{6,14},... | collective-permute-start | bytes 2211848 | tf_op jit(solution)/shard_map/ppermute | solution.py:87
  466.8 28.7 %collective-permute-start.32 = (bf16[4,48,1920]{2,1,0:T(8,128)(2,1)}, bf16[4,48,1920]{2,1,0:T(8,128)(2,1)}, u32[]{:S(2)}, u32[]{:S(2)}) collective-permute-start(bf16[4,48,1920]{2,1,0:T(8,128)(2,1)} %get-tuple-element.209), channel_id=1, source_target_pairs={{0,4},{4,0},{8,12},{12,8},{1,5},{5,1},{9,13},{13,9},{2,6},{6,2},{1... | collective-permute-start | bytes 2211848 | tf_op jit(solution)/shard_map/ppermute | solution.py:87
  545.2 28.6 %collective-permute-start.45 = (bf16[48,1536]{1,0:T(8,128)(2,1)}, bf16[48,1536]{1,0:T(8,128)(2,1)S(1)}, u32[]{:S(2)}, u32[]{:S(2)}) collective-permute-start(bf16[48,1536]{1,0:T(8,128)(2,1)} %broadcast_select_fusion.6), channel_id=1, source_target_pairs={{0,16},{16,0},{1,17},{17,1},{2,18},{18,2},{3,19},{19,3},{4,20},{20... | collective-permute-start | bytes 442376 | tf_op jit(solution)/shard_map/ppermute | solution.py:83
  (60 other events, 819.1 us)
Sparse Core Ops, SparseCore 0:
  35.6 83.9 all-gather.2
  123.0 101.5 all-gather.4
